TPU v7x, 256 devices: a whole 4x4x8 slice. The times are simulated.
256 devices in a mesh: subcube: 2 (over y_hi), row: 8 (over z), col: 16 (over x, y_lo, core).
Axes of the slice: x: 4, y: 4 (y_hi: 2, y_lo: 2; y = y_hi * 2 + y_lo), z: 8, core: 2. Of those that a mesh axis runs over, the one named last changes fastest.
Arguments:
- front_entries: float32 [16, 8, 64, 24576], P('col', 'row', None, 'subcube'), may hold values from -6 to 6
- child_blocks: float32 [2, 16, 8, 64, 12288], P('subcube', 'col', 'row'), may hold values from -6 to 6
- row_maps: int32 [2, 12288], replicated, may hold values from 0 to 24575, as said below
- pivot_inverses: float32 [2, 512, 512], P(None, 'row')
- tile_mask: int32 [48, 16], P(('subcube', 'row'), 'col'), may hold values 0 or 1
Outputs:
- factored: float32 [24576, 8192], P(('subcube', 'row'), 'col')
Inputs may be any that keep to these rules, and one draw needn't show every extreme that they name: Each row of row_maps lists 12288 distinct front rows in increasing order; its first is 0 and its last 24575.
All inputs are finite; a program needn't handle non-finite values. No bound on the sum of `tile_mask` on one device may be relied on, other than what follows from the above.
Results may differ from a plain program's by a relative error of at most 0.0001.
Values sent between devices are 32-bit elements; how exact they have to be, the bound alone decides.
No kernel may reach another device: no remote copies, remote signals or barrier semaphores. Data moves between devices by JAX's collectives and lax.ppermute only.
A program may use at most 128 MiB of HBM per device.

v0:
```python
import jax
import jax.numpy as jnp
from jax import lax
from jax.sharding import PartitionSpec as P

PANEL = 512
PANELS = 2


def broadcast(value, axis, source):
    kept = jnp.where(lax.axis_index(axis) == source, value, 0).astype(value.dtype)
    return lax.psum(kept, axis)


def from_partner(x, axis, distance):
    return lax.ppermute(x, axis, [(i, i ^ 1 << distance) for i in range(lax.axis_size(axis))])


def product(left, right):
    return jnp.dot(left, right, precision=lax.Precision.HIGHEST, preferred_element_type=jnp.float32)


def extend_add(target, child_rows, row_map, offset):
    local_rows = row_map - offset
    inside = (local_rows >= 0) & (local_rows < target.shape[1])
    target_rows = jnp.where(inside, local_rows, target.shape[1])
    return target.at[:, target_rows].add(child_rows, mode="drop")


def send_strip(row_strip, root_row):
    return broadcast(row_strip, ("subcube", "row"), root_row)


def local(front_entries, child_blocks, row_maps, pivot_inverses, tile_mask):
    half_rows = front_entries.shape[3]
    subcube_side = lax.axis_index("subcube")
    own_block = child_blocks[0, 0, 0]
    partner_block = from_partner(own_block, "subcube", 0)
    own_map = lax.dynamic_index_in_dim(row_maps, subcube_side, 0, keepdims=False)
    partner_map = lax.dynamic_index_in_dim(row_maps, 1 - subcube_side, 0, keepdims=False)
    assembled = front_entries[0, 0]
    assembled = extend_add(assembled, own_block, own_map, subcube_side * half_rows)
    assembled = extend_add(assembled, partner_block, partner_map, subcube_side * half_rows)
    regrouped = lax.all_to_all(assembled, "row", split_axis=1, concat_axis=0, tiled=True)
    local_block = regrouped.T
    row_count = local_block.shape[0]
    block_width = local_block.shape[1]
    column_place = lax.axis_index("col")
    column_ids = column_place * block_width + jnp.arange(block_width, dtype=jnp.int32)
    grid_row = subcube_side * lax.axis_size("row") + lax.axis_index("row")
    row_ids = grid_row * row_count + jnp.arange(row_count, dtype=jnp.int32)
    kept_tiles = jnp.repeat(jnp.repeat(tile_mask.astype(jnp.float32), PANEL, axis=0), PANEL, axis=1)
    for panel_index in range(PANELS):
        first_col = panel_index * PANEL
        after_col = first_col + PANEL
        owner_col = first_col // block_width
        local_start = first_col - owner_col * block_width
        root_row = first_col // row_count
        row_start = first_col - root_row * row_count
        panel_cols = local_block
        row_strip = local_block[row_start : row_start + PANEL, :]
        inverse = lax.all_gather(pivot_inverses[panel_index], "row", axis=0, tiled=True)
        scaled = broadcast(product(panel_cols, inverse), "col", owner_col)
        across = send_strip(row_strip, root_row)
        update = product(scaled, across)
        below = (row_ids >= after_col).astype(jnp.float32)[:, None]
        live_mask = kept_tiles * (column_ids >= after_col).astype(jnp.float32)[None, :] * below
        local_block = local_block - update * live_mask
        current = local_block
        replace = (column_place == owner_col) & (row_ids >= first_col)[:, None]
        local_block = local_block.at[:, local_start : local_start + PANEL].set(
            jnp.where(replace, scaled, current)
        )
    return local_block


def solution(mesh):
    return jax.shard_map(
        local,
        mesh=mesh,
        in_specs=(
            P("col", "row", None, "subcube"),
            P("subcube", "col", "row", None, None),
            P(),
            P(None, "row", None),
            P(("subcube", "row"), "col"),
        ),
        out_specs=P(("subcube", "row"), "col"),
        check_vma=False,
    )
```

profile of v0, /device:TPU:10, one launch (start us, length us, event | category | flops | bytes accessed | tf_op | source)
XLA Modules:
  0.0 854.8 jit_solution(14957715034153878558)
XLA Ops:
  7.4 2.3 collective-permute-start
  9.7 0.0 copy-start
  9.7 5.9 copy.10
  15.6 0.0 copy-done
  15.6 0.0 copy-start.2
  15.6 4.0 copy.11
  19.6 0.0 copy-done.2
  19.6 0.3 compare_select_fusion
  19.9 64.7 %scatter_fusion = f32[64,12288]{0,1:T(8,128)} fusion(f32[64,12288]{0,1:T(8,128)} %bitcast.31, s32[12288]{0:T(1024)S(1)} %bitcast.39, f32[12288,64]{1,0:T(8,128)} %copy.11), kind=kCustom, calls=%fused_computation | custom fusion | flops 786432 | bytes 9486336 | tf_op jit(solution)/shard_map/scatter-add | solution.py:27
  84.6 0.0 collective-permute-done
  84.6 5.8 copy.12
  90.4 64.7 %scatter_fusion.1 = f32[64,12288]{0,1:T(8,128)} fusion(f32[64,12288]{0,1:T(8,128)} %scatter_fusion, s32[12288]{0:T(1024)S(1)} %bitcast.38, f32[12288,64]{1,0:T(8,128)} %copy.12), kind=kCustom, calls=%fused_computation.1 | custom fusion | flops 786432 | bytes 9486336 | tf_op jit(solution)/shard_map/scatter-add | solution.py:27
  155.1 6.1 copy.13
  161.2 0.0 copy-start.1
  161.2 8.6 %all-to-all-start = ((f32[64,8,1536]{2,0,1:T(8,128)}), f32[64,8,1536]{2,0,1:T(8,128)S(1)}, u32[]{:S(2)}, u32[]{:S(2)}) async-start(f32[64,8,1536]{2,0,1:T(8,128)} %copy.13), calls=%async_computation | async-start | bytes 6291456 | tf_op jit(solution)/shard_map/all_to_all | solution.py:44
  169.8 0.0 all-gather.5.cloned.1.call-start
  169.9 0.0 copy-done.1
  169.9 0.7 fusion.17
  170.6 0.0 all-gather.5.cloned.1.call-update
  170.6 0.0 all-reduce.7.cloned.1.call-start
  170.7 82.5 %all-to-all-done = f32[64,8,1536]{2,0,1:T(8,128)S(1)} async-done(((f32[64,8,1536]{2,0,1:T(8,128)}), f32[64,8,1536]{2,0,1:T(8,128)S(1)}, u32[]{:S(2)}, u32[]{:S(2)}) %all-to-all-start) | async-done | bytes 3145760 | tf_op jit(solution)/shard_map/all_to_all | solution.py:44
  253.2 2.3 copy.14
  255.5 2.4 slice_select_fusion.1
  257.9 0.0 all-reduce.7.cloned.1.call-update
  257.9 0.2 all-reduce.5.cloned.1.call-start
  258.1 0.0 all-gather.5.cloned.1.call-done
  258.2 12.4 %convolution_select_fusion.1 = f32[1536,512]{1,0:T(8,128)} fusion(f32[512,1536]{1,0:T(8,128)S(1)} %bitcast.34, pred[]{:T(512)S(6)} %eq.13, f32[1,512,512]{2,1,0:T(8,128)} %all-gather.5.cloned.1.call-done), kind=kOutput, calls=%fused_computation.3 | convolution fusion | flops 4832624640 | bytes 7340033 | tf_op jit(solution)/shard_map/dot_general | solution.py:20
  270.6 0.0 copy-start.3
  270.6 0.0 all-reduce.5.cloned.1.call-update
  270.6 0.0 all-gather.7.cloned.1.call-start
  270.6 0.7 all-gather.7.cloned.1.call-update
  271.3 0.0 all-reduce.11.cloned.1.call-start
  271.4 0.0 copy-done.3
  271.4 0.1 broadcast_in_dim.44
  271.5 140.2 %all-reduce.7.cloned.1.call-done = f32[512,512]{1,0:T(8,128)} async-done(((f32[512,512]{1,0:T(8,128)}), f32[512,512]{1,0:T(8,128)}) %all-reduce.7.cloned.1.call-update) | async-done | bytes 1048592 | tf_op jit(solution)/shard_map/psum | solution.py:12
  411.7 123.7 %all-reduce.5.cloned.1.call-done = f32[1536,512]{1,0:T(8,128)} async-done(((f32[1536,512]{1,0:T(8,128)}), f32[1536,512]{1,0:T(8,128)}) %all-reduce.5.cloned.1.call-update) | async-done | bytes 3145744 | tf_op jit(solution)/shard_map/psum | solution.py:12
  535.4 9.6 %fusion.1 = f32[1536,512]{1,0:T(8,128)S(1)} fusion(f32[1536,512]{1,0:T(8,128)} %all-reduce.5.cloned.1.call-done, f32[512,512]{1,0:T(8,128)} %all-reduce.7.cloned.1.call-done, f32[1536]{0:T(1024)S(1)} %get-tuple-element.49, f32[512]{0:T(512)S(1)} %fusion.15, f32[1536]{0:T(1024)S(1)} %broadcast_in_dim.45, pred[1536]{0:T(1024)(128)(4,1)S(1)} %get-tuple-element.50, ...), kind=kOutput, calls=%fused_computation.7 | convolution fusion | flops 4835770368 | bytes 10501632 | tf_op jit(solution)/shard_map/dot_general | solution.py:20
  545.0 1.1 slice_select_fusion
  546.0 0.0 all-reduce.11.cloned.1.call-update
  546.0 0.3 all-reduce.9.cloned.1.call-start
  546.3 0.0 all-gather.7.cloned.1.call-done
  546.3 7.5 convolution_select_fusion
  553.8 0.0 all-reduce.9.cloned.1.call-update
  553.9 159.6 %all-reduce.11.cloned.1.call-done = f32[512,512]{1,0:T(8,128)} async-done(((f32[512,512]{1,0:T(8,128)}), f32[512,512]{1,0:T(8,128)}) %all-reduce.11.cloned.1.call-update) | async-done | bytes 1048592 | tf_op jit(solution)/shard_map/psum | solution.py:12
  713.5 123.8 %all-reduce.9.cloned.1.call-done = f32[1536,512]{1,0:T(8,128)} async-done(((f32[1536,512]{1,0:T(8,128)}), f32[1536,512]{1,0:T(8,128)}) %all-reduce.9.cloned.1.call-update) | async-done | bytes 3145744 | tf_op jit(solution)/shard_map/psum | solution.py:12
  837.3 9.9 %fusion.3 = f32[1536,512]{1,0:T(8,128)} fusion(f32[1536,512]{1,0:T(8,128)} %all-reduce.9.cloned.1.call-done, f32[1536,512]{1,0:T(8,128)S(1)} %fusion.1, f32[512,512]{1,0:T(8,128)} %all-reduce.11.cloned.1.call-done, f32[1536]{0:T(1024)S(1)} %get-tuple-element.52, f32[512]{0:T(512)S(1)} %fusion.16, f32[1536]{0:T(1024)S(1)} %broadcast_in_dim.45, ...), kind=kOutput, calls=%fused_computation.9 | convolution fusion | flops 4835770368 | bytes 10501632 | tf_op jit(solution)/shard_map/dot_general | solution.py:20
  (6 shorter events, 0.0 us)
Async XLA Ops:
  7.4 77.2 %collective-permute-start = (f32[64,12288]{1,0:T(8,128)}, f32[64,12288]{1,0:T(8,128)}, u32[]{:S(2)}, u32[]{:S(2)}) collective-permute-start(f32[64,12288]{1,0:T(8,128)} %bitcast.36), channel_id=1, source_target_pairs={{0,128},{128,0},{1,129},{129,1},{2,130},{130,2},{3,131},{131,3},{4... | collective-permute-start | bytes 9437192 | tf_op jit(solution)/shard_map/ppermute | solution.py:16
  9.7 5.9 copy-start
  15.6 4.0 copy-start.2
  161.2 8.6 %copy-start.1 = (f32[2,64,512]{2,1,0:T(8,128)S(1)}, f32[2,64,512]{2,1,0:T(8,128)}, u32[]{:S(2)}) copy-start(f32[2,64,512]{2,1,0:T(8,128)} %param.16) | copy-start | bytes 786436
  161.2 92.0 %all-to-all-start = ((f32[64,8,1536]{2,0,1:T(8,128)}), f32[64,8,1536]{2,0,1:T(8,128)S(1)}, u32[]{:S(2)}, u32[]{:S(2)}) async-start(f32[64,8,1536]{2,0,1:T(8,128)} %copy.13), calls=%async_computation | async-start | bytes 6291456 | tf_op jit(solution)/shard_map/all_to_all | solution.py:44
  169.8 88.4 %all-gather.5.cloned.1.call-start = ((), (), s32[]{:S(2)}) async-start(), calls=%async_computation.5 | async-start | bytes 1179648 | tf_op jit(solution)/shard_map/all_gather | solution.py:62
  170.6 241.1 %all-reduce.7.cloned.1.call-start = ((), (), s32[]{:S(2)}) async-start(), calls=%async_computation.2 | async-start | bytes 2097152 | tf_op jit(solution)/shard_map/psum | solution.py:12
  257.9 277.5 %all-reduce.5.cloned.1.call-start = ((), (), s32[]{:S(2)}) async-start(), calls=%async_computation.1 | async-start | bytes 6291456 | tf_op jit(solution)/shard_map/psum | solution.py:12
  270.6 0.8 copy-start.3
  270.6 275.8 %all-gather.7.cloned.1.call-start = ((), (), s32[]{:S(2)}) async-start(), calls=%async_computation.6 | async-start | bytes 1179648 | tf_op jit(solution)/shard_map/all_gather | solution.py:62
  271.3 442.1 %all-reduce.11.cloned.1.call-start = ((), (), s32[]{:S(2)}) async-start(), calls=%async_computation.4 | async-start | bytes 2097152 | tf_op jit(solution)/shard_map/psum | solution.py:12
  546.0 291.3 %all-reduce.9.cloned.1.call-start = ((), (), s32[]{:S(2)}) async-start(), calls=%async_computation.3 | async-start | bytes 6291456 | tf_op jit(solution)/shard_map/psum | solution.py:12
Sparse Core Ops, SparseCore 0:
  172.6 55.5 all-gather.4
  273.2 34.1 all-gather.6
Sparse Core Ops, SparseCore 1:
  258.0 153.7 all-reduce.6
  414.5 120.9 all-reduce.4
  546.1 167.3 all-reduce.10
  716.2 121.1 all-reduce.8
where the time goes:
time: 865 us; the launch traced here: 855 us
  waiting for transfers between devices  631 us (73%)
  other arithmetic  133 us (15%)
  matrix products  39.3 us (5%)
  local copies, waits for them, and re-layouts  24.9 us (3%)
  between operations  15.2 us (2%)
  starting transfers between devices  11.5 us (1%)
    psum x4, waiting for transfers between devices, broadcast(): return lax.psum(kept, axis)  547 us
    scatter-add x2, other arithmetic, extend_add(): return target.at[:, target_rows].add(child_rows, mode='drop')  129 us
    all_to_all x1, waiting for transfers between devices, local(): lax.all_to_all(assembled, 'row', split_axis=1, concat_axis=0, tiled=True)  82.5 us
    dot_general x4, matrix products, product(): jnp.dot(left, right, precision=lax.Precision.HIGHEST, preferred_element_t...  39.3 us
  transfers between devices with their start and end apart: 8, of which 5 were waited for; matrix products, arithmetic and copies ran while one was open for 13% of the time, Pallas kernels for 0%

commit v1 on v0

v1 whole, which is shorter than its diff:
```python
import functools

import jax
import jax.numpy as jnp
from jax import lax
from jax.experimental import pallas as pl
from jax.experimental.pallas import tpu as pltpu
from jax.sharding import PartitionSpec as P

PANEL = 512
PANELS = 2
LANES = 128
BIG = 2**30
VMEM_BYTES = 56 * 2**20


def extend_kernel(bases, scalars, maps_ref, front_ref, *refs):
    sources, out_ref = refs[: len(bases)], refs[len(bases)]
    low_ref, high_ref, place_ref = refs[len(bases) + 1 :]
    step = pl.program_id(0)
    steps = pl.num_programs(0)
    per_step = front_ref.shape[1] // LANES
    map_blocks = maps_ref.shape[1]
    blocks = steps * per_step
    first_row = scalars[len(bases) * (blocks + 1)]
    lane = lax.broadcasted_iota(jnp.int32, low_ref.shape, 1)
    row = lax.broadcasted_iota(jnp.int32, low_ref.shape, 0)
    wanted = first_row + (step * per_step + row) * LANES + lane
    for j in range(per_step):
        out_ref[0, :, j * LANES : (j + 1) * LANES] = front_ref[:, j * LANES : (j + 1) * LANES]
    for index, source in enumerate(sources):
        map_index = bases[index]
        source_blocks = source.shape[1] // LANES
        offset = scalars[len(bases) * blocks + index]
        blocks_at = []
        for j in range(per_step):
            start = scalars[index * blocks + step * per_step + j]
            at = jnp.minimum(start // LANES, map_blocks - 1)
            after = jnp.minimum(at + 1, map_blocks - 1)
            low_ref[j : j + 1, :] = maps_ref[map_index, pl.ds(at, 1), :]
            high_ref[j : j + 1, :] = jnp.where(at + 1 < map_blocks, maps_ref[map_index, pl.ds(after, 1), :], BIG)
            blocks_at.append(at)
        low, high = low_ref[...], high_ref[...]

        def pick(at):
            inner = at & (LANES - 1)
            return jnp.where(
                at < LANES, jnp.take_along_axis(low, inner, axis=1), jnp.take_along_axis(high, inner, axis=1)
            )

        place = jnp.zeros(low_ref.shape, jnp.int32)
        width = LANES
        while width >= 1:
            place = jnp.where(pick(place + (width - 1)) < wanted, place + width, place)
            width //= 2
        place_ref[...] = jnp.where(pick(place) == wanted, place, -1)
        for j in range(per_step):
            at = blocks_at[j] - offset
            inside_low = (at >= 0) & (at < source_blocks)
            inside_high = (at + 1 >= 0) & (at + 1 < source_blocks)
            low_at = pl.multiple_of(jnp.clip(at, 0, source_blocks - 1) * LANES, LANES)
            high_at = pl.multiple_of(jnp.clip(at + 1, 0, source_blocks - 1) * LANES, LANES)
            places = jnp.broadcast_to(place_ref[j : j + 1, :], (source.shape[0], LANES))
            inner = places & (LANES - 1)
            in_low = (places >= 0) & (places < LANES) & inside_low
            in_high = (places >= LANES) & inside_high
            gained = jnp.where(in_low, jnp.take_along_axis(source[:, pl.ds(low_at, LANES)], inner, axis=1), 0.0)
            gained = jnp.where(
                in_high, jnp.take_along_axis(source[:, pl.ds(high_at, LANES)], inner, axis=1), gained
            )
            out_ref[0, :, j * LANES : (j + 1) * LANES] += gained


def extend_add(front, sources, bases, offsets, maps, starts, first_row, steps):
    columns, rows = front.shape
    width = rows // steps
    per_step = width // LANES
    padded = -(-per_step // 8) * 8
    scalars = jnp.concatenate(
        [starts[base] for base in bases] + [jnp.stack(offsets), first_row.reshape(1)]
    ).astype(jnp.int32)
    whole = lambda shape: pl.BlockSpec(shape, lambda i, _: (0,) * len(shape), pipeline_mode=pl.Buffered(1))
    return pl.pallas_call(
        functools.partial(extend_kernel, tuple(bases)),
        out_shape=jax.ShapeDtypeStruct((steps, columns, width), jnp.float32),
        grid_spec=pltpu.PrefetchScalarGridSpec(
            num_scalar_prefetch=1,
            grid=(steps,),
            in_specs=[whole(maps.shape), pl.BlockSpec((columns, width), lambda i, _: (0, i))]
            + [whole(source.shape) for source in sources],
            out_specs=pl.BlockSpec((1, columns, width), lambda i, _: (i, 0, 0)),
            scratch_shapes=[pltpu.VMEM((padded, LANES), jnp.int32)] * 3,
        ),
        compiler_params=pltpu.CompilerParams(vmem_limit_bytes=VMEM_BYTES),
    )(scalars, maps, front, *sources)


def halves(x):
    high = x.astype(jnp.bfloat16)
    return high, (x - high.astype(jnp.float32)).astype(jnp.bfloat16)


def product(left, right, dims):
    left_high, left_low = left
    right_high, right_low = right
    dot = lambda a, b: lax.dot_general(a, b, (dims, ((), ())), preferred_element_type=jnp.float32)
    return dot(left_high, right_high) + (dot(left_high, right_low) + dot(left_low, right_high))


PLAIN = ((1,), (0,))
CROSS = ((1,), (1,))


def factor_kernel(flags, strip_ref, corner_ref, inverse_ref, first_ref, second_ref, fixed_ref):
    place, kept = flags[0], flags[1]
    inverse0 = halves(inverse_ref[0])
    inverse1 = halves(inverse_ref[1])
    pivot0 = halves(strip_ref[:, :PANEL])
    corner = corner_ref[...]
    corner10 = halves(corner[:, 0].reshape(PANEL, PANEL))
    corner01 = halves(corner[:, 1].reshape(PANEL, PANEL))
    first = product(pivot0, inverse0, CROSS)
    lowered = product(halves(first), corner10, PLAIN)
    pivot1 = strip_ref[:, PANEL : 2 * PANEL] - jnp.where(kept == 1, lowered, 0.0)
    second = product(halves(pivot1), inverse1, CROSS)
    second = jnp.where(place == 1, -inverse_ref[1].T, second)
    crossed = product(halves(second), corner01, PLAIN)
    fixed = product(halves(crossed), inverse0, CROSS)
    first = jnp.where(place == 0, -inverse_ref[0].T, jnp.where(place == 1, 0.0, first))
    first_ref[...] = first
    second_ref[...] = second
    fixed_ref[...] = fixed


def factor(flags, strip, corner, inverse):
    square = jax.ShapeDtypeStruct((PANEL, PANEL), jnp.float32)
    return pl.pallas_call(
        factor_kernel,
        out_shape=(square, square, square),
        grid_spec=pltpu.PrefetchScalarGridSpec(
            num_scalar_prefetch=1,
            grid=(1,),
            in_specs=[
                pl.BlockSpec(strip.shape, lambda i, _: (0, 0)),
                pl.BlockSpec(corner.shape[:3] + (PANEL,), lambda i, _: (0, 0, 0, corner.shape[3] // PANEL - 1)),
                pl.BlockSpec(inverse.shape, lambda i, _: (0, 0, 0)),
            ],
            out_specs=[pl.BlockSpec((PANEL, PANEL), lambda i, _: (0, 0))] * 3,
        ),
        compiler_params=pltpu.CompilerParams(vmem_limit_bytes=VMEM_BYTES),
    )(flags, strip, corner, inverse)


def update_kernel(flags, block_ref, panels_ref, first_ref, second_ref, fixed_ref, out_ref):
    tile = pl.program_id(0)
    keep, use_first, use_fixed, use_second = (flags[4 * tile + i] == 1 for i in range(4))
    left0 = first_ref[...] - jnp.where(use_fixed, fixed_ref[...], 0.0)
    left0 = halves(jnp.where(use_first, left0, 0.0))
    left1 = halves(jnp.where(use_second, second_ref[...], 0.0))
    panel = panels_ref[...]
    right0 = halves(panel[:, 0].reshape(PANEL, PANEL))
    right1 = halves(panel[:, 1].reshape(PANEL, PANEL))
    update = product(left0, right0, PLAIN) + product(left1, right1, PLAIN)
    out_ref[...] = (jnp.where(keep, block_ref[...], 0.0) - update).T


def update(flags, block, panels, first, second, fixed):
    tiles = block.shape[1] // PANEL
    square = pl.BlockSpec((PANEL, PANEL), lambda i, _: (0, 0))
    return pl.pallas_call(
        update_kernel,
        out_shape=jax.ShapeDtypeStruct(block.shape[::-1], jnp.float32),
        grid_spec=pltpu.PrefetchScalarGridSpec(
            num_scalar_prefetch=1,
            grid=(tiles,),
            in_specs=[
                pl.BlockSpec((PANEL, PANEL), lambda i, _: (0, i)),
                pl.BlockSpec(panels.shape[:3] + (PANEL,), lambda i, _: (0, 0, 0, i)),
                square,
                square,
                square,
            ],
            out_specs=pl.BlockSpec((PANEL, PANEL), lambda i, _: (i, 0)),
        ),
        compiler_params=pltpu.CompilerParams(vmem_limit_bytes=VMEM_BYTES),
    )(flags, block, panels, first, second, fixed)


def local(front_entries, child_blocks, row_maps, pivot_inverses, tile_mask):
    thin, half_rows = front_entries.shape[2:]
    child_rows = child_blocks.shape[4]
    grid_rows = lax.axis_size("row")
    grid_cols = lax.axis_size("col")
    side = lax.axis_index("subcube")
    row_place = lax.axis_index("row")
    place = lax.axis_index("col")
    row_count = half_rows // grid_rows
    own = child_blocks[0, 0, 0]

    mask_here = jnp.pad(tile_mask.astype(jnp.float32).reshape(1, -1), ((0, 0), (0, LANES - tile_mask.shape[0])))
    masks = lax.all_gather(mask_here, ("subcube", "row", "col"), axis=0, tiled=True)
    masks = (masks.reshape(2, grid_rows, grid_cols, LANES)[..., : tile_mask.shape[0]] > 0.5).astype(jnp.int32)
    inverse = lax.all_gather(pivot_inverses, "row", axis=0)
    chunks = thin // 8
    inverse = inverse.reshape(grid_rows, PANELS, chunks, 8, PANEL).transpose(1, 2, 0, 3, 4).reshape(PANELS, PANEL, PANEL)

    window = -(-(child_rows * 13 // 24) // LANES) * LANES
    rest = child_rows - window
    swap = [(0, 1), (1, 0)]
    to_send = jnp.where(side == 0, own[:, rest:], own[:, :window])
    received = lax.ppermute(to_send, "subcube", swap)

    first_row = (side * half_rows).astype(jnp.int32)
    own_map = lax.dynamic_index_in_dim(row_maps, side, 0, keepdims=False)
    other_map = lax.dynamic_index_in_dim(row_maps, 1 - side, 0, keepdims=False)
    maps = jnp.stack([own_map, other_map])
    edges = first_row + LANES * jnp.arange(half_rows // LANES, dtype=jnp.int32)
    starts = jnp.sum((maps[:, None, :] < edges[None, :, None]).astype(jnp.int32), axis=2)
    maps = maps.reshape(2, child_rows // LANES, LANES)
    lower = jnp.sum((row_maps < half_rows).astype(jnp.int32), axis=1)
    spill = (child_rows - lower[0] > window) | (lower[1] > window)
    zero = jnp.zeros((), jnp.int32)
    window_at = jnp.where(side == 0, 0, rest // LANES).astype(jnp.int32)
    rest_at = jnp.where(side == 0, window // LANES, 0).astype(jnp.int32)
    front = front_entries[0, 0]
    assembled = extend_add(front, [own, received], [0, 1], [zero, window_at], maps, starts, first_row, grid_rows)

    def add_rest(blocks):
        more = lax.ppermute(jnp.where(side == 0, own[:, :rest], own[:, window:]), "subcube", swap)
        flat = blocks.transpose(1, 0, 2).reshape(thin, half_rows)
        return extend_add(flat, [more], [1], [rest_at], maps, starts, first_row, grid_rows)

    assembled = lax.cond(spill, add_rest, lambda blocks: blocks, assembled)

    strip_here = assembled[0, :, : PANELS * PANEL]
    strip_there = lax.ppermute(strip_here, "subcube", [(0, 1)])
    strip_here = jnp.where(side == 0, strip_here, strip_there)
    strip = lax.all_gather(strip_here, "row", axis=0, tiled=True)

    flat = assembled.reshape(grid_rows, chunks, 8, row_count)
    mine = jnp.where(place // 2 == 0, flat[:, 0], 0.0)
    for chunk in range(1, chunks):
        sent = lax.ppermute(flat[:, chunk], "col", [(k, 2 * chunk + k) for k in range(PANELS)])
        mine = mine + sent
    corner_here = jnp.where(place % 2 == 0, mine[0, :, PANEL : 2 * PANEL], mine[0, :, :PANEL])
    corner_there = lax.ppermute(corner_here, "subcube", [(0, 1)])
    corner_here = jnp.where(side == 0, corner_here, corner_there)
    mine = jnp.concatenate([mine, jnp.broadcast_to(corner_here[None], (grid_rows,) + corner_here.shape)], axis=2)
    mine = lax.all_to_all(mine, "row", split_axis=0, concat_axis=0, tiled=True)
    assembled, mine = lax.optimization_barrier((assembled, mine))
    panels = lax.all_gather(mine.reshape(thin, -1), "col", axis=0, tiled=True)
    panels = panels.reshape(chunks, PANELS, thin, -1)

    block = lax.all_to_all(assembled, "row", split_axis=0, concat_axis=0, tiled=True)
    block = block.reshape(PANEL, row_count)

    kept = lax.dynamic_index_in_dim(masks[0, 0, :, 1], place, 0, keepdims=False)
    first, second, fixed = factor(jnp.stack([place, kept]).astype(jnp.int32), strip, panels, inverse)

    tiles = row_count // PANEL
    tile_ids = (side * grid_rows + row_place) * tiles + jnp.arange(tiles, dtype=jnp.int32)
    own_mask = tile_mask[:, 0] == 1
    side_masks = lax.dynamic_index_in_dim(masks[:, :, 1], side, 0, keepdims=False)
    cross_mask = lax.dynamic_index_in_dim(side_masks, row_place, 0, keepdims=False) == 1
    is0, is1 = place == 0, place == 1
    keep = jnp.where(is0, False, jnp.where(is1, tile_ids == 0, True))
    use_first = jnp.where(is0, True, jnp.where(is1, tile_ids >= 1, own_mask & (tile_ids >= 1)))
    use_fixed = jnp.where(is0, False, cross_mask & (tile_ids >= jnp.where(is1, 1, 2)))
    use_second = jnp.where(is0, False, jnp.where(is1, tile_ids >= 1, own_mask & (tile_ids >= 2)))
    flags = jnp.stack([keep, use_first, use_fixed, use_second], axis=1).astype(jnp.int32).reshape(-1)
    return update(flags, block, panels, first, second, fixed)


def solution(mesh):
    return jax.shard_map(
        local,
        mesh=mesh,
        in_specs=(
            P("col", "row", None, "subcube"),
            P("subcube", "col", "row", None, None),
            P(),
            P(None, "row", None),
            P(("subcube", "row"), "col"),
        ),
        out_specs=P(("subcube", "row"), "col"),
        check_vma=False,
    )
```

time: 865 us -> 578 us (0.67)
  the two profiles are of different devices: /device:TPU:10 before, /device:TPU:1 now
where the time goes in v1:
time: 578 us; the launch traced here: 577 us
  blocking collectives  415 us (72%)
  waiting for transfers between devices  62.4 us (11%)
  Pallas kernels  33.6 us (6%)
  starting transfers between devices  31.4 us (5%)
  between operations  14.6 us (3%)
  local copies, waits for them, and re-layouts  11.4 us (2%)
  other arithmetic  9.13 us (2%)
    all_gather x1, blocking collectives, local(): lax.all_gather(mask_here, ('subcube', 'row', 'col'), axis=0, tiled=True)  394 us
    ppermute x1, waiting for transfers between devices, local(): received = lax.ppermute(to_send, 'subcube', swap)  32.1 us
    ppermute x7, waiting for transfers between devices, local(): lax.ppermute(flat[:, chunk], 'col', [(k, 2 * chunk + k) for k in range(PA...  24.7 us
    all_to_all x1, blocking collectives, local(): mine = lax.all_to_all(mine, 'row', split_axis=0, concat_axis=0, tiled=True)  20.5 us
    pallas_call x1, Pallas kernels, extend_add(): pl.pallas_call(functools.partial(extend_kernel, tuple(bases)), out_shape=...  14 us
    ppermute x7, starting transfers between devices, local(): lax.ppermute(flat[:, chunk], 'col', [(k, 2 * chunk + k) for k in range(PA...  12 us
  transfers between devices with their start and end apart: 14, of which 7 were waited for; matrix products, arithmetic and copies ran while one was open for 3% of the time, Pallas kernels for 4%

profile of v1, /device:TPU:1, one launch (start us, length us, event | category | flops | bytes accessed | tf_op | source)
XLA Modules:
  0.0 577.3 jit_solution(14335284461840069748)
XLA Ops:
  6.5 0.7 all-gather.10.cloned.1.call-update
  7.3 0.0 all-gather.8.cloned.1.call-start
  7.3 3.5 slice_select_fusion.1
  10.8 3.7 collective-permute-start.1
  14.5 0.2 fusion.10
  14.8 0.6 fusion.15
  16.6 0.1 constant_dynamic-slice_fusion.2
  16.7 0.1 fusion.14
  16.8 1.1 convert_reduce_fusion
  17.9 0.7 concatenate.9.scalars
  18.6 32.1 %collective-permute-done.1.refs_1_ = f32[64,6656]{1,0:T(8,128)} collective-permute-done((f32[64,6656]{1,0:T(8,128)}, f32[64,6656]{1,0:T(8,128)}, u32[]{:S(2)}, u32[]{:S(2)}) %collective-permute-start.1) | collective-permute-done | bytes 1703968 | tf_op jit(solution)/shard_map/ppermute | solution.py:211
  50.7 14.0 %shard_map.55 = f32[8,64,1536]{2,1,0:T(8,128)} custom-call(s32[195]{0:T(256)} %concatenate.9.scalars, s32[2,96,128]{2,1,0:T(8,128)S(1)} %bitcast.122, f32[64,12288]{1,0:T(8,128)} %bitcast.119, f32[64,12288]{1,0:T(8,128)S(1)} %bitcast.114, f32[64,6656]{1,0:T(8,128)} %collective-permute-done.1.refs_1_), custom_call_target="tpu_custom_call" | custom-call | tf_op jit(solution)/shard_map/pallas_call | solution.py:83
  64.7 1.0 slice_bitcast_fusion.9
  65.7 5.6 collective-permute-start.10
  71.3 4.0 collective-permute-done.10
  75.3 1.7 broadcast_select_fusion
  77.0 0.0 all-gather.8.cloned.1.call-update
  77.0 0.0 all-gather.6.cloned.1.call-start
  77.1 2.8 slice_bitcast_fusion.7
  79.9 2.3 collective-permute-start.2
  82.2 3.1 collective-permute-start.6
  85.4 1.3 collective-permute-start.5
  86.7 1.3 collective-permute-start.4
  88.0 1.3 collective-permute-start.3
  89.4 0.0 collective-permute-done.2
  89.4 1.3 collective-permute-start.8
  90.7 0.6 collective-permute-done.6
  91.3 1.3 collective-permute-start.7
  92.6 7.2 %collective-permute-done.5 = f32[8,8,1536]{2,1,0:T(8,128)S(1)} collective-permute-done((f32[8,8,1536]{2,1,0:T(8,128)}, f32[8,8,1536]{2,1,0:T(8,128)S(1)}, u32[]{:S(2)}, u32[]{:S(2)}) %collective-permute-start.5) | collective-permute-done | bytes 393248 | tf_op jit(solution)/shard_map/ppermute | solution.py:243
  99.8 8.4 %collective-permute-done.4 = f32[8,8,1536]{2,1,0:T(8,128)S(1)} collective-permute-done((f32[8,8,1536]{2,1,0:T(8,128)}, f32[8,8,1536]{2,1,0:T(8,128)S(1)}, u32[]{:S(2)}, u32[]{:S(2)}) %collective-permute-start.4) | collective-permute-done | bytes 393248 | tf_op jit(solution)/shard_map/ppermute | solution.py:243
  108.2 8.4 %collective-permute-done.3 = f32[8,8,1536]{2,1,0:T(8,128)S(1)} collective-permute-done((f32[8,8,1536]{2,1,0:T(8,128)}, f32[8,8,1536]{2,1,0:T(8,128)S(1)}, u32[]{:S(2)}, u32[]{:S(2)}) %collective-permute-start.3) | collective-permute-done | bytes 393248 | tf_op jit(solution)/shard_map/ppermute | solution.py:243
  116.7 1.2 fusion.8
  117.9 6.2 %collective-permute-start.9 = (f32[8,512]{1,0:T(8,128)S(1)}, f32[8,512]{1,0:T(8,128)S(1)}, u32[]{:S(2)}, u32[]{:S(2)}) collective-permute-start(f32[8,512]{1,0:T(8,128)S(1)} %fusion.11), channel_id=1, source_target_pairs={{0,128},{1,129},{2,130},{3,131},{4,132},{5,133},{6,134},{7,135},{8... | collective-permute-start | bytes 49160 | tf_op jit(solution)/shard_map/ppermute | solution.py:246
  124.1 0.9 collective-permute-done.9
  125.0 20.5 %all_to_all.10 = f32[8,8,2048]{2,1,0:T(8,128)} all-to-all(f32[8,8,2048]{2,1,0:T(8,128)S(1)} %pad_maximum_fusion), channel_id=1, replica_groups=mesh['subcube'=2,'row'=8,'col'=16] {'row'}, dimensions={0} | all-to-all | bytes 1048576 | tf_op jit(solution)/shard_map/all_to_all | solution.py:249
  145.6 0.0 all-gather.6.cloned.1.call-update
  145.6 0.0 copy-start.4
  145.6 3.7 all-to-all-start.1
  149.3 394.3 %all-gather.1 = f32[256,1,128]{2,1,0:T(1,128)S(1)} all-gather(f32[1,1,128]{2,1,0:T(1,128)S(1)} %pad_bitcast_fusion), channel_id=1, replica_groups=mesh['subcube'=2,'row'=8,'col'=16] {'subcube','row','col'}, dimensions={0}, use_global_device_ids=true | all-gather | bytes 131584 | tf_op jit(solution)/shard_map/all_gather | solution.py:201
  543.6 0.1 slice.103
  543.8 0.1 copy.26
  543.9 0.7 reshape.122.flags
  544.6 0.5 constant_dynamic-slice_fusion
  545.1 1.2 pad_add_fusion.2.flags
  546.3 3.1 copy.35
  549.5 8.9 %shard_map.56 = (f32[512,512]{1,0:T(8,128)}, f32[512,512]{1,0:T(8,128)}, f32[512,512]{1,0:T(8,128)}) custom-call(s32[2]{0:T(128)} %pad_add_fusion.2.flags, f32[512,1024]{1,0:T(8,128)} %all-gather.8.cloned.1.call-done.strip_ref, f32[8,2,64,2048]{3,2,1,0:T(8,128)} %bitcast.111, f32[2,512,512]{2,1,0:T(8,128)} %bitcast.118), custom_call_target="tpu_custom_call" | custom-call | tf_op jit(solution)/shard_map/pallas_call | solution.py:137
  558.4 1.7 copy-done.1
  560.0 10.8 %shard_map.57 = f32[1536,512]{1,0:T(8,128)} custom-call(s32[12]{0:T(128)} %reshape.122.flags, f32[512,1536]{1,0:T(8,128)} %bitcast.116, f32[8,2,64,2048]{3,2,1,0:T(8,128)} %bitcast.112, f32[512,512]{1,0:T(8,128)} %get-tuple-element.40.first_ref, f32[512,512]{1,0:T(8,128)} %get-tuple-element.41.second_ref, f32[512,512]{1,0:T(8,128)} %get-tuple-element.42.fixed_ref), custom_call_target="tpu_custom_call" | custom-call | tf_op jit(solution)/shard_map/pallas_call | solution.py:170
  (28 shorter events, 0.2 us)
Async XLA Ops:
  6.5 44.2 %copy-start = (f32[1,1,1,64,12288]{4,3,2,1,0:T(8,128)S(1)}, f32[1,1,1,64,12288]{4,3,2,1,0:T(8,128)}, u32[]{:S(2)}) copy-start(f32[1,1,1,64,12288]{4,3,2,1,0:T(8,128)} %param.8) | copy-start | bytes 9437188
  6.5 8.0 %copy-start.3 = (s32[2,12288]{1,0:T(2,128)S(1)}, s32[2,12288]{1,0:T(2,128)}, u32[]{:S(2)}) copy-start(s32[2,12288]{1,0:T(2,128)} %param.9) | copy-start | bytes 294916
  6.5 539.8 %all-gather.10.cloned.1.call-start = ((), (), s32[]{:S(2)}) async-start(), calls=%async_computation.4 | async-start | bytes 2359296 | tf_op jit(solution)/shard_map/all_gather | solution.py:203
  7.3 542.2 %all-gather.8.cloned.1.call-start = ((), (), s32[]{:S(2)}) async-start(), calls=%async_computation.3 | async-start | bytes 2359296 | tf_op jit(solution)/shard_map/all_gather | solution.py:238
  10.8 39.9 %collective-permute-start.1 = (f32[64,6656]{1,0:T(8,128)}, f32[64,6656]{1,0:T(8,128)}, u32[]{:S(2)}, u32[]{:S(2)}) collective-permute-start(f32[64,6656]{1,0:T(8,128)} %slice_select_fusion.1), channel_id=1, source_target_pairs={{0,128},{128,0},{1,129},{129,1},{2,130},{130,2},{3,131},{131,3},{4... | collective-permute-start | bytes 5111816 | tf_op jit(solution)/shard_map/ppermute | solution.py:211
  65.7 9.7 %collective-permute-start.10 = (f32[64,1024]{1,0:T(8,128)S(1)}, f32[64,1024]{1,0:T(8,128)S(1)}, u32[]{:S(2)}, u32[]{:S(2)}) collective-permute-start(f32[64,1024]{1,0:T(8,128)S(1)} %slice_bitcast_fusion.9), channel_id=1, source_target_pairs={{0,128},{1,129},{2,130},{3,131},{4,132},{5,133},{6,134},{7,135},{8... | collective-permute-start | bytes 786440 | tf_op jit(solution)/shard_map/ppermute | solution.py:236
  77.0 472.4 %all-gather.6.cloned.1.call-start = ((), (), s32[]{:S(2)}) async-start(), calls=%async_computation.2 | async-start | bytes 8912896 | tf_op jit(solution)/shard_map/all_gather | solution.py:251
  79.9 9.4 %collective-permute-start.2 = (f32[8,8,1536]{2,1,0:T(8,128)S(1)}, f32[8,8,1536]{2,1,0:T(8,128)S(1)}, u32[]{:S(2)}, u32[]{:S(2)}) collective-permute-start(f32[8,8,1536]{2,1,0:T(8,128)S(1)} %get-tuple-element.64), channel_id=1, source_target_pairs={{0,2},{1,3},{16,18},{17,19},{32,34},{33,35},{48,50},{49,51},{64,66... | collective-permute-start | bytes 1179656 | tf_op jit(solution)/shard_map/ppermute | solution.py:243
  82.2 9.1 %collective-permute-start.6 = (f32[8,8,1536]{2,1,0:T(8,128)S(1)}, f32[8,8,1536]{2,1,0:T(8,128)S(1)}, u32[]{:S(2)}, u32[]{:S(2)}) collective-permute-start(f32[8,8,1536]{2,1,0:T(8,128)S(1)} %get-tuple-element.65), channel_id=1, source_target_pairs={{0,10},{1,11},{16,26},{17,27},{32,42},{33,43},{48,58},{49,59},{64,... | collective-permute-start | bytes 1179656 | tf_op jit(solution)/shard_map/ppermute | solution.py:243
  85.4 14.4 %collective-permute-start.5 = (f32[8,8,1536]{2,1,0:T(8,128)}, f32[8,8,1536]{2,1,0:T(8,128)S(1)}, u32[]{:S(2)}, u32[]{:S(2)}) collective-permute-start(f32[8,8,1536]{2,1,0:T(8,128)} %get-tuple-element.66), channel_id=1, source_target_pairs={{0,8},{1,9},{16,24},{17,25},{32,40},{33,41},{48,56},{49,57},{64,72... | collective-permute-start | bytes 1179656 | tf_op jit(solution)/shard_map/ppermute | solution.py:243
  86.7 21.5 %collective-permute-start.4 = (f32[8,8,1536]{2,1,0:T(8,128)}, f32[8,8,1536]{2,1,0:T(8,128)S(1)}, u32[]{:S(2)}, u32[]{:S(2)}) collective-permute-start(f32[8,8,1536]{2,1,0:T(8,128)} %get-tuple-element.67), channel_id=1, source_target_pairs={{0,6},{1,7},{16,22},{17,23},{32,38},{33,39},{48,54},{49,55},{64,70... | collective-permute-start | bytes 1179656 | tf_op jit(solution)/shard_map/ppermute | solution.py:243
  88.0 28.6 %collective-permute-start.3 = (f32[8,8,1536]{2,1,0:T(8,128)}, f32[8,8,1536]{2,1,0:T(8,128)S(1)}, u32[]{:S(2)}, u32[]{:S(2)}) collective-permute-start(f32[8,8,1536]{2,1,0:T(8,128)} %get-tuple-element.68), channel_id=1, source_target_pairs={{0,4},{1,5},{16,20},{17,21},{32,36},{33,37},{48,52},{49,53},{64,68... | collective-permute-start | bytes 1179656 | tf_op jit(solution)/shard_map/ppermute | solution.py:243
  89.4 27.3 %collective-permute-start.8 = (f32[8,8,1536]{2,1,0:T(8,128)S(1)}, f32[8,8,1536]{2,1,0:T(8,128)S(1)}, u32[]{:S(2)}, u32[]{:S(2)}) collective-permute-start(f32[8,8,1536]{2,1,0:T(8,128)S(1)} %get-tuple-element.69), channel_id=1, source_target_pairs={{0,14},{1,15},{16,30},{17,31},{32,46},{33,47},{48,62},{49,63},{64,... | collective-permute-start | bytes 1179656 | tf_op jit(solution)/shard_map/ppermute | solution.py:243
  91.3 25.4 %collective-permute-start.7 = (f32[8,8,1536]{2,1,0:T(8,128)S(1)}, f32[8,8,1536]{2,1,0:T(8,128)S(1)}, u32[]{:S(2)}, u32[]{:S(2)}) collective-permute-start(f32[8,8,1536]{2,1,0:T(8,128)S(1)} %get-tuple-element.70), channel_id=1, source_target_pairs={{0,12},{1,13},{16,28},{17,29},{32,44},{33,45},{48,60},{49,61},{64,... | collective-permute-start | bytes 1179656 | tf_op jit(solution)/shard_map/ppermute | solution.py:243
  117.9 7.1 %collective-permute-start.9 = (f32[8,512]{1,0:T(8,128)S(1)}, f32[8,512]{1,0:T(8,128)S(1)}, u32[]{:S(2)}, u32[]{:S(2)}) collective-permute-start(f32[8,512]{1,0:T(8,128)S(1)} %fusion.11), channel_id=1, source_target_pairs={{0,128},{1,129},{2,130},{3,131},{4,132},{5,133},{6,134},{7,135},{8... | collective-permute-start | bytes 49160 | tf_op jit(solution)/shard_map/ppermute | solution.py:246
  145.6 3.7 copy-start.4
  145.6 412.8 %all-to-all-start.1 = ((f32[8,64,1536]{2,1,0:T(8,128)}), f32[8,64,1536]{2,1,0:T(8,128)S(1)}, u32[]{:S(2)}, u32[]{:S(2)}) async-start(f32[8,64,1536]{2,1,0:T(8,128)} %get-tuple-element.83), calls=%async_computation.1 | async-start | bytes 6291456 | tf_op jit(solution)/shard_map/all_to_all | solution.py:254
  558.4 1.7 copy-start.1
Sparse Core Ops, SparseCore 0:
  9.1 41.1 all-gather.9
  77.2 42.9 all-gather.7
  145.7 56.5 all-gather.5

commit v2 on v1

v2 whole, which is shorter than its diff:
```python
import functools

import jax
import jax.numpy as jnp
from jax import lax
from jax.experimental import pallas as pl
from jax.experimental.pallas import tpu as pltpu
from jax.sharding import PartitionSpec as P

PANEL = 512
PANELS = 2
LANES = 128
BIG = 2**30
VMEM_BYTES = 56 * 2**20


def search_kernel(sections, scalars, maps_ref, places_ref, low_ref, high_ref):
    map_blocks = maps_ref.shape[1]
    at_row = 0
    for section, count in enumerate(sections):
        child = scalars[section]
        first = scalars[len(sections) + section]
        for block in range(count):
            at = jnp.minimum(scalars[2 * len(sections) + at_row + block] // LANES, map_blocks - 1)
            after = jnp.minimum(at + 1, map_blocks - 1)
            row = at_row + block
            low_ref[row : row + 1, :] = maps_ref[child, pl.ds(at, 1), :]
            high_ref[row : row + 1, :] = jnp.where(at + 1 < map_blocks, maps_ref[child, pl.ds(after, 1), :], BIG)
        low, high = low_ref[at_row : at_row + count, :], high_ref[at_row : at_row + count, :]
        lane = lax.broadcasted_iota(jnp.int32, low.shape, 1)
        block_id = lax.broadcasted_iota(jnp.int32, low.shape, 0)
        wanted = first + block_id * LANES + lane

        def pick(at):
            inner = at & (LANES - 1)
            return jnp.where(
                at < LANES, jnp.take_along_axis(low, inner, axis=1), jnp.take_along_axis(high, inner, axis=1)
            )

        place = jnp.zeros(low.shape, jnp.int32)
        width = LANES
        while width >= 1:
            place = jnp.where(pick(place + (width - 1)) < wanted, place + width, place)
            width //= 2
        places_ref[at_row : at_row + count, :] = jnp.where(pick(place) == wanted, place, -1)
        at_row += count


def search(maps, children, firsts, starts):
    sections = tuple(start.shape[0] for start in starts)
    total = sum(sections)
    scalars = jnp.concatenate([jnp.stack(children), jnp.stack(firsts)] + list(starts)).astype(jnp.int32)
    return pl.pallas_call(
        functools.partial(search_kernel, sections),
        out_shape=jax.ShapeDtypeStruct((total, LANES), jnp.int32),
        grid_spec=pltpu.PrefetchScalarGridSpec(
            num_scalar_prefetch=1,
            grid=(1,),
            in_specs=[pl.BlockSpec(maps.shape, lambda i, _: (0, 0, 0))],
            out_specs=pl.BlockSpec((total, LANES), lambda i, _: (0, 0)),
            scratch_shapes=[pltpu.VMEM((total, LANES), jnp.int32)] * 2,
        ),
        compiler_params=pltpu.CompilerParams(vmem_limit_bytes=VMEM_BYTES),
    )(scalars, maps)


def extend_kernel(first_place, map_blocks, scalars, places_ref, front_ref, source_ref, out_ref):
    step = pl.program_id(0)
    columns, width = out_ref.shape[1:]
    per_step = width // LANES
    source_blocks = source_ref.shape[1] // LANES
    offset = scalars[scalars.shape[0] - 1]
    for j in range(per_step):
        block = step * per_step + j
        at = jnp.minimum(scalars[block] // LANES, map_blocks - 1) - offset
        inside_low = (at >= 0) & (at < source_blocks)
        inside_high = (at + 1 >= 0) & (at + 1 < source_blocks)
        low_at = pl.multiple_of(jnp.clip(at, 0, source_blocks - 1) * LANES, LANES)
        high_at = pl.multiple_of(jnp.clip(at + 1, 0, source_blocks - 1) * LANES, LANES)
        place = jnp.broadcast_to(places_ref[pl.ds(first_place + block, 1), :], (columns, LANES))
        inner = place & (LANES - 1)
        in_low = (place >= 0) & (place < LANES) & inside_low
        in_high = (place >= LANES) & inside_high
        here = slice(j * LANES, (j + 1) * LANES)
        gained = jnp.where(in_low, jnp.take_along_axis(source_ref[:, pl.ds(low_at, LANES)], inner, axis=1), 0.0)
        gained = jnp.where(
            in_high, jnp.take_along_axis(source_ref[:, pl.ds(high_at, LANES)], inner, axis=1), gained
        )
        out_ref[0, :, here] = front_ref[..., here].reshape(columns, LANES) + gained


def extend_add(front, source, places, first_place, starts, offset, map_blocks, steps):
    if front.ndim == 2:
        columns, rows = front.shape
        width = rows // steps
        front_spec = pl.BlockSpec((columns, width), lambda i, _: (0, i))
    else:
        columns, width = front.shape[1:]
        front_spec = pl.BlockSpec((1, columns, width), lambda i, _: (i, 0, 0))
    scalars = jnp.concatenate([starts, offset.reshape(1)]).astype(jnp.int32)
    whole = lambda shape: pl.BlockSpec(shape, lambda i, _: (0,) * len(shape), pipeline_mode=pl.Buffered(1))
    return pl.pallas_call(
        functools.partial(extend_kernel, first_place, map_blocks),
        out_shape=jax.ShapeDtypeStruct((steps, columns, width), jnp.float32),
        grid_spec=pltpu.PrefetchScalarGridSpec(
            num_scalar_prefetch=1,
            grid=(steps,),
            in_specs=[whole(places.shape), front_spec, whole(source.shape)],
            out_specs=pl.BlockSpec((1, columns, width), lambda i, _: (i, 0, 0)),
        ),
        compiler_params=pltpu.CompilerParams(vmem_limit_bytes=VMEM_BYTES),
    )(scalars, places, front, source)


def halves(x):
    high = x.astype(jnp.bfloat16)
    return high, (x - high.astype(jnp.float32)).astype(jnp.bfloat16)


def product(left, right, dims):
    left_high, left_low = left
    right_high, right_low = right
    dot = lambda a, b: lax.dot_general(a, b, (dims, ((), ())), preferred_element_type=jnp.float32)
    return dot(left_high, right_high) + (dot(left_high, right_low) + dot(left_low, right_high))


PLAIN = ((1,), (0,))
CROSS = ((1,), (1,))


def factor_kernel(flags, gathered_ref, corner_ref, first_ref, second_ref, fixed_ref):
    place, kept = flags[0], flags[1]
    gathered = gathered_ref[...]
    thin = (gathered.shape[1] - 8) // 2
    strip = gathered[:, :thin].reshape(PANEL, 2 * PANEL)
    pieces = gathered[:, thin : 2 * thin]
    inverse = jnp.concatenate([pieces[:, 8 * q : 8 * q + 8].reshape(PANEL * 8 // thin, 2 * PANEL) for q in range(thin // 8)])
    inverse0, inverse1 = inverse[:, :PANEL], inverse[:, PANEL:]
    halves0, halves1 = halves(inverse0), halves(inverse1)
    corner10 = halves(corner_ref[:, 0, :, :PANEL].reshape(PANEL, PANEL))
    corner01 = halves(corner_ref[:, 1, :, :PANEL].reshape(PANEL, PANEL))
    first = product(halves(strip[:, :PANEL]), halves0, CROSS)
    lowered = product(halves(first), corner10, PLAIN)
    pivot1 = strip[:, PANEL:] - jnp.where(kept == 1, lowered, 0.0)
    second = product(halves(pivot1), halves1, CROSS)
    second = jnp.where(place == 1, -inverse1.T, second)
    crossed = product(halves(second), corner01, PLAIN)
    fixed = product(halves(crossed), halves0, CROSS)
    first_ref[...] = jnp.where(place == 0, -inverse0.T, jnp.where(place == 1, 0.0, first))
    second_ref[...] = second
    fixed_ref[...] = fixed


def factor(flags, gathered, corner):
    square = jax.ShapeDtypeStruct((PANEL, PANEL), jnp.float32)
    return pl.pallas_call(
        factor_kernel,
        out_shape=(square, square, square),
        grid_spec=pltpu.PrefetchScalarGridSpec(
            num_scalar_prefetch=1,
            grid=(1,),
            in_specs=[
                pl.BlockSpec(gathered.shape, lambda i, _: (0, 0, 0)),
                pl.BlockSpec(corner.shape, lambda i, _: (0, 0, 0, 0)),
            ],
            out_specs=[pl.BlockSpec((PANEL, PANEL), lambda i, _: (0, 0))] * 3,
        ),
        compiler_params=pltpu.CompilerParams(vmem_limit_bytes=VMEM_BYTES),
    )(flags, gathered, corner)


def update_kernel(flags, block_ref, panels_ref, first_ref, second_ref, fixed_ref, out_ref):
    tile = pl.program_id(0)
    keep, use_first, use_fixed, use_second = (flags[4 * tile + i] == 1 for i in range(4))
    left0 = first_ref[...] - jnp.where(use_fixed, fixed_ref[...], 0.0)
    left0 = halves(jnp.where(use_first, left0, 0.0))
    left1 = halves(jnp.where(use_second, second_ref[...], 0.0))
    panel = panels_ref[...]
    right0 = halves(panel[:, 0].reshape(PANEL, PANEL))
    right1 = halves(panel[:, 1].reshape(PANEL, PANEL))
    update = product(left0, right0, PLAIN) + product(left1, right1, PLAIN)
    out_ref[...] = (jnp.where(keep, block_ref[...], 0.0) - update).T


def update(flags, block, panels, first, second, fixed):
    tiles = block.shape[1] // PANEL
    square = pl.BlockSpec((PANEL, PANEL), lambda i, _: (0, 0))
    return pl.pallas_call(
        update_kernel,
        out_shape=jax.ShapeDtypeStruct(block.shape[::-1], jnp.float32),
        grid_spec=pltpu.PrefetchScalarGridSpec(
            num_scalar_prefetch=1,
            grid=(tiles,),
            in_specs=[
                pl.BlockSpec((PANEL, PANEL), lambda i, _: (0, i)),
                pl.BlockSpec(panels.shape[:3] + (PANEL,), lambda i, _: (0, 0, 0, i)),
                square,
                square,
                square,
            ],
            out_specs=pl.BlockSpec((PANEL, PANEL), lambda i, _: (i, 0)),
        ),
        compiler_params=pltpu.CompilerParams(vmem_limit_bytes=VMEM_BYTES),
    )(flags, block, panels, first, second, fixed)


def local(front_entries, child_blocks, row_maps, pivot_inverses, tile_mask):
    thin, half_rows = front_entries.shape[2:]
    child_rows = child_blocks.shape[4]
    grid_rows = lax.axis_size("row")
    grid_cols = lax.axis_size("col")
    side = lax.axis_index("subcube")
    row_place = lax.axis_index("row")
    place = lax.axis_index("col")
    row_count = half_rows // grid_rows
    chunks = thin // 8
    pivot_rows = PANELS * PANEL
    own = child_blocks[0, 0, 0]
    front = front_entries[0, 0]
    one = jnp.ones((), jnp.int32)

    window = -(-(child_rows * 13 // 24) // LANES) * LANES
    rest = child_rows - window
    to_send = jnp.where(side == 0, own[:, rest:], own[:, :window])
    swap = lambda cols: [(s * grid_cols + c, (1 - s) * grid_cols + c) for s in range(2) for c in cols]
    panel_cols, other_cols = range(PANELS), range(PANELS, grid_cols)
    exchange = lambda x, cols: lax.ppermute(x, ("subcube", "col"), swap(cols))
    received_panel = exchange(to_send, panel_cols)

    map_blocks = child_rows // LANES
    blocks = half_rows // LANES
    strip_blocks = pivot_rows // LANES
    first_row = (side * half_rows).astype(jnp.int32)
    own_map = lax.dynamic_index_in_dim(row_maps, side, 0, keepdims=False)
    other_map = lax.dynamic_index_in_dim(row_maps, 1 - side, 0, keepdims=False)
    count = lambda maps, edges: jnp.sum((maps[:, None, :] < edges[None, :, None]).astype(jnp.int32), axis=2)
    edges = LANES * jnp.arange(blocks, dtype=jnp.int32)
    starts = count(jnp.stack([own_map, other_map]), first_row + edges)
    strip_starts = count(row_maps[1:2], edges[:strip_blocks])[0]
    places = search(
        row_maps.reshape(2, map_blocks, LANES),
        [side.astype(jnp.int32), (1 - side).astype(jnp.int32), one],
        [first_row, first_row, one * 0],
        [starts[0], starts[1], strip_starts],
    )
    lower = jnp.sum((row_maps < half_rows).astype(jnp.int32), axis=1)
    spill = (child_rows - lower[0] > window) | (lower[1] > window)
    window_at = jnp.where(side == 0, 0, rest // LANES).astype(jnp.int32)
    rest_at = jnp.where(side == 0, window // LANES, 0).astype(jnp.int32)
    assembled_own = extend_add(front, own, places, 0, starts[0], one * 0, map_blocks, grid_rows)

    def add_other(base, received, cols):
        def add_rest(x):
            more = exchange(jnp.where(side == 0, own[:, :rest], own[:, window:]), cols)
            return extend_add(x, more, places, blocks, starts[1], rest_at, map_blocks, grid_rows)

        added = extend_add(base, received, places, blocks, starts[1], window_at, map_blocks, grid_rows)
        return lax.cond(spill, add_rest, lambda x: x, added)

    masks_here = tile_mask.astype(jnp.float32)[:, 0]
    mask_rows = jnp.zeros((8, pivot_rows), jnp.float32).at[0, : tile_mask.shape[0]].set(masks_here)
    prefix = own[:, :pivot_rows]
    base_here = assembled_own[0, :, :pivot_rows]
    strip_sent = jnp.concatenate([jnp.where(side == 0, base_here, prefix), mask_rows])
    strip_got = lax.ppermute(strip_sent, "subcube", [(0, 1), (1, 0)])
    strip = extend_add(
        jnp.where(side == 0, base_here, strip_got[:thin]),
        jnp.where(side == 0, strip_got[:thin], prefix),
        places, 2 * blocks, strip_starts, one * 0, map_blocks, 1,
    )[0]
    first_masks = jnp.where(side == 0, mask_rows, strip_got[thin:])

    to_chips = lambda chunk: [(k, PANELS * chunk + k) for k in range(PANELS)]

    def scatter(pieces):
        mine = jnp.where(place // PANELS == 0, pieces[0], 0.0)
        for chunk in range(1, chunks):
            mine = mine + lax.ppermute(pieces[chunk], "col", to_chips(chunk))
        return mine

    corner_source = jnp.where(place == 0, strip[:, PANEL:], strip[:, :PANEL])
    corner_here = scatter([corner_source[8 * q : 8 * q + 8] for q in range(chunks)])
    pieces = jnp.concatenate([pivot_inverses[k] for k in range(PANELS)], axis=1)
    tail = jnp.concatenate([corner_here, first_masks[:, :PANEL]], axis=1)
    gathered = lax.all_gather(jnp.concatenate([strip, pieces, tail]), "row", axis=0)
    corner = gathered[:, 2 * thin :, :PANEL].reshape(thin, PANEL)
    mask_lanes = jnp.broadcast_to(mask_rows[:1, :LANES], (thin, LANES))
    corner = lax.all_gather(jnp.concatenate([corner, mask_lanes], axis=1), "col", axis=0, tiled=True)
    corner = corner.reshape(chunks, PANELS, thin, PANEL + LANES)
    kept = gathered[0, 2 * thin, PANEL + 1] > 0.5
    cross_mask = corner[0, 1, 0, PANEL : PANEL + tile_mask.shape[0]] > 0.5

    assembled_panel = add_other(assembled_own, received_panel, panel_cols)
    to_send, received_panel = lax.optimization_barrier((to_send, received_panel))
    received_other = exchange(to_send, other_cols)
    flat = assembled_panel.reshape(grid_rows, chunks, 8, row_count)
    mine = scatter([flat[:, q] for q in range(chunks)])
    mine = lax.all_to_all(mine, "row", split_axis=0, concat_axis=0, tiled=True)
    panels = lax.all_gather(mine.reshape(thin, row_count), "col", axis=0, tiled=True)
    panels = panels.reshape(chunks, PANELS, thin, row_count)

    assembled = add_other(assembled_panel, received_other, other_cols)
    assembled, mine = lax.optimization_barrier((assembled, mine))
    block = lax.all_to_all(assembled, "row", split_axis=0, concat_axis=0, tiled=True)
    block = block.reshape(PANEL, row_count)

    first, second, fixed = factor(jnp.stack([place, kept.astype(place.dtype)]).astype(jnp.int32), gathered, corner)

    tiles = row_count // PANEL
    tile_ids = (side * grid_rows + row_place) * tiles + jnp.arange(tiles, dtype=jnp.int32)
    own_mask = tile_mask[:, 0] == 1
    is0, is1 = place == 0, place == 1
    keep = jnp.where(is0, False, jnp.where(is1, tile_ids == 0, True))
    use_first = jnp.where(is0, True, jnp.where(is1, tile_ids >= 1, own_mask & (tile_ids >= 1)))
    use_fixed = jnp.where(is0, False, cross_mask & (tile_ids >= jnp.where(is1, 1, 2)))
    use_second = jnp.where(is0, False, jnp.where(is1, tile_ids >= 1, own_mask & (tile_ids >= 2)))
    flags = jnp.stack([keep, use_first, use_fixed, use_second], axis=1).astype(jnp.int32).reshape(-1)
    return update(flags, block, panels, first, second, fixed)


def solution(mesh):
    return jax.shard_map(
        local,
        mesh=mesh,
        in_specs=(
            P("col", "row", None, "subcube"),
            P("subcube", "col", "row", None, None),
            P(),
            P(None, "row", None),
            P(("subcube", "row"), "col"),
        ),
        out_specs=P(("subcube", "row"), "col"),
        check_vma=False,
    )
```

time: 578 us -> 396 us (0.69)
  the two profiles are of different devices: /device:TPU:1 before, /device:TPU:22 now
where the time goes in v2:
time: 396 us; the launch traced here: 394 us
  waiting for transfers between devices  258 us (65%)
  Pallas kernels  52.8 us (13%)
  starting transfers between devices  20.5 us (5%)
  blocking collectives  16.8 us (4%)
  other arithmetic  16.3 us (4%)
  between operations  15.4 us (4%)
  local copies, waits for them, and re-layouts  14.9 us (4%)
    ppermute x14, waiting for transfers between devices, scatter(): mine = mine + lax.ppermute(pieces[chunk], 'col', to_chips(chunk))  75.3 us
    all_gather x1, waiting for transfers between devices, local(): lax.all_gather(jnp.concatenate([strip, pieces, tail]), 'row', axis=0)  64.3 us
    ppermute x2, waiting for transfers between devices, local(): exchange = lambda x, cols: lax.ppermute(x, ('subcube', 'col'), swap(cols))  62.1 us
    all_to_all x1, waiting for transfers between devices, local(): lax.all_to_all(assembled, 'row', split_axis=0, concat_axis=0, tiled=True)  46.4 us
    pallas_call x4, Pallas kernels, extend_add(): pl.pallas_call(functools.partial(extend_kernel, first_place, map_blocks),...  28.6 us
    all_to_all x1, blocking collectives, local(): mine = lax.all_to_all(mine, 'row', split_axis=0, concat_axis=0, tiled=True)  16.8 us
    ppermute x14, starting transfers between devices, scatter(): mine = mine + lax.ppermute(pieces[chunk], 'col', to_chips(chunk))  11.8 us
    pallas_call x1, Pallas kernels, update(): pl.pallas_call(update_kernel, out_shape=jax.ShapeDtypeStruct(block.shape[...  10.8 us
  transfers between devices with their start and end apart: 21, of which 6 were waited for; matrix products, arithmetic and copies ran while one was open for 3% of the time, Pallas kernels for 7%

profile of v2, /device:TPU:22, one launch (start us, length us, event | category | flops | bytes accessed | tf_op | source)
XLA Modules:
  0.0 394.4 jit_solution(6655978214045727890)
XLA Ops:
  7.2 1.5 copy.31
  8.7 1.2 fusion.23
  10.0 1.1 convert_reduce_fusion
  12.8 4.4 %shard_map.55.places_ref = s32[200,128]{1,0:T(8,128)S(1)} custom-call(s32[206]{0:T(256)} %concatenate.37.scalars, s32[2,96,128]{2,1,0:T(8,128)} %bitcast.134), custom_call_target="tpu_custom_call" | custom-call | tf_op jit(solution)/shard_map/pallas_call | solution.py:53
  17.2 9.1 %shard_map.56.front_ref = f32[8,64,1536]{2,1,0:T(8,128)} custom-call(s32[97]{0:T(128)} %pad_add_fusion.4.scalars, s32[200,128]{1,0:T(8,128)S(1)} %shard_map.55.places_ref, f32[64,12288]{1,0:T(8,128)} %bitcast.127, f32[64,12288]{1,0:T(8,128)} %bitcast.114), custom_call_target="tpu_custom_call" | custom-call | tf_op jit(solution)/shard_map/pallas_call | solution.py:102
  26.2 1.0 fusion.10
  27.2 0.7 pad_maximum_fusion
  29.0 9.5 %collective-permute-done.2 = f32[72,1024]{1,0:T(8,128)S(1)} collective-permute-done((f32[72,1024]{1,0:T(8,128)}, f32[72,1024]{1,0:T(8,128)S(1)}, u32[]{:S(2)}, u32[]{:S(2)}) %collective-permute-start.2) | collective-permute-done | bytes 294944 | tf_op jit(solution)/shard_map/ppermute | solution.py:265
  38.5 1.9 slice_select_fusion.3
  40.4 2.7 shard_map.57
  43.0 1.0 slice_select_fusion.4
  44.7 1.2 collective-permute-start.3
  45.9 1.3 collective-permute-start.9
  47.2 1.6 slice_bitcast_fusion.13
  48.8 1.3 collective-permute-start.8
  51.4 0.8 slice.199
  53.6 3.6 collective-permute-done.8
  57.2 0.8 fusion.18
  58.0 1.9 maximum_maximum_fusion
  60.0 64.3 %all-gather.9.cloned.1.call-done = f32[1088,1024]{1,0:T(8,128)} async-done(((f32[136,1024]{1,0:T(8,128)}), f32[1088,1024]{1,0:T(8,128)}) %all-gather.9.cloned.1.call-update) | async-done | bytes 4456464 | tf_op jit(solution)/shard_map/all_gather | solution.py:285
  124.3 0.9 slice_bitcast_fusion.11
  125.2 0.7 pad_maximum_fusion.1
  126.0 1.4 slice_select_fusion.2
  127.4 1.9 collective-permute-start.10
  132.1 8.5 %shard_map.58 = f32[8,64,1536]{2,1,0:T(8,128)} custom-call(s32[97]{0:T(128)} %pad_add_fusion.5.scalars, s32[200,128]{1,0:T(8,128)S(1)} %shard_map.55.places_ref, f32[8,64,1536]{2,1,0:T(8,128)} %shard_map.56.front_ref, f32[64,6656]{1,0:T(8,128)} %collective-permute-done.10.source_ref), custom_call_target="tpu_custom_call" | custom-call | tf_op jit(solution)/shard_map/pallas_call | solution.py:102
  140.5 1.9 slice_bitcast_fusion.8
  142.4 0.7 collective-permute-start.12
  143.1 0.7 collective-permute-start.16
  143.8 0.7 collective-permute-start.15
  144.5 0.7 collective-permute-start.14
  145.2 0.7 collective-permute-start.13
  145.9 0.7 collective-permute-start.18
  146.6 1.3 collective-permute-start.17
  147.9 71.6 %collective-permute-done.17 = f32[8,8,1536]{2,1,0:T(8,128)S(1)} collective-permute-done((f32[8,8,1536]{2,1,0:T(8,128)S(1)}, f32[8,8,1536]{2,1,0:T(8,128)S(1)}, u32[]{:S(2)}, u32[]{:S(2)}) %collective-permute-start.17) | collective-permute-done | bytes 393248 | tf_op jit(solution)/shard_map/ppermute | solution.py:278
  219.6 1.2 fusion.8
  220.7 16.8 %all_to_all.10 = f32[8,8,1536]{2,1,0:T(8,128)} all-to-all(f32[8,8,1536]{2,1,0:T(8,128)S(1)} %fusion.8), channel_id=1, replica_groups=mesh['subcube'=2,'row'=8,'col'=16] {'row'}, dimensions={0} | all-to-all | bytes 786432 | tf_op jit(solution)/shard_map/all_to_all | solution.py:298
  237.5 2.4 collective-permute-start.11
  240.0 62.1 %collective-permute-done.11.source_ref = f32[64,6656]{1,0:T(8,128)S(1)} collective-permute-done((f32[64,6656]{1,0:T(8,128)}, f32[64,6656]{1,0:T(8,128)S(1)}, u32[]{:S(2)}, u32[]{:S(2)}) %collective-permute-start.11) | collective-permute-done | bytes 1703968 | tf_op jit(solution)/shard_map/ppermute | solution.py:227
  302.1 1.2 copy-done.4
  303.3 8.4 %shard_map.59 = f32[8,64,1536]{2,1,0:T(8,128)} custom-call(s32[97]{0:T(128)} %pad_add_fusion.5.scalars, s32[200,128]{1,0:T(8,128)S(1)} %shard_map.55.places_ref, f32[8,64,1536]{2,1,0:T(8,128)} %get-tuple-element.98.front_ref, f32[64,6656]{1,0:T(8,128)} %copy-done.4), custom_call_target="tpu_custom_call" | custom-call | tf_op jit(solution)/shard_map/pallas_call | solution.py:102
  311.7 4.0 %all-to-all-start.1 = ((f32[8,64,1536]{2,1,0:T(8,128)}), f32[8,64,1536]{2,1,0:T(8,128)S(1)}, u32[]{:S(2)}, u32[]{:S(2)}) async-start(f32[8,64,1536]{2,1,0:T(8,128)} %get-tuple-element.99), calls=%async_computation.1 | async-start | bytes 6291456 | tf_op jit(solution)/shard_map/all_to_all | solution.py:304
  315.7 1.3 slice.213
  318.4 9.1 %shard_map.60 = (f32[512,512]{1,0:T(8,128)}, f32[512,512]{1,0:T(8,128)}, f32[512,512]{1,0:T(8,128)}) custom-call(s32[2]{0:T(128)} %pad_add_fusion.6.flags, f32[8,136,1024]{2,1,0:T(8,128)} %bitcast.126, f32[8,2,64,640]{3,2,1,0:T(8,128)} %bitcast.128), custom_call_target="tpu_custom_call" | custom-call | tf_op jit(solution)/shard_map/pallas_call | solution.py:156
  327.5 0.7 fusion.20
  328.3 0.7 reshape.201.flags
  329.0 46.4 %all-to-all-done.1 = f32[8,64,1536]{2,1,0:T(8,128)S(1)} async-done(((f32[8,64,1536]{2,1,0:T(8,128)}), f32[8,64,1536]{2,1,0:T(8,128)S(1)}, u32[]{:S(2)}, u32[]{:S(2)}) %all-to-all-start.1) | async-done | bytes 3145760 | tf_op jit(solution)/shard_map/all_to_all | solution.py:304
  375.4 1.7 copy-done.3
  377.1 10.8 %shard_map.61 = f32[1536,512]{1,0:T(8,128)} custom-call(s32[12]{0:T(128)} %reshape.201.flags, f32[512,1536]{1,0:T(8,128)} %bitcast.122, f32[8,2,64,1536]{3,2,1,0:T(8,128)} %bitcast.123, f32[512,512]{1,0:T(8,128)} %get-tuple-element.68.first_ref, f32[512,512]{1,0:T(8,128)} %get-tuple-element.69.second_ref, f32[512,512]{1,0:T(8,128)} %get-tuple-element.70.fixed_ref), custom_call_target="tpu_custom_call" | custom-call | tf_op jit(solution)/shard_map/pallas_call | solution.py:188
  (64 shorter events, 9.1 us)
Async XLA Ops:
  6.5 117.8 %all-gather.9.cloned.1.call-start = ((), (), s32[]{:S(2)}) async-start(), calls=%async_computation.4 | async-start | bytes 5013504 | tf_op jit(solution)/shard_map/all_gather | solution.py:285
  11.1 1.6 copy-start.9
  17.2 9.1 %copy-start = (f32[1,1,1,64,12288]{4,3,2,1,0:T(8,128)S(1)}, f32[1,1,1,64,12288]{4,3,2,1,0:T(8,128)}, u32[]{:S(2)}) copy-start(f32[1,1,1,64,12288]{4,3,2,1,0:T(8,128)} %param.12) | copy-start | bytes 9437188
  28.0 10.5 %collective-permute-start.2 = (f32[72,1024]{1,0:T(8,128)}, f32[72,1024]{1,0:T(8,128)S(1)}, u32[]{:S(2)}, u32[]{:S(2)}) collective-permute-start(f32[72,1024]{1,0:T(8,128)} %pad_maximum_fusion), channel_id=1, source_target_pairs={{0,128},{128,0},{1,129},{129,1},{2,130},{130,2},{3,131},{131,3},{4... | collective-permute-start | bytes 884744 | tf_op jit(solution)/shard_map/ppermute | solution.py:265
  38.4 4.6 %copy-start.8 = (f32[72,1024]{1,0:T(8,128)}, f32[72,1024]{1,0:T(8,128)S(1)}, u32[]{:S(2)}) copy-start(f32[72,1024]{1,0:T(8,128)S(1)} %collective-permute-done.2) | copy-start | bytes 884740
  44.7 7.5 %collective-permute-start.3 = (f32[8,512]{1,0:T(8,128)}, f32[8,512]{1,0:T(8,128)}, u32[]{:S(2)}, u32[]{:S(2)}) collective-permute-start(f32[8,512]{1,0:T(8,128)} %get-tuple-element.82), channel_id=1, source_target_pairs={{0,2},{1,3},{16,18},{17,19},{32,34},{33,35},{48,50},{49,51},{64,66... | collective-permute-start | bytes 49160 | tf_op jit(solution)/shard_map/ppermute | solution.py:278
  45.9 6.9 %collective-permute-start.9 = (f32[8,512]{1,0:T(8,128)}, f32[8,512]{1,0:T(8,128)}, u32[]{:S(2)}, u32[]{:S(2)}) collective-permute-start(f32[8,512]{1,0:T(8,128)} %get-tuple-element.83), channel_id=1, source_target_pairs={{0,14},{1,15},{16,30},{17,31},{32,46},{33,47},{48,62},{49,63},{64,... | collective-permute-start | bytes 49160 | tf_op jit(solution)/shard_map/ppermute | solution.py:278
  48.8 8.4 %collective-permute-start.8 = (f32[8,512]{1,0:T(8,128)}, f32[8,512]{1,0:T(8,128)S(1)}, u32[]{:S(2)}, u32[]{:S(2)}) collective-permute-start(f32[8,512]{1,0:T(8,128)} %get-tuple-element.84), channel_id=1, source_target_pairs={{0,12},{1,13},{16,28},{17,29},{32,44},{33,45},{48,60},{49,61},{64,... | collective-permute-start | bytes 49160 | tf_op jit(solution)/shard_map/ppermute | solution.py:278
  50.1 7.1 %collective-permute-start.7 = (f32[8,512]{1,0:T(8,128)}, f32[8,512]{1,0:T(8,128)S(1)}, u32[]{:S(2)}, u32[]{:S(2)}) collective-permute-start(f32[8,512]{1,0:T(8,128)} %get-tuple-element.85), channel_id=1, source_target_pairs={{0,10},{1,11},{16,26},{17,27},{32,42},{33,43},{48,58},{49,59},{64,... | collective-permute-start | bytes 49160 | tf_op jit(solution)/shard_map/ppermute | solution.py:278
  50.8 6.4 %collective-permute-start.6 = (f32[8,512]{1,0:T(8,128)}, f32[8,512]{1,0:T(8,128)S(1)}, u32[]{:S(2)}, u32[]{:S(2)}) collective-permute-start(f32[8,512]{1,0:T(8,128)} %get-tuple-element.86), channel_id=1, source_target_pairs={{0,8},{1,9},{16,24},{17,25},{32,40},{33,41},{48,56},{49,57},{64,72... | collective-permute-start | bytes 49160 | tf_op jit(solution)/shard_map/ppermute | solution.py:278
  52.2 5.0 %collective-permute-start.5 = (f32[8,512]{1,0:T(8,128)S(1)}, f32[8,512]{1,0:T(8,128)S(1)}, u32[]{:S(2)}, u32[]{:S(2)}) collective-permute-start(f32[8,512]{1,0:T(8,128)S(1)} %get-tuple-element.87), channel_id=1, source_target_pairs={{0,6},{1,7},{16,22},{17,23},{32,38},{33,39},{48,54},{49,55},{64,70... | collective-permute-start | bytes 49160 | tf_op jit(solution)/shard_map/ppermute | solution.py:278
  52.9 4.3 %collective-permute-start.4 = (f32[8,512]{1,0:T(8,128)S(1)}, f32[8,512]{1,0:T(8,128)S(1)}, u32[]{:S(2)}, u32[]{:S(2)}) collective-permute-start(f32[8,512]{1,0:T(8,128)S(1)} %get-tuple-element.88), channel_id=1, source_target_pairs={{0,4},{1,5},{16,20},{17,21},{32,36},{33,37},{48,52},{49,53},{64,68... | collective-permute-start | bytes 49160 | tf_op jit(solution)/shard_map/ppermute | solution.py:278
  59.9 69.4 %copy-start.7 = (s32[2,12288]{1,0:T(2,128)S(1)}, s32[2,12288]{1,0:T(2,128)}, u32[]{:S(2)}) copy-start(s32[2,12288]{1,0:T(2,128)} %param.13) | copy-start | bytes 294916
  59.9 71.5 %copy-start.10 = (s32[96]{0:T(128)S(1)}, s32[96]{0:T(128)}, u32[]{:S(2)}) copy-start(s32[96]{0:T(128)} %copy-done.9) | copy-start | bytes 1156
  59.9 258.5 %all-gather.5.cloned.1.call-start = ((), (), s32[]{:S(2)}) async-start(), calls=%async_computation.2 | async-start | bytes 2785280 | tf_op jit(solution)/shard_map/all_gather | solution.py:288
  125.9 249.5 %all-gather.7.cloned.1.call-start = ((), (), s32[]{:S(2)}) async-start(), calls=%async_computation.3 | async-start | bytes 6684672 | tf_op jit(solution)/shard_map/all_gather | solution.py:299
  127.4 4.7 %collective-permute-start.10 = (f32[64,6656]{1,0:T(8,128)}, f32[64,6656]{1,0:T(8,128)}, u32[]{:S(2)}, u32[]{:S(2)}) collective-permute-start(f32[64,6656]{1,0:T(8,128)} %slice_select_fusion.2), channel_id=1, source_target_pairs={{0,128},{1,129},{128,0},{129,1},{16,144},{17,145},{144,16},{145,17... | collective-permute-start | bytes 5111816 | tf_op jit(solution)/shard_map/ppermute | solution.py:227
  142.4 3.5 collective-permute-start.12
  143.1 3.5 collective-permute-start.16
  143.8 4.1 %collective-permute-start.15 = (f32[8,8,1536]{2,1,0:T(8,128)S(1)}, f32[8,8,1536]{2,1,0:T(8,128)S(1)}, u32[]{:S(2)}, u32[]{:S(2)}) collective-permute-start(f32[8,8,1536]{2,1,0:T(8,128)S(1)} %get-tuple-element.73), channel_id=1, source_target_pairs={{0,8},{1,9},{16,24},{17,25},{32,40},{33,41},{48,56},{49,57},{64,72... | collective-permute-start | bytes 1179656 | tf_op jit(solution)/shard_map/ppermute | solution.py:278
  144.5 3.4 collective-permute-start.14
  145.2 2.7 collective-permute-start.13
  145.9 2.0 collective-permute-start.18
  146.6 73.0 %collective-permute-start.17 = (f32[8,8,1536]{2,1,0:T(8,128)S(1)}, f32[8,8,1536]{2,1,0:T(8,128)S(1)}, u32[]{:S(2)}, u32[]{:S(2)}) collective-permute-start(f32[8,8,1536]{2,1,0:T(8,128)S(1)} %get-tuple-element.77), channel_id=1, source_target_pairs={{0,12},{1,13},{16,28},{17,29},{32,44},{33,45},{48,60},{49,61},{64,... | collective-permute-start | bytes 1179656 | tf_op jit(solution)/shard_map/ppermute | solution.py:278
  237.5 64.5 %collective-permute-start.11 = (f32[64,6656]{1,0:T(8,128)}, f32[64,6656]{1,0:T(8,128)S(1)}, u32[]{:S(2)}, u32[]{:S(2)}) collective-permute-start(f32[64,6656]{1,0:T(8,128)} %slice_select_fusion.2), channel_id=1, source_target_pairs={{2,130},{3,131},{4,132},{5,133},{6,134},{7,135},{8,136},{9,137},{1... | collective-permute-start | bytes 5111816 | tf_op jit(solution)/shard_map/ppermute | solution.py:227
  302.1 1.2 copy-start.4
  311.7 4.0 %copy-start.11 = (s32[3,1]{0,1:T(1,128)S(1)}, s32[3,1]{0,1:T(1,128)}, u32[]{:S(2)}) copy-start(s32[3,1]{0,1:T(1,128)} %param.15) | copy-start | bytes 40
  311.7 63.7 %all-to-all-start.1 = ((f32[8,64,1536]{2,1,0:T(8,128)}), f32[8,64,1536]{2,1,0:T(8,128)S(1)}, u32[]{:S(2)}, u32[]{:S(2)}) async-start(f32[8,64,1536]{2,1,0:T(8,128)} %get-tuple-element.99), calls=%async_computation.1 | async-start | bytes 6291456 | tf_op jit(solution)/shard_map/all_to_all | solution.py:304
  375.4 1.7 copy-start.3
Sparse Core Ops, SparseCore 0:
  60.0 64.2 all-gather.8
  126.1 36.1 all-gather.4
  237.6 66.9 all-gather.6

commit v3 on v2

v3 whole, which is shorter than its diff:
```python
import functools

import jax
import jax.numpy as jnp
from jax import lax
from jax.experimental import pallas as pl
from jax.experimental.pallas import tpu as pltpu
from jax.sharding import PartitionSpec as P

PANEL = 512
PANELS = 2
LANES = 128
BIG = 2**30
VMEM_BYTES = 56 * 2**20


def search_kernel(sections, scalars, maps_ref, places_ref, low_ref, high_ref):
    map_blocks = maps_ref.shape[1]
    at_row = 0
    for section, count in enumerate(sections):
        child = scalars[section]
        first = scalars[len(sections) + section]
        for block in range(count):
            at = jnp.minimum(scalars[2 * len(sections) + at_row + block] // LANES, map_blocks - 1)
            after = jnp.minimum(at + 1, map_blocks - 1)
            row = at_row + block
            low_ref[row : row + 1, :] = maps_ref[child, pl.ds(at, 1), :]
            high_ref[row : row + 1, :] = jnp.where(at + 1 < map_blocks, maps_ref[child, pl.ds(after, 1), :], BIG)
        low, high = low_ref[at_row : at_row + count, :], high_ref[at_row : at_row + count, :]
        lane = lax.broadcasted_iota(jnp.int32, low.shape, 1)
        block_id = lax.broadcasted_iota(jnp.int32, low.shape, 0)
        wanted = first + block_id * LANES + lane

        def pick(at):
            inner = at & (LANES - 1)
            return jnp.where(
                at < LANES, jnp.take_along_axis(low, inner, axis=1), jnp.take_along_axis(high, inner, axis=1)
            )

        place = jnp.zeros(low.shape, jnp.int32)
        width = LANES
        while width >= 1:
            place = jnp.where(pick(place + (width - 1)) < wanted, place + width, place)
            width //= 2
        places_ref[at_row : at_row + count, :] = jnp.where(pick(place) == wanted, place, -1)
        at_row += count


def search(maps, children, firsts, starts):
    sections = tuple(start.shape[0] for start in starts)
    total = sum(sections)
    scalars = jnp.concatenate([jnp.stack(children), jnp.stack(firsts)] + list(starts)).astype(jnp.int32)
    return pl.pallas_call(
        functools.partial(search_kernel, sections),
        out_shape=jax.ShapeDtypeStruct((total, LANES), jnp.int32),
        grid_spec=pltpu.PrefetchScalarGridSpec(
            num_scalar_prefetch=1,
            grid=(1,),
            in_specs=[pl.BlockSpec(maps.shape, lambda i, _: (0, 0, 0))],
            out_specs=pl.BlockSpec((total, LANES), lambda i, _: (0, 0)),
            scratch_shapes=[pltpu.VMEM((total, LANES), jnp.int32)] * 2,
        ),
        compiler_params=pltpu.CompilerParams(vmem_limit_bytes=VMEM_BYTES),
    )(scalars, maps)


def extend_kernel(first_place, map_blocks, scalars, places_ref, front_ref, source_ref, out_ref, *piece_refs):
    step = pl.program_id(0)
    columns = out_ref.shape[1]
    per_step = out_ref.shape[2] // LANES
    source_blocks = source_ref.shape[1] // LANES
    offset = scalars[scalars.shape[0] - 1]
    lane = lax.broadcasted_iota(jnp.int32, (8, LANES), 1)
    for j in range(per_step):
        block = step * per_step + j
        start = scalars[block]
        at = jnp.minimum(start // LANES, map_blocks - 1)
        split = jnp.where(start // LANES < map_blocks, start & (LANES - 1), LANES)
        at = at - offset
        inside_low = (at >= 0) & (at < source_blocks)
        inside_high = (at + 1 >= 0) & (at + 1 < source_blocks)
        low_at = pl.multiple_of(jnp.clip(at, 0, source_blocks - 1) * LANES, LANES)
        high_at = pl.multiple_of(jnp.clip(at + 1, 0, source_blocks - 1) * LANES, LANES)
        place = jnp.broadcast_to(places_ref[pl.ds(first_place + block, 1), :], (8, LANES))
        inner = place & (LANES - 1)
        hit = ((place >= 0) & (place < LANES) & inside_low) | ((place >= LANES) & inside_high)
        from_low = lane >= split
        here = slice(j * LANES, (j + 1) * LANES)
        for row in range(0, columns, 8):
            rows = slice(row, row + 8)
            merged = jnp.where(from_low, source_ref[rows, pl.ds(low_at, LANES)], source_ref[rows, pl.ds(high_at, LANES)])
            gained = jnp.where(hit, jnp.take_along_axis(merged, inner, axis=1), 0.0)
            value = front_ref[..., rows, here].reshape(8, LANES) + gained
            out_ref[0, rows, here] = value
            if piece_refs:
                piece_refs[row // 8][0, :, here] = value


def extend_add(front, source, places, first_place, starts, offset, map_blocks, steps, part=0, pieces=0):
    columns = source.shape[0]
    if front.ndim == 2:
        width = front.shape[1] // steps
        front_spec = pl.BlockSpec((columns, width), lambda i, _: (0, i))
    else:
        width = front.shape[2]
        front_spec = pl.BlockSpec((1, columns, width), lambda i, _: (i, part, 0))
    scalars = jnp.concatenate([starts, offset.reshape(1)]).astype(jnp.int32)
    whole = lambda shape: pl.BlockSpec(shape, lambda i, _: (0,) * len(shape), pipeline_mode=pl.Buffered(1))
    sizes = [columns] + [8] * pieces
    outs = pl.pallas_call(
        functools.partial(extend_kernel, first_place, map_blocks),
        out_shape=[jax.ShapeDtypeStruct((steps, size, width), jnp.float32) for size in sizes],
        grid_spec=pltpu.PrefetchScalarGridSpec(
            num_scalar_prefetch=1,
            grid=(steps,),
            in_specs=[whole(places.shape), front_spec, whole(source.shape)],
            out_specs=[pl.BlockSpec((1, size, width), lambda i, _: (i, 0, 0)) for size in sizes],
        ),
        compiler_params=pltpu.CompilerParams(vmem_limit_bytes=VMEM_BYTES),
    )(scalars, places, front, source)
    return outs if pieces else outs[0]


def halves(x):
    high = x.astype(jnp.bfloat16)
    return high, (x - high.astype(jnp.float32)).astype(jnp.bfloat16)


def product(left, right, dims):
    left_high, left_low = left
    right_high, right_low = right
    dot = lambda a, b: lax.dot_general(a, b, (dims, ((), ())), preferred_element_type=jnp.float32)
    return dot(left_high, right_high) + (dot(left_high, right_low) + dot(left_low, right_high))


PLAIN = ((1,), (0,))
CROSS = ((1,), (1,))


def factor_kernel(flags, gathered_ref, first_ref, second_ref, fixed_ref):
    place, kept = flags[0], flags[1]
    thin = (gathered_ref.shape[1] - 8) // 3
    by_chip = lambda x: jnp.concatenate([x[:, 8 * q : 8 * q + 8].reshape(-1, x.shape[2]) for q in range(thin // 8)])
    strip = gathered_ref[:, :thin].reshape(PANEL, 2 * PANEL)
    corner = by_chip(gathered_ref[:, thin : 2 * thin])
    inverse = by_chip(gathered_ref[:, 2 * thin : 3 * thin])
    inverse0, inverse1 = inverse[:, :PANEL], inverse[:, PANEL:]
    halves0, halves1 = halves(inverse0), halves(inverse1)
    corner10, corner01 = halves(corner[:, :PANEL]), halves(corner[:, PANEL:])
    first = product(halves(strip[:, :PANEL]), halves0, CROSS)
    lowered = product(halves(first), corner10, PLAIN)
    pivot1 = strip[:, PANEL:] - jnp.where(kept == 1, lowered, 0.0)
    second = product(halves(pivot1), halves1, CROSS)
    second = jnp.where(place == 1, -inverse1.T, second)
    crossed = product(halves(second), corner01, PLAIN)
    fixed = product(halves(crossed), halves0, CROSS)
    first_ref[...] = jnp.where(place == 0, -inverse0.T, jnp.where(place == 1, 0.0, first))
    second_ref[...] = second
    fixed_ref[...] = fixed


def factor(flags, gathered):
    square = jax.ShapeDtypeStruct((PANEL, PANEL), jnp.float32)
    return pl.pallas_call(
        factor_kernel,
        out_shape=(square, square, square),
        grid_spec=pltpu.PrefetchScalarGridSpec(
            num_scalar_prefetch=1,
            grid=(1,),
            in_specs=[pl.BlockSpec(gathered.shape, lambda i, _: (0, 0, 0))],
            out_specs=[pl.BlockSpec((PANEL, PANEL), lambda i, _: (0, 0))] * 3,
        ),
        compiler_params=pltpu.CompilerParams(vmem_limit_bytes=VMEM_BYTES),
    )(flags, gathered)


def update_kernel(flags, *refs):
    part_refs, (panels_ref, first_ref, second_ref, fixed_ref, out_ref) = refs[:-5], refs[-5:]
    tile = pl.program_id(0)
    keep, use_first, use_fixed, use_second = (flags[4 * tile + i] == 1 for i in range(4))
    left0 = first_ref[...] - jnp.where(use_fixed, fixed_ref[...], 0.0)
    left0 = halves(jnp.where(use_first, left0, 0.0))
    left1 = halves(jnp.where(use_second, second_ref[...], 0.0))
    panel = panels_ref[...]
    right0 = halves(panel[:, 0].reshape(PANEL, PANEL))
    right1 = halves(panel[:, 1].reshape(PANEL, PANEL))
    update = product(left0, right0, PLAIN) + product(left1, right1, PLAIN)
    block = jnp.concatenate([part[...] for part in part_refs], axis=1).reshape(PANEL, PANEL)
    out_ref[...] = (jnp.where(keep, block, 0.0) - update).T


def update(flags, parts, panels, first, second, fixed):
    rows = panels.shape[3]
    square = pl.BlockSpec((PANEL, PANEL), lambda i, _: (0, 0))
    return pl.pallas_call(
        update_kernel,
        out_shape=jax.ShapeDtypeStruct((rows, PANEL), jnp.float32),
        grid_spec=pltpu.PrefetchScalarGridSpec(
            num_scalar_prefetch=1,
            grid=(rows // PANEL,),
            in_specs=[pl.BlockSpec(part.shape[:2] + (PANEL,), lambda i, _: (0, 0, i)) for part in parts]
            + [
                pl.BlockSpec(panels.shape[:3] + (PANEL,), lambda i, _: (0, 0, 0, i)),
                square,
                square,
                square,
            ],
            out_specs=pl.BlockSpec((PANEL, PANEL), lambda i, _: (i, 0)),
        ),
        compiler_params=pltpu.CompilerParams(vmem_limit_bytes=VMEM_BYTES),
    )(flags, *parts, panels, first, second, fixed)


def local(front_entries, child_blocks, row_maps, pivot_inverses, tile_mask):
    thin, half_rows = front_entries.shape[2:]
    child_rows = child_blocks.shape[4]
    grid_rows = lax.axis_size("row")
    side = lax.axis_index("subcube")
    row_place = lax.axis_index("row")
    place = lax.axis_index("col")
    row_count = half_rows // grid_rows
    chunks = thin // 8
    pivot_rows = PANELS * PANEL
    own = child_blocks[0, 0, 0]
    front = front_entries[0, 0]
    zero = jnp.zeros((), jnp.int32)
    exchange = lambda x: lax.ppermute(x, "subcube", [(0, 1), (1, 0)])

    window = -(-(child_rows * 13 // 24) // LANES) * LANES
    rest = child_rows - window
    parts = chunks // 2
    share = thin // parts
    received = []
    for p in range(parts):
        late, early = own[p * share : (p + 1) * share, rest:], own[p * share : (p + 1) * share, :window]
        received.append(exchange(jnp.where(side == 0, late, early)))

    map_blocks = child_rows // LANES
    blocks = half_rows // LANES
    strip_blocks = pivot_rows // LANES
    maps = row_maps.reshape(2, map_blocks, LANES)
    count = lambda maps, edges: jnp.sum((maps[:, None, :] < edges[None, :, None]).astype(jnp.int32), axis=2)
    edges = LANES * jnp.arange(blocks, dtype=jnp.int32)
    strip_starts = count(row_maps, edges[:strip_blocks])
    strip_places = search(maps, [zero, zero + 1], [zero, zero], [strip_starts[0], strip_starts[1]])
    strip_add = lambda base, child, t: extend_add(
        base, child, strip_places, t * strip_blocks, strip_starts[t], zero, map_blocks, 1
    )[0]
    mask_rows = jnp.zeros((8, pivot_rows), jnp.float32)
    mask_rows = mask_rows.at[0, : tile_mask.shape[0]].set(tile_mask.astype(jnp.float32)[:, 0])
    prefix = own[:, :pivot_rows]
    base = strip_add(front[:, :pivot_rows], prefix, 0)
    got = exchange(jnp.concatenate([jnp.where(side == 0, base, prefix), mask_rows]))
    strip = strip_add(jnp.where(side == 0, base, got[:thin]), jnp.where(side == 0, got[:thin], prefix), 1)
    first_masks = jnp.where(side == 0, mask_rows, got[thin:])

    def to_chips(pieces):
        mine = jnp.where(place // PANELS == 0, pieces[0], 0.0)
        for chunk in range(1, chunks):
            pairs = [(k, PANELS * chunk + k) for k in range(PANELS)]
            mine = mine + lax.ppermute(pieces[chunk], "col", pairs)
        return mine

    corner = jnp.where(place == 0, strip[:, PANEL:], strip[:, :PANEL])
    corner, received[2] = lax.optimization_barrier((corner, received[2]))
    corner = to_chips([jnp.concatenate([corner, mask_rows[:, :PANEL]])] * chunks)
    corner, received[1] = lax.optimization_barrier((corner, received[1]))
    other = lax.ppermute(corner, "col", [(c, c ^ 1) for c in range(lax.axis_size("col"))])
    core0 = place % PANELS == 0
    corner = jnp.concatenate([jnp.where(core0, corner, other), jnp.where(core0, other, corner)], axis=1)
    cross_mask = corner[thin, PANEL : PANEL + tile_mask.shape[0]] > 0.5
    inverse = jnp.concatenate([pivot_inverses[k] for k in range(PANELS)], axis=1)
    gathered = lax.all_gather(jnp.concatenate([strip, corner[:thin], inverse, first_masks]), "row", axis=0)
    kept = gathered[0, 3 * thin, 1] > 0.5

    first_row = (side * half_rows).astype(jnp.int32)
    own_map = lax.dynamic_index_in_dim(row_maps, side, 0, keepdims=False)
    other_map = lax.dynamic_index_in_dim(row_maps, 1 - side, 0, keepdims=False)
    starts = count(jnp.stack([own_map, other_map]), first_row + edges)
    places = search(
        maps,
        [side.astype(jnp.int32), (1 - side).astype(jnp.int32)],
        [first_row, first_row],
        [starts[0], starts[1]],
    )
    lower = jnp.sum((row_maps < half_rows).astype(jnp.int32), axis=1)
    spill = (child_rows - lower[0] > window) | (lower[1] > window)
    window_at = jnp.where(side == 0, 0, rest // LANES).astype(jnp.int32)
    rest_at = jnp.where(side == 0, window // LANES, 0).astype(jnp.int32)
    add = functools.partial(extend_add, places=places, map_blocks=map_blocks, steps=grid_rows)
    base = add(front, own, first_place=0, starts=starts[0], offset=zero)
    add_other = functools.partial(add, first_place=blocks, starts=starts[1])

    def add_rest(base):
        more = exchange(jnp.where(side == 0, own[:, :rest], own[:, window:]))
        return add_other(base, more, offset=rest_at)

    base = lax.cond(spill, add_rest, lambda x: x, base)

    across = lambda x: lax.all_to_all(x, "row", split_axis=0, concat_axis=0, tiled=True)
    wholes, pieces = [], []
    for p in range(parts):
        whole, *halves_of = add_other(base, received[p], offset=window_at, part=p, pieces=2)
        wholes.append(whole)
        pieces += halves_of
    mine = across(to_chips(pieces))
    panels = lax.all_gather(mine.reshape(thin, row_count), "col", axis=0, tiled=True)
    panels = panels.reshape(chunks, PANELS, thin, row_count)
    late = parts // 2
    *last, mine = lax.optimization_barrier((*wholes[late:], mine))
    moved = [across(x) for x in wholes[:late]] + [across(x) for x in last]

    first, second, fixed = factor(jnp.stack([place, kept.astype(place.dtype)]).astype(jnp.int32), gathered)

    tiles = row_count // PANEL
    tile_ids = (side * grid_rows + row_place) * tiles + jnp.arange(tiles, dtype=jnp.int32)
    own_mask = tile_mask[:, 0] == 1
    is0, is1 = place == 0, place == 1
    keep = jnp.where(is0, False, jnp.where(is1, tile_ids == 0, True))
    use_first = jnp.where(is0, True, jnp.where(is1, tile_ids >= 1, own_mask & (tile_ids >= 1)))
    use_fixed = jnp.where(is0, False, cross_mask & (tile_ids >= jnp.where(is1, 1, 2)))
    use_second = jnp.where(is0, False, jnp.where(is1, tile_ids >= 1, own_mask & (tile_ids >= 2)))
    flags = jnp.stack([keep, use_first, use_fixed, use_second], axis=1).astype(jnp.int32).reshape(-1)
    return update(flags, moved, panels, first, second, fixed)


def solution(mesh):
    return jax.shard_map(
        local,
        mesh=mesh,
        in_specs=(
            P("col", "row", None, "subcube"),
            P("subcube", "col", "row", None, None),
            P(),
            P(None, "row", None),
            P(("subcube", "row"), "col"),
        ),
        out_specs=P(("subcube", "row"), "col"),
        check_vma=False,
    )
```

time: 396 us -> 273 us (0.69)
  the two profiles are of different devices: /device:TPU:22 before, /device:TPU:10 now
where the time goes in v3:
time: 273 us; the launch traced here: 271 us
  waiting for transfers between devices  71.5 us (26%)
  blocking collectives  69.3 us (25%)
  Pallas kernels  61.4 us (22%)
  starting transfers between devices  27.9 us (10%)
  between operations  15.7 us (6%)
  other arithmetic  14.6 us (5%)
  local copies, waits for them, and re-layouts  10.8 us (4%)
    all_to_all x3, blocking collectives, local(): lax.all_to_all(x, 'row', split_axis=0, concat_axis=0, tiled=True)  69.3 us
    ppermute x14, waiting for transfers between devices, to_chips(): mine = mine + lax.ppermute(pieces[chunk], 'col', pairs)  36.2 us
    pallas_call x7, Pallas kernels, extend_add(): pl.pallas_call(functools.partial(extend_kernel, first_place, map_blocks),...  34.4 us
    all_to_all x2, waiting for transfers between devices, local(): lax.all_to_all(x, 'row', split_axis=0, concat_axis=0, tiled=True)  25.8 us
    ppermute x14, starting transfers between devices, to_chips(): mine = mine + lax.ppermute(pieces[chunk], 'col', pairs)  11.1 us
    pallas_call x1, Pallas kernels, update(): pl.pallas_call(update_kernel, out_shape=jax.ShapeDtypeStruct((rows, PANEL...  10.9 us
    ppermute x5, starting transfers between devices, local(): exchange = lambda x: lax.ppermute(x, 'subcube', [(0, 1), (1, 0)])  9.53 us
    pallas_call x1, Pallas kernels, factor(): pl.pallas_call(factor_kernel, out_shape=(square, square, square), grid_sp...  8.9 us
  transfers between devices with their start and end apart: 24, of which 7 were waited for; matrix products, arithmetic and copies ran while one was open for 5% of the time, Pallas kernels for 17%

profile of v3, /device:TPU:10, one launch (start us, length us, event | category | flops | bytes accessed | tf_op | source)
XLA Modules:
  0.0 271.0 jit_solution(6727777239169376985)
XLA Ops:
  6.5 0.8 convert_bitcast_fusion
  7.4 1.3 convert_reduce_fusion.1
  8.7 1.6 copy.10
  10.2 1.7 slice.135.front_ref
  11.9 1.7 slice.136.source_ref
  14.8 2.9 %shard_map.55.places_ref = s32[16,128]{1,0:T(8,128)} custom-call(s32[20]{0:T(128)} %concatenate.42.scalars, s32[2,96,128]{2,1,0:T(8,128)} %bitcast.55), custom_call_target="tpu_custom_call" | custom-call | tf_op jit(solution)/shard_map/pallas_call | solution.py:53
  17.7 2.6 shard_map.56
  20.3 1.1 bitcast_select_fusion.1
  21.4 0.7 pad_maximum_fusion
  22.1 2.3 collective-permute-start.1
  24.4 1.2 slice_select_fusion.1
  25.6 1.2 collective-permute-start.2
  27.5 6.3 %collective-permute-done.1 = f32[72,1024]{1,0:T(8,128)} collective-permute-done((f32[72,1024]{1,0:T(8,128)}, f32[72,1024]{1,0:T(8,128)}, u32[]{:S(2)}, u32[]{:S(2)}) %collective-permute-start.1) | collective-permute-done | bytes 294944 | tf_op jit(solution)/shard_map/ppermute | solution.py:227
  33.9 1.8 slice_select_fusion.5
  35.7 2.7 shard_map.57
  38.4 1.0 slice_select_fusion.6
  39.4 2.4 collective-permute-done.2.source_ref
  43.9 2.4 collective-permute-start.10
  46.3 1.3 collective-permute-start.5
  49.6 1.0 slice_bitcast_fusion.1
  50.6 8.6 %collective-permute-done.5 = f32[72,512]{1,0:T(8,128)S(1)} collective-permute-done((f32[72,512]{1,0:T(8,128)S(1)}, f32[72,512]{1,0:T(8,128)S(1)}, u32[]{:S(2)}, u32[]{:S(2)}) %collective-permute-start.5) | collective-permute-done | bytes 147488 | tf_op jit(solution)/shard_map/ppermute | solution.py:261
  59.5 0.8 slice_select_fusion.7
  60.9 1.0 fusion.2
  61.9 2.6 collective-permute-start.13
  64.5 1.0 collective-permute-start.12
  65.7 1.1 convert_reduce_fusion
  70.7 4.3 %shard_map.58.places_ref = s32[192,128]{1,0:T(8,128)S(1)} custom-call(s32[196]{0:T(256)} %concatenate.47.scalars, s32[2,96,128]{2,1,0:T(8,128)} %bitcast.56), custom_call_target="tpu_custom_call" | custom-call | tf_op jit(solution)/shard_map/pallas_call | solution.py:53
  75.0 7.0 %shard_map.59 = f32[8,64,1536]{2,1,0:T(8,128)S(1)} custom-call(s32[97]{0:T(128)} %pad_add_fusion.5.scalars, s32[192,128]{1,0:T(8,128)S(1)} %shard_map.58.places_ref, f32[64,12288]{1,0:T(8,128)} %bitcast.50, f32[64,12288]{1,0:T(8,128)} %bitcast.42), custom_call_target="tpu_custom_call" | custom-call | tf_op jit(solution)/shard_map/pallas_call | solution.py:110
  82.0 5.5 %shard_map.63 = (f32[8,16,1536]{2,1,0:T(8,128)}, f32[8,8,1536]{2,1,0:T(8,128)}, f32[8,8,1536]{2,1,0:T(8,128)}) custom-call(s32[97]{0:T(128)} %pad_add_fusion.4.scalars, s32[192,128]{1,0:T(8,128)S(1)} %shard_map.58.places_ref, f32[8,64,1536]{2,1,0:T(8,128)S(1)} %get-tuple-element.104.front_ref, f32[16,6656]{1,0:T(8,128)} %collective-permute-done.13.source_ref), custom_call_target="tpu_custom_call" | custom-call | tf_op jit(solution)/shard_map/pallas_call | solution.py:110
  89.0 5.6 %shard_map.62 = (f32[8,16,1536]{2,1,0:T(8,128)}, f32[8,8,1536]{2,1,0:T(8,128)}, f32[8,8,1536]{2,1,0:T(8,128)}) custom-call(s32[97]{0:T(128)} %pad_add_fusion.4.scalars, s32[192,128]{1,0:T(8,128)S(1)} %shard_map.58.places_ref, f32[8,64,1536]{2,1,0:T(8,128)S(1)} %get-tuple-element.104.front_ref, f32[16,6656]{1,0:T(8,128)} %collective-permute-done.2.source_ref), custom_call_target="tpu_custom_call" | custom-call | tf_op jit(solution)/shard_map/pallas_call | solution.py:110
  95.2 0.9 collective-permute-start.18
  96.1 5.5 %shard_map.60 = (f32[8,16,1536]{2,1,0:T(8,128)}, f32[8,8,1536]{2,1,0:T(8,128)}, f32[8,8,1536]{2,1,0:T(8,128)}) custom-call(s32[97]{0:T(128)} %pad_add_fusion.4.scalars, s32[192,128]{1,0:T(8,128)S(1)} %shard_map.58.places_ref, f32[8,64,1536]{2,1,0:T(8,128)S(1)} %get-tuple-element.104.front_ref, f32[16,6656]{1,0:T(8,128)} %collective-permute-done.12.source_ref), custom_call_target="tpu_custom_call" | custom-call | tf_op jit(solution)/shard_map/pallas_call | solution.py:110
  101.6 0.8 collective-permute-start.14
  102.4 5.6 %shard_map.61 = (f32[8,16,1536]{2,1,0:T(8,128)}, f32[8,8,1536]{2,1,0:T(8,128)}, f32[8,8,1536]{2,1,0:T(8,128)}) custom-call(s32[97]{0:T(128)} %pad_add_fusion.4.scalars, s32[192,128]{1,0:T(8,128)S(1)} %shard_map.58.places_ref, f32[8,64,1536]{2,1,0:T(8,128)S(1)} %get-tuple-element.104.front_ref, f32[16,6656]{1,0:T(8,128)} %copy-done.8), custom_call_target="tpu_custom_call" | custom-call | tf_op jit(solution)/shard_map/pallas_call | solution.py:110
  108.0 0.8 collective-permute-start.15
  108.8 1.3 collective-permute-start.16
  110.1 27.6 %collective-permute-done.16 = f32[8,8,1536]{2,1,0:T(8,128)S(1)} collective-permute-done((f32[8,8,1536]{2,1,0:T(8,128)}, f32[8,8,1536]{2,1,0:T(8,128)S(1)}, u32[]{:S(2)}, u32[]{:S(2)}) %collective-permute-start.16) | collective-permute-done | bytes 393248 | tf_op jit(solution)/shard_map/ppermute | solution.py:261
  137.9 22.1 %all_to_all.25 = f32[8,8,1536]{2,1,0:T(8,128)} all-to-all(f32[8,8,1536]{2,1,0:T(8,128)S(1)} %add_add_fusion), channel_id=1, replica_groups=mesh['subcube'=2,'row'=8,'col'=16] {'row'}, dimensions={0} | all-to-all | bytes 786432 | tf_op jit(solution)/shard_map/all_to_all | solution.py:300
  160.0 24.2 %all_to_all.26.refs_0_ = f32[8,16,1536]{2,1,0:T(8,128)} all-to-all(f32[8,16,1536]{2,1,0:T(8,128)S(1)} %copy-done.7), channel_id=1, replica_groups=mesh['subcube'=2,'row'=8,'col'=16] {'row'}, dimensions={0} | all-to-all | bytes 1572864 | tf_op jit(solution)/shard_map/all_to_all | solution.py:300
  184.2 3.5 %all-to-all-start.1 = ((f32[8,16,1536]{2,1,0:T(8,128)}), f32[8,16,1536]{2,1,0:T(8,128)S(1)}, u32[]{:S(2)}, u32[]{:S(2)}) async-start(f32[8,16,1536]{2,1,0:T(8,128)} %get-tuple-element.67), calls=%async_computation.1 | async-start | bytes 1572864 | tf_op jit(solution)/shard_map/all_to_all | solution.py:300
  187.8 19.6 %all-to-all-done.1.refs_1_ = f32[8,16,1536]{2,1,0:T(8,128)S(1)} async-done(((f32[8,16,1536]{2,1,0:T(8,128)}), f32[8,16,1536]{2,1,0:T(8,128)S(1)}, u32[]{:S(2)}, u32[]{:S(2)}) %all-to-all-start.1) | async-done | bytes 786464 | tf_op jit(solution)/shard_map/all_to_all | solution.py:300
  207.4 23.0 %all_to_all.27.refs_2_ = f32[8,16,1536]{2,1,0:T(8,128)} all-to-all(f32[8,16,1536]{2,1,0:T(8,128)S(1)} %copy-done.6), channel_id=1, replica_groups=mesh['subcube'=2,'row'=8,'col'=16] {'row'}, dimensions={0} | all-to-all | bytes 1572864 | tf_op jit(solution)/shard_map/all_to_all | solution.py:300
  230.4 3.5 %all-to-all-start.4 = ((f32[8,16,1536]{2,1,0:T(8,128)}), f32[8,16,1536]{2,1,0:T(8,128)S(1)}, u32[]{:S(2)}, u32[]{:S(2)}) async-start(f32[8,16,1536]{2,1,0:T(8,128)} %get-tuple-element.80), calls=%async_computation.4 | async-start | bytes 1572864 | tf_op jit(solution)/shard_map/all_to_all | solution.py:300
  234.8 1.3 slice.150
  237.3 8.9 %shard_map.64 = (f32[512,512]{1,0:T(8,128)}, f32[512,512]{1,0:T(8,128)}, f32[512,512]{1,0:T(8,128)}) custom-call(s32[2]{0:T(128)} %pad_add_fusion.6.flags, f32[8,200,1024]{2,1,0:T(8,128)} %bitcast.47), custom_call_target="tpu_custom_call" | custom-call | tf_op jit(solution)/shard_map/pallas_call | solution.py:164
  246.2 6.2 %all-to-all-done.4.refs_3_ = f32[8,16,1536]{2,1,0:T(8,128)S(1)} async-done(((f32[8,16,1536]{2,1,0:T(8,128)}), f32[8,16,1536]{2,1,0:T(8,128)S(1)}, u32[]{:S(2)}, u32[]{:S(2)}) %all-to-all-start.4) | async-done | bytes 786464 | tf_op jit(solution)/shard_map/all_to_all | solution.py:300
  252.4 0.9 copy-done.2
  253.3 10.9 %shard_map.65 = f32[1536,512]{1,0:T(8,128)} custom-call(s32[12]{0:T(128)} %reshape.126.flags, f32[8,16,1536]{2,1,0:T(8,128)} %all_to_all.26.refs_0_, f32[8,16,1536]{2,1,0:T(8,128)} %copy-done.1, f32[8,16,1536]{2,1,0:T(8,128)} %all_to_all.27.refs_2_, f32[8,16,1536]{2,1,0:T(8,128)} %copy-done.2, f32[8,2,64,1536]{3,2,1,0:T(8,128)} %bitcast.48, ...), custom_call_target="tpu_custom_call" | custom-call | tf_op jit(solution)/shard_map/pallas_call | solution.py:195
  (82 shorter events, 13.2 us)
Async XLA Ops:
  6.5 17.9 %copy-start = (f32[1,1,1,64,12288]{4,3,2,1,0:T(8,128)S(1)}, f32[1,1,1,64,12288]{4,3,2,1,0:T(8,128)}, u32[]{:S(2)}) copy-start(f32[1,1,1,64,12288]{4,3,2,1,0:T(8,128)} %param.10) | copy-start | bytes 9437188
  6.5 228.3 %all-gather.6.cloned.1.call-start = ((), (), s32[]{:S(2)}) async-start(), calls=%async_computation.6 | async-start | bytes 7372800 | tf_op jit(solution)/shard_map/all_gather | solution.py:273
  20.3 13.6 %copy-start.4 = (f32[1,64,1024]{2,1,0:T(8,128)S(1)}, f32[1,64,1024]{2,1,0:T(8,128)}, u32[]{:S(2)}) copy-start(f32[1,64,1024]{2,1,0:T(8,128)} %shard_map.56) | copy-start | bytes 786436
  22.1 11.7 %collective-permute-start.1 = (f32[72,1024]{1,0:T(8,128)}, f32[72,1024]{1,0:T(8,128)}, u32[]{:S(2)}, u32[]{:S(2)}) collective-permute-start(f32[72,1024]{1,0:T(8,128)} %pad_maximum_fusion), channel_id=1, source_target_pairs={{0,128},{128,0},{1,129},{129,1},{2,130},{130,2},{3,131},{131,3},{4... | collective-permute-start | bytes 884744 | tf_op jit(solution)/shard_map/ppermute | solution.py:227
  25.6 16.2 %collective-permute-start.2 = (f32[16,6656]{1,0:T(8,128)}, f32[16,6656]{1,0:T(8,128)}, u32[]{:S(2)}, u32[]{:S(2)}) collective-permute-start(f32[16,6656]{1,0:T(8,128)} %get-tuple-element.87), channel_id=1, source_target_pairs={{0,128},{128,0},{1,129},{129,1},{2,130},{130,2},{3,131},{131,3},{4... | collective-permute-start | bytes 1277960 | tf_op jit(solution)/shard_map/ppermute | solution.py:227
  35.7 29.9 %copy-start.5 = (s32[2,12288]{1,0:T(2,128)S(1)}, s32[2,12288]{1,0:T(2,128)}, u32[]{:S(2)}) copy-start(s32[2,12288]{1,0:T(2,128)} %param.11) | copy-start | bytes 294916
  38.4 22.5 %copy-start.3 = (f32[1,64,1024]{2,1,0:T(8,128)S(1)}, f32[1,64,1024]{2,1,0:T(8,128)}, u32[]{:S(2)}) copy-start(f32[1,64,1024]{2,1,0:T(8,128)} %shard_map.57) | copy-start | bytes 786436
  41.8 5.7 %collective-permute-start.8 = (f32[72,512]{1,0:T(8,128)S(1)}, f32[72,512]{1,0:T(8,128)S(1)}, u32[]{:S(2)}, u32[]{:S(2)}) collective-permute-start(f32[72,512]{1,0:T(8,128)S(1)} %pad_maximum_fusion.1), channel_id=1, source_target_pairs={{0,12},{1,13},{16,28},{17,29},{32,44},{33,45},{48,60},{49,61},{64,... | collective-permute-start | bytes 442376 | tf_op jit(solution)/shard_map/ppermute | solution.py:261
  42.5 5.7 %collective-permute-start.7 = (f32[72,512]{1,0:T(8,128)S(1)}, f32[72,512]{1,0:T(8,128)S(1)}, u32[]{:S(2)}, u32[]{:S(2)}) collective-permute-start(f32[72,512]{1,0:T(8,128)S(1)} %pad_maximum_fusion.1), channel_id=1, source_target_pairs={{0,10},{1,11},{16,26},{17,27},{32,42},{33,43},{48,58},{49,59},{64,... | collective-permute-start | bytes 442376 | tf_op jit(solution)/shard_map/ppermute | solution.py:261
  43.2 5.7 %collective-permute-start.6 = (f32[72,512]{1,0:T(8,128)S(1)}, f32[72,512]{1,0:T(8,128)S(1)}, u32[]{:S(2)}, u32[]{:S(2)}) collective-permute-start(f32[72,512]{1,0:T(8,128)S(1)} %pad_maximum_fusion.1), channel_id=1, source_target_pairs={{0,8},{1,9},{16,24},{17,25},{32,40},{33,41},{48,56},{49,57},{64,72... | collective-permute-start | bytes 442376 | tf_op jit(solution)/shard_map/ppermute | solution.py:261
  43.9 15.5 %collective-permute-start.10 = (f32[16,6656]{1,0:T(8,128)}, f32[16,6656]{1,0:T(8,128)S(1)}, u32[]{:S(2)}, u32[]{:S(2)}) collective-permute-start(f32[16,6656]{1,0:T(8,128)} %get-tuple-element.85), channel_id=1, source_target_pairs={{0,128},{128,0},{1,129},{129,1},{2,130},{130,2},{3,131},{131,3},{4... | collective-permute-start | bytes 1277960 | tf_op jit(solution)/shard_map/ppermute | solution.py:227
  46.3 13.0 %collective-permute-start.5 = (f32[72,512]{1,0:T(8,128)S(1)}, f32[72,512]{1,0:T(8,128)S(1)}, u32[]{:S(2)}, u32[]{:S(2)}) collective-permute-start(f32[72,512]{1,0:T(8,128)S(1)} %pad_maximum_fusion.1), channel_id=1, source_target_pairs={{0,6},{1,7},{16,22},{17,23},{32,38},{33,39},{48,54},{49,55},{64,70... | collective-permute-start | bytes 442376 | tf_op jit(solution)/shard_map/ppermute | solution.py:261
  47.6 11.7 %collective-permute-start.4 = (f32[72,512]{1,0:T(8,128)S(1)}, f32[72,512]{1,0:T(8,128)S(1)}, u32[]{:S(2)}, u32[]{:S(2)}) collective-permute-start(f32[72,512]{1,0:T(8,128)S(1)} %pad_maximum_fusion.1), channel_id=1, source_target_pairs={{0,4},{1,5},{16,20},{17,21},{32,36},{33,37},{48,52},{49,53},{64,68... | collective-permute-start | bytes 442376 | tf_op jit(solution)/shard_map/ppermute | solution.py:261
  48.2 11.0 %collective-permute-start.3 = (f32[72,512]{1,0:T(8,128)S(1)}, f32[72,512]{1,0:T(8,128)S(1)}, u32[]{:S(2)}, u32[]{:S(2)}) collective-permute-start(f32[72,512]{1,0:T(8,128)S(1)} %pad_maximum_fusion.1), channel_id=1, source_target_pairs={{0,2},{1,3},{16,18},{17,19},{32,34},{33,35},{48,50},{49,51},{64,66... | collective-permute-start | bytes 442376 | tf_op jit(solution)/shard_map/ppermute | solution.py:261
  48.9 10.3 %collective-permute-start.9 = (f32[72,512]{1,0:T(8,128)S(1)}, f32[72,512]{1,0:T(8,128)S(1)}, u32[]{:S(2)}, u32[]{:S(2)}) collective-permute-start(f32[72,512]{1,0:T(8,128)S(1)} %pad_maximum_fusion.1), channel_id=1, source_target_pairs={{0,14},{1,15},{16,30},{17,31},{32,46},{33,47},{48,62},{49,63},{64,... | collective-permute-start | bytes 442376 | tf_op jit(solution)/shard_map/ppermute | solution.py:261
  59.4 11.4 %copy-start.8 = (f32[16,6656]{1,0:T(8,128)}, f32[16,6656]{1,0:T(8,128)S(1)}, u32[]{:S(2)}) copy-start(f32[16,6656]{1,0:T(8,128)S(1)} %collective-permute-done.10.source_ref) | copy-start | bytes 1277956
  59.4 1.5 collective-permute-start.11
  61.9 190.5 %all-gather.4.cloned.1.call-start = ((), (), s32[]{:S(2)}) async-start(), calls=%async_computation.5 | async-start | bytes 6684672 | tf_op jit(solution)/shard_map/all_gather | solution.py:307
  61.9 20.1 %collective-permute-start.13 = (f32[16,6656]{1,0:T(8,128)}, f32[16,6656]{1,0:T(8,128)}, u32[]{:S(2)}, u32[]{:S(2)}) collective-permute-start(f32[16,6656]{1,0:T(8,128)} %get-tuple-element.84), channel_id=1, source_target_pairs={{0,128},{128,0},{1,129},{129,1},{2,130},{130,2},{3,131},{131,3},{4... | collective-permute-start | bytes 1277960 | tf_op jit(solution)/shard_map/ppermute | solution.py:227
  64.5 31.5 %collective-permute-start.12 = (f32[16,6656]{1,0:T(8,128)}, f32[16,6656]{1,0:T(8,128)}, u32[]{:S(2)}, u32[]{:S(2)}) collective-permute-start(f32[16,6656]{1,0:T(8,128)} %get-tuple-element.86), channel_id=1, source_target_pairs={{0,128},{128,0},{1,129},{129,1},{2,130},{130,2},{3,131},{131,3},{4... | collective-permute-start | bytes 1277960 | tf_op jit(solution)/shard_map/ppermute | solution.py:227
  87.6 20.4 %collective-permute-start.19 = (f32[8,8,1536]{2,1,0:T(8,128)}, f32[8,8,1536]{2,1,0:T(8,128)S(1)}, u32[]{:S(2)}, u32[]{:S(2)}) collective-permute-start(f32[8,8,1536]{2,1,0:T(8,128)} %get-tuple-element.77), channel_id=1, source_target_pairs={{0,12},{1,13},{16,28},{17,29},{32,44},{33,45},{48,60},{49,61},{64,... | collective-permute-start | bytes 1179656 | tf_op jit(solution)/shard_map/ppermute | solution.py:261
  88.3 20.5 %collective-permute-start.20 = (f32[8,8,1536]{2,1,0:T(8,128)}, f32[8,8,1536]{2,1,0:T(8,128)S(1)}, u32[]{:S(2)}, u32[]{:S(2)}) collective-permute-start(f32[8,8,1536]{2,1,0:T(8,128)} %get-tuple-element.78), channel_id=1, source_target_pairs={{0,14},{1,15},{16,30},{17,31},{32,46},{33,47},{48,62},{49,63},{64,... | collective-permute-start | bytes 1179656 | tf_op jit(solution)/shard_map/ppermute | solution.py:261
  94.5 15.6 %collective-permute-start.17 = (f32[8,8,1536]{2,1,0:T(8,128)}, f32[8,8,1536]{2,1,0:T(8,128)S(1)}, u32[]{:S(2)}, u32[]{:S(2)}) collective-permute-start(f32[8,8,1536]{2,1,0:T(8,128)} %get-tuple-element.75), channel_id=1, source_target_pairs={{0,8},{1,9},{16,24},{17,25},{32,40},{33,41},{48,56},{49,57},{64,72... | collective-permute-start | bytes 1179656 | tf_op jit(solution)/shard_map/ppermute | solution.py:261
  95.2 14.9 %collective-permute-start.18 = (f32[8,8,1536]{2,1,0:T(8,128)}, f32[8,8,1536]{2,1,0:T(8,128)S(1)}, u32[]{:S(2)}, u32[]{:S(2)}) collective-permute-start(f32[8,8,1536]{2,1,0:T(8,128)} %get-tuple-element.76), channel_id=1, source_target_pairs={{0,10},{1,11},{16,26},{17,27},{32,42},{33,43},{48,58},{49,59},{64,... | collective-permute-start | bytes 1179656 | tf_op jit(solution)/shard_map/ppermute | solution.py:261
  101.6 36.1 %copy-start.9 = (f32[8,8,1536]{2,1,0:T(8,128)S(1)}, f32[8,8,1536]{2,1,0:T(8,128)}, u32[]{:S(2)}) copy-start(f32[8,8,1536]{2,1,0:T(8,128)} %get-tuple-element.71) | copy-start | bytes 1179652
  101.6 8.5 %collective-permute-start.14 = (f32[8,8,1536]{2,1,0:T(8,128)}, f32[8,8,1536]{2,1,0:T(8,128)S(1)}, u32[]{:S(2)}, u32[]{:S(2)}) collective-permute-start(f32[8,8,1536]{2,1,0:T(8,128)} %get-tuple-element.72), channel_id=1, source_target_pairs={{0,2},{1,3},{16,18},{17,19},{32,34},{33,35},{48,50},{49,51},{64,66... | collective-permute-start | bytes 1179656 | tf_op jit(solution)/shard_map/ppermute | solution.py:261
  107.9 52.1 %copy-start.7 = (f32[8,16,1536]{2,1,0:T(8,128)S(1)}, f32[8,16,1536]{2,1,0:T(8,128)}, u32[]{:S(2)}) copy-start(f32[8,16,1536]{2,1,0:T(8,128)} %get-tuple-element.65) | copy-start | bytes 2359300
  108.0 2.2 collective-permute-start.15
  108.8 28.9 %collective-permute-start.16 = (f32[8,8,1536]{2,1,0:T(8,128)}, f32[8,8,1536]{2,1,0:T(8,128)S(1)}, u32[]{:S(2)}, u32[]{:S(2)}) collective-permute-start(f32[8,8,1536]{2,1,0:T(8,128)} %get-tuple-element.74), channel_id=1, source_target_pairs={{0,6},{1,7},{16,22},{17,23},{32,38},{33,39},{48,54},{49,55},{64,70... | collective-permute-start | bytes 1179656 | tf_op jit(solution)/shard_map/ppermute | solution.py:261
  137.7 69.7 %copy-start.6 = (f32[8,16,1536]{2,1,0:T(8,128)S(1)}, f32[8,16,1536]{2,1,0:T(8,128)}, u32[]{:S(2)}) copy-start(f32[8,16,1536]{2,1,0:T(8,128)} %get-tuple-element.79) | copy-start | bytes 2359300
  160.0 74.0 %copy-start.10 = (s32[3,1]{0,1:T(1,128)S(1)}, s32[3,1]{0,1:T(1,128)}, u32[]{:S(2)}) copy-start(s32[3,1]{0,1:T(1,128)} %param.13) | copy-start | bytes 40
  184.2 23.2 %all-to-all-start.1 = ((f32[8,16,1536]{2,1,0:T(8,128)}), f32[8,16,1536]{2,1,0:T(8,128)S(1)}, u32[]{:S(2)}, u32[]{:S(2)}) async-start(f32[8,16,1536]{2,1,0:T(8,128)} %get-tuple-element.67), calls=%async_computation.1 | async-start | bytes 1572864 | tf_op jit(solution)/shard_map/all_to_all | solution.py:300
  207.4 38.8 %copy-start.1 = (f32[8,16,1536]{2,1,0:T(8,128)}, f32[8,16,1536]{2,1,0:T(8,128)S(1)}, u32[]{:S(2)}) copy-start(f32[8,16,1536]{2,1,0:T(8,128)S(1)} %all-to-all-done.1.refs_1_) | copy-start | bytes 2359300
  230.4 21.9 %all-to-all-start.4 = ((f32[8,16,1536]{2,1,0:T(8,128)}), f32[8,16,1536]{2,1,0:T(8,128)S(1)}, u32[]{:S(2)}, u32[]{:S(2)}) async-start(f32[8,16,1536]{2,1,0:T(8,128)} %get-tuple-element.80), calls=%async_computation.4 | async-start | bytes 1572864 | tf_op jit(solution)/shard_map/all_to_all | solution.py:300
  252.4 0.9 copy-start.2
Sparse Core Ops, SparseCore 0:
  62.0 81.4 all-gather.5
  160.1 53.5 all-gather.3

commit v4 on v3

--- a/solution.py
+++ b/solution.py
@@ -71,41 +71,49 @@
     source_blocks = source_ref.shape[1] // LANES
     offset = scalars[scalars.shape[0] - 1]
     lane = lax.broadcasted_iota(jnp.int32, (8, LANES), 1)
-    for j in range(per_step):
-        block = step * per_step + j
-        start = scalars[block]
-        at = jnp.minimum(start // LANES, map_blocks - 1)
-        split = jnp.where(start // LANES < map_blocks, start & (LANES - 1), LANES)
-        at = at - offset
-        inside_low = (at >= 0) & (at < source_blocks)
-        inside_high = (at + 1 >= 0) & (at + 1 < source_blocks)
-        low_at = pl.multiple_of(jnp.clip(at, 0, source_blocks - 1) * LANES, LANES)
-        high_at = pl.multiple_of(jnp.clip(at + 1, 0, source_blocks - 1) * LANES, LANES)
-        place = jnp.broadcast_to(places_ref[pl.ds(first_place + block, 1), :], (8, LANES))
-        inner = place & (LANES - 1)
-        hit = ((place >= 0) & (place < LANES) & inside_low) | ((place >= LANES) & inside_high)
-        from_low = lane >= split
-        here = slice(j * LANES, (j + 1) * LANES)
-        for row in range(0, columns, 8):
-            rows = slice(row, row + 8)
-            merged = jnp.where(from_low, source_ref[rows, pl.ds(low_at, LANES)], source_ref[rows, pl.ds(high_at, LANES)])
-            gained = jnp.where(hit, jnp.take_along_axis(merged, inner, axis=1), 0.0)
-            value = front_ref[..., rows, here].reshape(8, LANES) + gained
-            out_ref[0, rows, here] = value
-            if piece_refs:
-                piece_refs[row // 8][0, :, here] = value
-
-
-def extend_add(front, source, places, first_place, starts, offset, map_blocks, steps, part=0, pieces=0):
-    columns = source.shape[0]
+    group = max(1, 256 // columns)
+    for group_start in range(0, per_step, group):
+        gained = {}
+        members = range(group_start, min(per_step, group_start + group))
+        for j in members:
+            block = step * per_step + j
+            start = scalars[block]
+            at = jnp.minimum(start // LANES, map_blocks - 1)
+            split = jnp.where(start // LANES < map_blocks, start & (LANES - 1), LANES)
+            at = at - offset
+            inside_low = (at >= 0) & (at < source_blocks)
+            inside_high = (at + 1 >= 0) & (at + 1 < source_blocks)
+            low_at = pl.multiple_of(jnp.clip(at, 0, source_blocks - 1) * LANES, LANES)
+            high_at = pl.multiple_of(jnp.clip(at + 1, 0, source_blocks - 1) * LANES, LANES)
+            place = jnp.broadcast_to(places_ref[pl.ds(first_place + block, 1), :], (8, LANES))
+            inner = place & (LANES - 1)
+            hit = ((place >= 0) & (place < LANES) & inside_low) | ((place >= LANES) & inside_high)
+            from_low = lane >= split
+            for row in range(0, columns, 8):
+                rows = slice(row, row + 8)
+                merged = jnp.where(
+                    from_low, source_ref[rows, pl.ds(low_at, LANES)], source_ref[rows, pl.ds(high_at, LANES)]
+                )
+                gained[j, row] = jnp.where(hit, jnp.take_along_axis(merged, inner, axis=1), 0.0)
+        for j in members:
+            here = slice(j * LANES, (j + 1) * LANES)
+            for row in range(0, columns, 8):
+                rows = slice(row, row + 8)
+                value = front_ref[..., rows, here].reshape(8, LANES) + gained[j, row]
+                out_ref[0, rows, here] = value
+                if piece_refs:
+                    piece_refs[row // 8][0, :, here] = value
+
+
+def extend_add(front, source, places, first_place, starts, offset, map_blocks, steps, width, columns=None, part=0, pieces=0):
+    columns = source.shape[0] if columns is None else columns
     if front.ndim == 2:
-        width = front.shape[1] // steps
-        front_spec = pl.BlockSpec((columns, width), lambda i, _: (0, i))
+        front_spec = pl.BlockSpec((columns, width), lambda i, _: (part, i))
     else:
-        width = front.shape[2]
-        front_spec = pl.BlockSpec((1, columns, width), lambda i, _: (i, part, 0))
+        front_spec = pl.BlockSpec((1, columns, width), lambda i, _: (i, 0, 0))
+    source_width = min(source.shape[1], map_blocks * LANES if steps > 1 else width)
     scalars = jnp.concatenate([starts, offset.reshape(1)]).astype(jnp.int32)
-    whole = lambda shape: pl.BlockSpec(shape, lambda i, _: (0,) * len(shape), pipeline_mode=pl.Buffered(1))
+    whole = lambda shape, row=0: pl.BlockSpec(shape, lambda i, _: (row, 0), pipeline_mode=pl.Buffered(1))
     sizes = [columns] + [8] * pieces
     outs = pl.pallas_call(
         functools.partial(extend_kernel, first_place, map_blocks),
@@ -113,7 +121,7 @@
         grid_spec=pltpu.PrefetchScalarGridSpec(
             num_scalar_prefetch=1,
             grid=(steps,),
-            in_specs=[whole(places.shape), front_spec, whole(source.shape)],
+            in_specs=[whole(places.shape), front_spec, whole((columns, source_width), part)],
             out_specs=[pl.BlockSpec((1, size, width), lambda i, _: (i, 0, 0)) for size in sizes],
         ),
         compiler_params=pltpu.CompilerParams(vmem_limit_bytes=VMEM_BYTES),
@@ -137,13 +145,13 @@
 CROSS = ((1,), (1,))
 
 
-def factor_kernel(flags, gathered_ref, first_ref, second_ref, fixed_ref):
+def factor_kernel(order, flags, gathered_ref, inverse_ref, first_ref, second_ref, fixed_ref):
     place, kept = flags[0], flags[1]
-    thin = (gathered_ref.shape[1] - 8) // 3
-    by_chip = lambda x: jnp.concatenate([x[:, 8 * q : 8 * q + 8].reshape(-1, x.shape[2]) for q in range(thin // 8)])
+    thin = inverse_ref.shape[1]
+    by_chip = lambda x: jnp.concatenate([x[:, 8 * q : 8 * q + 8].reshape(-1, x.shape[2]) for q in order])
     strip = gathered_ref[:, :thin].reshape(PANEL, 2 * PANEL)
     corner = by_chip(gathered_ref[:, thin : 2 * thin])
-    inverse = by_chip(gathered_ref[:, 2 * thin : 3 * thin])
+    inverse = by_chip(inverse_ref[...])
     inverse0, inverse1 = inverse[:, :PANEL], inverse[:, PANEL:]
     halves0, halves1 = halves(inverse0), halves(inverse1)
     corner10, corner01 = halves(corner[:, :PANEL]), halves(corner[:, PANEL:])
@@ -159,19 +167,19 @@
     fixed_ref[...] = fixed
 
 
-def factor(flags, gathered):
+def factor(order, flags, gathered, inverse):
     square = jax.ShapeDtypeStruct((PANEL, PANEL), jnp.float32)
     return pl.pallas_call(
-        factor_kernel,
+        functools.partial(factor_kernel, order),
         out_shape=(square, square, square),
         grid_spec=pltpu.PrefetchScalarGridSpec(
             num_scalar_prefetch=1,
             grid=(1,),
-            in_specs=[pl.BlockSpec(gathered.shape, lambda i, _: (0, 0, 0))],
+            in_specs=[pl.BlockSpec(x.shape, lambda i, _: (0, 0, 0)) for x in (gathered, inverse)],
             out_specs=[pl.BlockSpec((PANEL, PANEL), lambda i, _: (0, 0))] * 3,
         ),
         compiler_params=pltpu.CompilerParams(vmem_limit_bytes=VMEM_BYTES),
-    )(flags, gathered)
+    )(flags, gathered, inverse)
 
 
 def update_kernel(flags, *refs):
@@ -226,14 +234,13 @@
     zero = jnp.zeros((), jnp.int32)
     exchange = lambda x: lax.ppermute(x, "subcube", [(0, 1), (1, 0)])
 
+    inverse = lax.all_gather(jnp.concatenate([pivot_inverses[k] for k in range(PANELS)], axis=1), "row", axis=0)
+
     window = -(-(child_rows * 13 // 24) // LANES) * LANES
     rest = child_rows - window
-    parts = chunks // 2
-    share = thin // parts
-    received = []
-    for p in range(parts):
-        late, early = own[p * share : (p + 1) * share, rest:], own[p * share : (p + 1) * share, :window]
-        received.append(exchange(jnp.where(side == 0, late, early)))
+    tail = thin // 4
+    parts = [(thin - tail, thin), (0, thin - tail)]
+    received = [exchange(jnp.where(side == 0, own[a:b, rest:], own[a:b, :window])) for a, b in parts]
 
     map_blocks = child_rows // LANES
     blocks = half_rows // LANES
@@ -244,34 +251,32 @@
     strip_starts = count(row_maps, edges[:strip_blocks])
     strip_places = search(maps, [zero, zero + 1], [zero, zero], [strip_starts[0], strip_starts[1]])
     strip_add = lambda base, child, t: extend_add(
-        base, child, strip_places, t * strip_blocks, strip_starts[t], zero, map_blocks, 1
+        base, child, strip_places, t * strip_blocks, strip_starts[t], zero, map_blocks, 1, pivot_rows
     )[0]
     mask_rows = jnp.zeros((8, pivot_rows), jnp.float32)
     mask_rows = mask_rows.at[0, : tile_mask.shape[0]].set(tile_mask.astype(jnp.float32)[:, 0])
     prefix = own[:, :pivot_rows]
-    base = strip_add(front[:, :pivot_rows], prefix, 0)
+    base = strip_add(front, own, 0)
     got = exchange(jnp.concatenate([jnp.where(side == 0, base, prefix), mask_rows]))
+    got, received[0] = lax.optimization_barrier((got, received[0]))
     strip = strip_add(jnp.where(side == 0, base, got[:thin]), jnp.where(side == 0, got[:thin], prefix), 1)
     first_masks = jnp.where(side == 0, mask_rows, got[thin:])
 
-    def to_chips(pieces):
-        mine = jnp.where(place // PANELS == 0, pieces[0], 0.0)
-        for chunk in range(1, chunks):
-            pairs = [(k, PANELS * chunk + k) for k in range(PANELS)]
-            mine = mine + lax.ppermute(pieces[chunk], "col", pairs)
-        return mine
-
+    cols = lax.axis_size("col")
     corner = jnp.where(place == 0, strip[:, PANEL:], strip[:, :PANEL])
-    corner, received[2] = lax.optimization_barrier((corner, received[2]))
-    corner = to_chips([jnp.concatenate([corner, mask_rows[:, :PANEL]])] * chunks)
-    corner, received[1] = lax.optimization_barrier((corner, received[1]))
-    other = lax.ppermute(corner, "col", [(c, c ^ 1) for c in range(lax.axis_size("col"))])
+    corner = jnp.where(place < PANELS, jnp.concatenate([corner, mask_rows[:, :PANEL]]), 0.0)
+    reach = cols // 2
+    while reach >= PANELS:
+        pairs = [(c, c + reach) for c in range(cols) if c % (2 * reach) < PANELS]
+        corner = corner + lax.ppermute(corner, "col", pairs)
+        reach //= 2
+    corner, received[1], inverse = lax.optimization_barrier((corner, received[1], inverse))
+    other = lax.ppermute(corner, "col", [(c, c ^ 1) for c in range(cols)])
     core0 = place % PANELS == 0
     corner = jnp.concatenate([jnp.where(core0, corner, other), jnp.where(core0, other, corner)], axis=1)
     cross_mask = corner[thin, PANEL : PANEL + tile_mask.shape[0]] > 0.5
-    inverse = jnp.concatenate([pivot_inverses[k] for k in range(PANELS)], axis=1)
-    gathered = lax.all_gather(jnp.concatenate([strip, corner[:thin], inverse, first_masks]), "row", axis=0)
-    kept = gathered[0, 3 * thin, 1] > 0.5
+    gathered = lax.all_gather(jnp.concatenate([strip, corner[:thin], first_masks]), "row", axis=0)
+    kept = gathered[0, 2 * thin, 1] > 0.5
 
     first_row = (side * half_rows).astype(jnp.int32)
     own_map = lax.dynamic_index_in_dim(row_maps, side, 0, keepdims=False)
@@ -287,30 +292,43 @@
     spill = (child_rows - lower[0] > window) | (lower[1] > window)
     window_at = jnp.where(side == 0, 0, rest // LANES).astype(jnp.int32)
     rest_at = jnp.where(side == 0, window // LANES, 0).astype(jnp.int32)
-    add = functools.partial(extend_add, places=places, map_blocks=map_blocks, steps=grid_rows)
-    base = add(front, own, first_place=0, starts=starts[0], offset=zero)
+    add = functools.partial(extend_add, places=places, map_blocks=map_blocks, steps=grid_rows, width=row_count)
+    add_own = functools.partial(add, first_place=0, starts=starts[0], offset=zero)
     add_other = functools.partial(add, first_place=blocks, starts=starts[1])
-
-    def add_rest(base):
+    bases = [add_own(front, own, columns=b - a, part=a // (b - a)) for a, b in parts]
+
+    def add_rest(bases):
         more = exchange(jnp.where(side == 0, own[:, :rest], own[:, window:]))
-        return add_other(base, more, offset=rest_at)
-
-    base = lax.cond(spill, add_rest, lambda x: x, base)
+        return tuple(
+            add_other(base, more, offset=rest_at, columns=b - a, part=a // (b - a)) for base, (a, b) in zip(bases, parts)
+        )
+
+    bases = lax.cond(spill, add_rest, lambda x: x, tuple(bases))
 
     across = lambda x: lax.all_to_all(x, "row", split_axis=0, concat_axis=0, tiled=True)
-    wholes, pieces = [], []
-    for p in range(parts):
-        whole, *halves_of = add_other(base, received[p], offset=window_at, part=p, pieces=2)
+    wholes, pieces = [], {}
+    for base, part, (a, b) in zip(bases, received, parts):
+        whole, *chunk_list = add_other(base, part, offset=window_at, pieces=(b - a) // 8)
         wholes.append(whole)
-        pieces += halves_of
-    mine = across(to_chips(pieces))
+        pieces.update({a // 8 + i: chunk for i, chunk in enumerate(chunk_list)})
+    order = list(range(chunks))
+    middle = chunks // 2
+    order[middle : middle + 2], order[-2:] = order[-2:], order[middle : middle + 2]
+    mine = jnp.where(place // PANELS == 0, pieces[order[0]], 0.0)
+    for chip in range(1, chunks):
+        pairs = [(k, PANELS * chip + k) for k in range(PANELS)]
+        mine = mine + lax.ppermute(pieces[order[chip]], "col", pairs)
+    moved = [across(wholes[0])]
+    mine, moved[0] = lax.optimization_barrier((mine, moved[0]))
+    mine = across(mine)
     panels = lax.all_gather(mine.reshape(thin, row_count), "col", axis=0, tiled=True)
     panels = panels.reshape(chunks, PANELS, thin, row_count)
-    late = parts // 2
-    *last, mine = lax.optimization_barrier((*wholes[late:], mine))
-    moved = [across(x) for x in wholes[:late]] + [across(x) for x in last]
-
-    first, second, fixed = factor(jnp.stack([place, kept.astype(place.dtype)]).astype(jnp.int32), gathered)
+    last, mine = lax.optimization_barrier((wholes[1], mine))
+    moved.append(across(last))
+
+    first, second, fixed = factor(
+        order, jnp.stack([place, kept.astype(place.dtype)]).astype(jnp.int32), gathered, inverse
+    )
 
     tiles = row_count // PANEL
     tile_ids = (side * grid_rows + row_place) * tiles + jnp.arange(tiles, dtype=jnp.int32)
@@ -321,7 +339,7 @@
     use_fixed = jnp.where(is0, False, cross_mask & (tile_ids >= jnp.where(is1, 1, 2)))
     use_second = jnp.where(is0, False, jnp.where(is1, tile_ids >= 1, own_mask & (tile_ids >= 2)))
     flags = jnp.stack([keep, use_first, use_fixed, use_second], axis=1).astype(jnp.int32).reshape(-1)
-    return update(flags, moved, panels, first, second, fixed)
+    return update(flags, moved[::-1], panels, first, second, fixed)
 
 
 def solution(mesh):

time: 273 us -> 254 us (0.930)
  blocking collectives: 69.3 us -> 20.3 us
  waiting for transfers between devices: 71.5 us -> 100 us
  other arithmetic: 14.6 us -> 20 us
    all_to_all x3 -> x1, blocking collectives: 69.3 us -> 20.3 us  [local(): lax.all_to_all(x, 'row', split_axis=0, concat_axis=0, tiled=True)]
    all_to_all x2, waiting for transfers between devices: 25.8 us -> 41 us  [local(): lax.all_to_all(x, 'row', split_axis=0, concat_axis=0, tiled=True)]
    ppermute x15 -> x11, waiting for transfers between devices: 36.8 us -> 46.8 us  [the longest x7 25.3 us: local(): mine = mine + lax.ppermute(pieces[order[chip]], 'col', pairs)]
    all_to_all x2, starting transfers between devices: 7.09 us -> 12.3 us  [local(): lax.all_to_all(x, 'row', split_axis=0, concat_axis=0, tiled=True)]
    ppermute x5 -> x3, starting transfers between devices: 9.53 us -> 5.83 us  [local(): exchange = lambda x: lax.ppermute(x, 'subcube', [(0, 1), (1, 0)])]
    ppermute x5 -> x3, waiting for transfers between devices: 8.79 us -> 12.4 us  [local(): exchange = lambda x: lax.ppermute(x, 'subcube', [(0, 1), (1, 0)])]
    add x2 -> x4, other arithmetic: 0.31 us -> 3.7 us  [the longest x3 2.37 us: local(): corner = corner + lax.ppermute(corner, 'col', pairs)]
    slice x3 -> x1, local copies, waits for them, and re-layouts: 4.59 us -> 1.25 us  [local(): kept = gathered[0, 2 * thin, 1] > 0.5]
  transfers between devices with their start and end apart: 24 -> 19, of which waited for: 7 -> 6; matrix products, arithmetic and copies ran while one was open for 5% -> 9% of each run, Pallas kernels for 17% -> 19%
where the time goes in v4:
time: 254 us; the launch traced here: 252 us
  waiting for transfers between devices  100 us (39%)
  Pallas kernels  59.8 us (24%)
  starting transfers between devices  27.7 us (11%)
  blocking collectives  20.3 us (8%)
  other arithmetic  20 us (8%)
  between operations  15.4 us (6%)
  local copies, waits for them, and re-layouts  8.66 us (3%)
    all_to_all x2, waiting for transfers between devices, local(): lax.all_to_all(x, 'row', split_axis=0, concat_axis=0, tiled=True)  41 us
    pallas_call x6, Pallas kernels, extend_add(): pl.pallas_call(functools.partial(extend_kernel, first_place, map_blocks),...  32.7 us
    ppermute x7, waiting for transfers between devices, local(): mine = mine + lax.ppermute(pieces[order[chip]], 'col', pairs)  25.3 us
    ppermute x3, waiting for transfers between devices, local(): corner = corner + lax.ppermute(corner, 'col', pairs)  20.6 us
    all_to_all x1, blocking collectives, local(): lax.all_to_all(x, 'row', split_axis=0, concat_axis=0, tiled=True)  20.3 us
    ppermute x3, waiting for transfers between devices, local(): exchange = lambda x: lax.ppermute(x, 'subcube', [(0, 1), (1, 0)])  12.4 us
    all_to_all x2, starting transfers between devices, local(): lax.all_to_all(x, 'row', split_axis=0, concat_axis=0, tiled=True)  12.3 us
    pallas_call x1, Pallas kernels, update(): pl.pallas_call(update_kernel, out_shape=jax.ShapeDtypeStruct((rows, PANEL...  10.9 us
  transfers between devices with their start and end apart: 19, of which 6 were waited for; matrix products, arithmetic and copies ran while one was open for 9% of the time, Pallas kernels for 19%

profile of v4, /device:TPU:10, one launch (start us, length us, event | category | flops | bytes accessed | tf_op | source)
XLA Modules:
  0.0 252.2 jit_solution(16999213370089966030)
XLA Ops:
  6.5 1.0 slice_bitcast_fusion.1
  7.5 0.7 pad_maximum_fusion.1
  9.0 1.2 convert_reduce_fusion.1
  10.2 1.5 copy.10
  13.0 2.9 %shard_map.55.places_ref = s32[16,128]{1,0:T(8,128)} custom-call(s32[20]{0:T(128)} %concatenate.42.scalars, s32[2,96,128]{2,1,0:T(8,128)} %bitcast.60), custom_call_target="tpu_custom_call" | custom-call | tf_op jit(solution)/shard_map/pallas_call | solution.py:53
  15.8 2.9 %shard_map.56 = f32[1,64,1024]{2,1,0:T(8,128)} custom-call(s32[9]{0:T(128)} %pad_add_fusion.2.scalars, s32[16,128]{1,0:T(8,128)} %shard_map.55.places_ref, f32[64,12288]{1,0:T(8,128)} %bitcast.49, f32[64,12288]{1,0:T(8,128)} %bitcast.41), custom_call_target="tpu_custom_call" | custom-call | tf_op jit(solution)/shard_map/pallas_call | solution.py:118
  18.7 1.0 bitcast_select_fusion.1
  19.7 0.7 pad_maximum_fusion
  20.4 2.3 collective-permute-start.1
  22.7 0.8 slice_select_fusion.2
  23.5 1.2 collective-permute-start.2
  24.8 1.2 slice_select_fusion.1
  26.0 2.3 collective-permute-start.6
  28.9 3.3 %collective-permute-done.1 = f32[72,1024]{1,0:T(8,128)} collective-permute-done((f32[72,1024]{1,0:T(8,128)}, f32[72,1024]{1,0:T(8,128)}, u32[]{:S(2)}, u32[]{:S(2)}) %collective-permute-start.1) | collective-permute-done | bytes 294944 | tf_op jit(solution)/shard_map/ppermute | solution.py:235
  32.2 9.1 %collective-permute-done.2.source_ref = f32[16,6656]{1,0:T(8,128)} collective-permute-done((f32[16,6656]{1,0:T(8,128)}, f32[16,6656]{1,0:T(8,128)}, u32[]{:S(2)}, u32[]{:S(2)}) %collective-permute-start.2) | collective-permute-done | bytes 426016 | tf_op jit(solution)/shard_map/ppermute | solution.py:235
  41.3 1.8 slice_select_fusion.3
  43.1 2.6 %shard_map.57 = f32[1,64,1024]{2,1,0:T(8,128)} custom-call(s32[9]{0:T(128)} %pad_add_fusion.3.scalars, s32[16,128]{1,0:T(8,128)} %shard_map.55.places_ref, f32[64,1024]{1,0:T(8,128)} %get-tuple-element.94.front_ref, f32[64,1024]{1,0:T(8,128)} %get-tuple-element.93.source_ref), custom_call_target="tpu_custom_call" | custom-call | tf_op jit(solution)/shard_map/pallas_call | solution.py:118
  45.7 1.0 slice_select_fusion.4
  48.9 1.3 collective-permute-start.5
  50.2 20.6 %collective-permute-done.5 = f32[72,512]{1,0:T(8,128)} collective-permute-done((f32[72,512]{1,0:T(8,128)}, f32[72,512]{1,0:T(8,128)}, u32[]{:S(2)}, u32[]{:S(2)}) %collective-permute-start.5) | collective-permute-done | bytes 147488 | tf_op jit(solution)/shard_map/ppermute | solution.py:271
  70.8 1.7 add.91
  72.5 0.8 slice_select_fusion.5
  73.2 0.8 collective-permute-done.7
  74.1 0.9 broadcast_select_fusion
  75.7 0.8 fusion.1
  76.7 1.1 convert_reduce_fusion
  78.5 4.3 %shard_map.58.places_ref = s32[192,128]{1,0:T(8,128)S(1)} custom-call(s32[196]{0:T(256)} %concatenate.48.scalars, s32[2,96,128]{2,1,0:T(8,128)} %bitcast.61), custom_call_target="tpu_custom_call" | custom-call | tf_op jit(solution)/shard_map/pallas_call | solution.py:53
  83.4 6.5 %shard_map.59 = f32[8,16,1536]{2,1,0:T(8,128)} custom-call(s32[97]{0:T(128)} %get-tuple-element.108.scalars, s32[192,128]{1,0:T(8,128)S(1)} %shard_map.58.places_ref, f32[64,12288]{1,0:T(8,128)} %bitcast.50, f32[64,12288]{1,0:T(8,128)S(1)} %bitcast.46), custom_call_target="tpu_custom_call" | custom-call | tf_op jit(solution)/shard_map/pallas_call | solution.py:118
  89.9 7.2 %shard_map.60 = f32[8,48,1536]{2,1,0:T(8,128)} custom-call(s32[97]{0:T(128)} %get-tuple-element.108.scalars, s32[192,128]{1,0:T(8,128)S(1)} %shard_map.58.places_ref, f32[64,12288]{1,0:T(8,128)} %bitcast.51, f32[64,12288]{1,0:T(8,128)S(1)} %bitcast.47), custom_call_target="tpu_custom_call" | custom-call | tf_op jit(solution)/shard_map/pallas_call | solution.py:118
  99.3 7.0 %shard_map.62 = (f32[8,16,1536]{2,1,0:T(8,128)}, f32[8,8,1536]{2,1,0:T(8,128)}, f32[8,8,1536]{2,1,0:T(8,128)}) custom-call(s32[97]{0:T(128)} %get-tuple-element.107.scalars, s32[192,128]{1,0:T(8,128)S(1)} %shard_map.58.places_ref, f32[8,16,1536]{2,1,0:T(8,128)} %get-tuple-element.77.front_ref, f32[16,6656]{1,0:T(8,128)} %collective-permute-done.2.source_ref), custom_call_target="tpu_custom_call" | custom-call | tf_op jit(solution)/shard_map/pallas_call | solution.py:118
  106.4 8.5 %all-to-all-start = ((f32[8,16,1536]{2,1,0:T(8,128)}), f32[8,16,1536]{2,1,0:T(8,128)S(1)}, u32[]{:S(2)}, u32[]{:S(2)}) async-start(f32[8,16,1536]{2,1,0:T(8,128)} %get-tuple-element.83), calls=%async_computation | async-start | bytes 1572864 | tf_op jit(solution)/shard_map/all_to_all | solution.py:308
  114.9 1.4 collective-permute-start.11
  116.3 1.4 collective-permute-start.12
  117.7 6.5 %shard_map.61 = (f32[8,48,1536]{2,1,0:T(8,128)}, f32[8,8,1536]{2,1,0:T(8,128)}, f32[8,8,1536]{2,1,0:T(8,128)}, f32[8,8,1536]{2,1,0:T(8,128)}, f32[8,8,1536]{2,1,...) custom-call(s32[97]{0:T(128)} %get-tuple-element.107.scalars, s32[192,128]{1,0:T(8,128)S(1)} %shard_map.58.places_ref, ...), custom_call_target="tpu_custom_call" | custom-call | tf_op jit(solution)/shard_map/pallas_call | solution.py:118
  124.2 0.7 collective-permute-start.8
  124.9 0.7 collective-permute-start.9
  125.6 1.3 collective-permute-start.10
  127.6 0.7 collective-permute-start.14
  128.3 25.3 %collective-permute-done.10 = f32[8,8,1536]{2,1,0:T(8,128)S(1)} collective-permute-done((f32[8,8,1536]{2,1,0:T(8,128)}, f32[8,8,1536]{2,1,0:T(8,128)S(1)}, u32[]{:S(2)}, u32[]{:S(2)}) %collective-permute-start.10) | collective-permute-done | bytes 393248 | tf_op jit(solution)/shard_map/ppermute | solution.py:320
  153.7 1.3 add_add_fusion
  155.0 20.3 %all_to_all.15 = f32[8,8,1536]{2,1,0:T(8,128)} all-to-all(f32[8,8,1536]{2,1,0:T(8,128)S(1)} %add_add_fusion), channel_id=1, replica_groups=mesh['subcube'=2,'row'=8,'col'=16] {'row'}, dimensions={0} | all-to-all | bytes 786432 | tf_op jit(solution)/shard_map/all_to_all | solution.py:308
  175.4 3.8 %all-to-all-start.2 = ((f32[8,48,1536]{2,1,0:T(8,128)}), f32[8,48,1536]{2,1,0:T(8,128)S(1)}, u32[]{:S(2)}, u32[]{:S(2)}) async-start(f32[8,48,1536]{2,1,0:T(8,128)} %get-tuple-element.85), calls=%async_computation.2 | async-start | bytes 4718592 | tf_op jit(solution)/shard_map/all_to_all | solution.py:308
  179.2 0.7 fusion.5
  180.7 1.3 slice.123
  183.1 9.1 %shard_map.63 = (f32[512,512]{1,0:T(8,128)}, f32[512,512]{1,0:T(8,128)}, f32[512,512]{1,0:T(8,128)}) custom-call(s32[2]{0:T(128)} %pad_add_fusion.6.flags, f32[8,136,1024]{2,1,0:T(8,128)} %bitcast.54, f32[8,64,1024]{2,1,0:T(8,128)} %bitcast.57), custom_call_target="tpu_custom_call" | custom-call | tf_op jit(solution)/shard_map/pallas_call | solution.py:172
  192.3 41.0 %all-to-all-done.2.refs_0_ = f32[8,48,1536]{2,1,0:T(8,128)S(1)} async-done(((f32[8,48,1536]{2,1,0:T(8,128)}), f32[8,48,1536]{2,1,0:T(8,128)S(1)}, u32[]{:S(2)}, u32[]{:S(2)}) %all-to-all-start.2) | async-done | bytes 2359328 | tf_op jit(solution)/shard_map/all_to_all | solution.py:308
  233.3 1.5 copy-done.3
  234.8 10.9 %shard_map.64 = f32[1536,512]{1,0:T(8,128)} custom-call(s32[12]{0:T(128)} %reshape.125.flags, f32[8,48,1536]{2,1,0:T(8,128)} %copy-done.3, f32[8,16,1536]{2,1,0:T(8,128)} %copy-done.6, f32[8,2,64,1536]{3,2,1,0:T(8,128)} %bitcast.52, f32[512,512]{1,0:T(8,128)} %get-tuple-element.88.refs_3_, f32[512,512]{1,0:T(8,128)} %get-tuple-element.89.refs_4_, ...), custom_call_target="tpu_custom_call" | custom-call | tf_op jit(solution)/shard_map/pallas_call | solution.py:203
  (67 shorter events, 9.8 us)
Async XLA Ops:
  6.5 65.9 %all-gather.8.cloned.1.call-start = ((), (), s32[]{:S(2)}) async-start(), calls=%async_computation.4 | async-start | bytes 2359296 | tf_op jit(solution)/shard_map/all_gather | solution.py:237
  8.3 172.4 %all-gather.10.cloned.1.call-start = ((), (), s32[]{:S(2)}) async-start(), calls=%async_computation.5 | async-start | bytes 5013504 | tf_op jit(solution)/shard_map/all_gather | solution.py:278
  15.8 2.9 %copy-start = (f32[1,1,1,64,12288]{4,3,2,1,0:T(8,128)S(1)}, f32[1,1,1,64,12288]{4,3,2,1,0:T(8,128)}, u32[]{:S(2)}) copy-start(f32[1,1,1,64,12288]{4,3,2,1,0:T(8,128)} %param.10) | copy-start | bytes 9437188
  20.4 20.8 %copy-start.8 = (f32[1,64,1024]{2,1,0:T(8,128)S(1)}, f32[1,64,1024]{2,1,0:T(8,128)}, u32[]{:S(2)}) copy-start(f32[1,64,1024]{2,1,0:T(8,128)} %shard_map.56) | copy-start | bytes 786436
  20.4 11.7 %collective-permute-start.1 = (f32[72,1024]{1,0:T(8,128)}, f32[72,1024]{1,0:T(8,128)}, u32[]{:S(2)}, u32[]{:S(2)}) collective-permute-start(f32[72,1024]{1,0:T(8,128)} %pad_maximum_fusion), channel_id=1, source_target_pairs={{0,128},{128,0},{1,129},{129,1},{2,130},{130,2},{3,131},{131,3},{4... | collective-permute-start | bytes 884744 | tf_op jit(solution)/shard_map/ppermute | solution.py:235
  23.5 17.7 %collective-permute-start.2 = (f32[16,6656]{1,0:T(8,128)}, f32[16,6656]{1,0:T(8,128)}, u32[]{:S(2)}, u32[]{:S(2)}) collective-permute-start(f32[16,6656]{1,0:T(8,128)} %slice_select_fusion.2), channel_id=1, source_target_pairs={{0,128},{128,0},{1,129},{129,1},{2,130},{130,2},{3,131},{131,3},{4... | collective-permute-start | bytes 1277960 | tf_op jit(solution)/shard_map/ppermute | solution.py:235
  26.0 46.5 %collective-permute-start.6 = (f32[48,6656]{1,0:T(8,128)}, f32[48,6656]{1,0:T(8,128)}, u32[]{:S(2)}, u32[]{:S(2)}) collective-permute-start(f32[48,6656]{1,0:T(8,128)} %slice_select_fusion.1), channel_id=1, source_target_pairs={{0,128},{128,0},{1,129},{129,1},{2,130},{130,2},{3,131},{131,3},{4... | collective-permute-start | bytes 3833864 | tf_op jit(solution)/shard_map/ppermute | solution.py:235
  45.7 30.0 %copy-start.7 = (f32[1,64,1024]{2,1,0:T(8,128)S(1)}, f32[1,64,1024]{2,1,0:T(8,128)}, u32[]{:S(2)}) copy-start(f32[1,64,1024]{2,1,0:T(8,128)} %shard_map.57) | copy-start | bytes 786436
  45.7 30.8 %copy-start.9 = (s32[2,12288]{1,0:T(2,128)S(1)}, s32[2,12288]{1,0:T(2,128)}, u32[]{:S(2)}) copy-start(s32[2,12288]{1,0:T(2,128)} %param.11) | copy-start | bytes 294916
  46.8 0.7 collective-permute-start.3
  47.5 0.7 collective-permute-start.4
  48.9 21.9 %collective-permute-start.5 = (f32[72,512]{1,0:T(8,128)}, f32[72,512]{1,0:T(8,128)}, u32[]{:S(2)}, u32[]{:S(2)}) collective-permute-start(f32[72,512]{1,0:T(8,128)} %add.90), channel_id=1, source_target_pairs={{0,2},{1,3},{4,6},{5,7},{8,10},{9,11},{12,14},{13,15},{16,18},{17,... | collective-permute-start | bytes 442376 | tf_op jit(solution)/shard_map/ppermute | solution.py:271
  72.5 1.6 collective-permute-start.7
  75.0 0.7 copy-start.10
  99.3 18.4 %copy-start.2 = (f32[8,48,1536]{2,1,0:T(8,128)S(1)}, f32[8,48,1536]{2,1,0:T(8,128)}, u32[]{:S(2)}) copy-start(f32[8,48,1536]{2,1,0:T(8,128)} %get-tuple-element.70.front_ref) | copy-start | bytes 7077892
  106.4 48.6 %all-to-all-start = ((f32[8,16,1536]{2,1,0:T(8,128)}), f32[8,16,1536]{2,1,0:T(8,128)S(1)}, u32[]{:S(2)}, u32[]{:S(2)}) async-start(f32[8,16,1536]{2,1,0:T(8,128)} %get-tuple-element.83), calls=%async_computation | async-start | bytes 1572864 | tf_op jit(solution)/shard_map/all_to_all | solution.py:308
  114.9 118.4 %all-gather.6.cloned.1.call-start = ((), (), s32[]{:S(2)}) async-start(), calls=%async_computation.3 | async-start | bytes 6684672 | tf_op jit(solution)/shard_map/all_gather | solution.py:324
  114.9 12.0 %collective-permute-start.11 = (f32[8,8,1536]{2,1,0:T(8,128)}, f32[8,8,1536]{2,1,0:T(8,128)}, u32[]{:S(2)}, u32[]{:S(2)}) collective-permute-start(f32[8,8,1536]{2,1,0:T(8,128)} %get-tuple-element.79), channel_id=1, source_target_pairs={{0,8},{1,9},{16,24},{17,25},{32,40},{33,41},{48,56},{49,57},{64,72... | collective-permute-start | bytes 1179656 | tf_op jit(solution)/shard_map/ppermute | solution.py:320
  116.3 11.3 %collective-permute-start.12 = (f32[8,8,1536]{2,1,0:T(8,128)}, f32[8,8,1536]{2,1,0:T(8,128)}, u32[]{:S(2)}, u32[]{:S(2)}) collective-permute-start(f32[8,8,1536]{2,1,0:T(8,128)} %get-tuple-element.80), channel_id=1, source_target_pairs={{0,10},{1,11},{16,26},{17,27},{32,42},{33,43},{48,58},{49,59},{64,... | collective-permute-start | bytes 1179656 | tf_op jit(solution)/shard_map/ppermute | solution.py:320
  124.2 4.1 %collective-permute-start.8 = (f32[8,8,1536]{2,1,0:T(8,128)}, f32[8,8,1536]{2,1,0:T(8,128)S(1)}, u32[]{:S(2)}, u32[]{:S(2)}) collective-permute-start(f32[8,8,1536]{2,1,0:T(8,128)} %get-tuple-element.74), channel_id=1, source_target_pairs={{0,2},{1,3},{16,18},{17,19},{32,34},{33,35},{48,50},{49,51},{64,66... | collective-permute-start | bytes 1179656 | tf_op jit(solution)/shard_map/ppermute | solution.py:320
  124.9 3.4 %collective-permute-start.9 = (f32[8,8,1536]{2,1,0:T(8,128)}, f32[8,8,1536]{2,1,0:T(8,128)S(1)}, u32[]{:S(2)}, u32[]{:S(2)}) collective-permute-start(f32[8,8,1536]{2,1,0:T(8,128)} %get-tuple-element.75), channel_id=1, source_target_pairs={{0,4},{1,5},{16,20},{17,21},{32,36},{33,37},{48,52},{49,53},{64,68... | collective-permute-start | bytes 1179656 | tf_op jit(solution)/shard_map/ppermute | solution.py:320
  125.6 28.1 %collective-permute-start.10 = (f32[8,8,1536]{2,1,0:T(8,128)}, f32[8,8,1536]{2,1,0:T(8,128)S(1)}, u32[]{:S(2)}, u32[]{:S(2)}) collective-permute-start(f32[8,8,1536]{2,1,0:T(8,128)} %get-tuple-element.76), channel_id=1, source_target_pairs={{0,6},{1,7},{16,22},{17,23},{32,38},{33,39},{48,54},{49,55},{64,70... | collective-permute-start | bytes 1179656 | tf_op jit(solution)/shard_map/ppermute | solution.py:320
  126.9 26.7 %collective-permute-start.13 = (f32[8,8,1536]{2,1,0:T(8,128)}, f32[8,8,1536]{2,1,0:T(8,128)S(1)}, u32[]{:S(2)}, u32[]{:S(2)}) collective-permute-start(f32[8,8,1536]{2,1,0:T(8,128)} %get-tuple-element.81), channel_id=1, source_target_pairs={{0,12},{1,13},{16,28},{17,29},{32,44},{33,45},{48,60},{49,61},{64,... | collective-permute-start | bytes 1179656 | tf_op jit(solution)/shard_map/ppermute | solution.py:320
  127.6 26.0 %collective-permute-start.14 = (f32[8,8,1536]{2,1,0:T(8,128)}, f32[8,8,1536]{2,1,0:T(8,128)S(1)}, u32[]{:S(2)}, u32[]{:S(2)}) collective-permute-start(f32[8,8,1536]{2,1,0:T(8,128)} %get-tuple-element.82), channel_id=1, source_target_pairs={{0,14},{1,15},{16,30},{17,31},{32,46},{33,47},{48,62},{49,63},{64,... | collective-permute-start | bytes 1179656 | tf_op jit(solution)/shard_map/ppermute | solution.py:320
  155.0 20.3 %copy-start.6 = (f32[8,16,1536]{2,1,0:T(8,128)}, f32[8,16,1536]{2,1,0:T(8,128)S(1)}, u32[]{:S(2)}) copy-start(f32[8,16,1536]{2,1,0:T(8,128)S(1)} %all-to-all-done.refs_1_) | copy-start | bytes 2359300
  175.3 3.9 %copy-start.11 = (s32[3,1]{0,1:T(1,128)S(1)}, s32[3,1]{0,1:T(1,128)}, u32[]{:S(2)}) copy-start(s32[3,1]{0,1:T(1,128)} %param.13) | copy-start | bytes 40
  175.4 57.9 %all-to-all-start.2 = ((f32[8,48,1536]{2,1,0:T(8,128)}), f32[8,48,1536]{2,1,0:T(8,128)S(1)}, u32[]{:S(2)}, u32[]{:S(2)}) async-start(f32[8,48,1536]{2,1,0:T(8,128)} %get-tuple-element.85), calls=%async_computation.2 | async-start | bytes 4718592 | tf_op jit(solution)/shard_map/all_to_all | solution.py:308
  233.3 1.5 copy-start.3
Sparse Core Ops, SparseCore 0:
  9.1 44.1 all-gather.7
  76.6 75.3 all-gather.9
  175.5 38.0 all-gather.5

commit v5 on v4

--- a/solution.py
+++ b/solution.py
@@ -66,63 +66,61 @@
 
 def extend_kernel(first_place, map_blocks, scalars, places_ref, front_ref, source_ref, out_ref, *piece_refs):
     step = pl.program_id(0)
-    columns = out_ref.shape[1]
-    per_step = out_ref.shape[2] // LANES
+    groups, columns, width = out_ref.shape
+    per_group = width // LANES
     source_blocks = source_ref.shape[1] // LANES
     offset = scalars[scalars.shape[0] - 1]
     lane = lax.broadcasted_iota(jnp.int32, (8, LANES), 1)
-    group = max(1, 256 // columns)
-    for group_start in range(0, per_step, group):
-        gained = {}
-        members = range(group_start, min(per_step, group_start + group))
-        for j in members:
-            block = step * per_step + j
-            start = scalars[block]
-            at = jnp.minimum(start // LANES, map_blocks - 1)
-            split = jnp.where(start // LANES < map_blocks, start & (LANES - 1), LANES)
-            at = at - offset
-            inside_low = (at >= 0) & (at < source_blocks)
-            inside_high = (at + 1 >= 0) & (at + 1 < source_blocks)
-            low_at = pl.multiple_of(jnp.clip(at, 0, source_blocks - 1) * LANES, LANES)
-            high_at = pl.multiple_of(jnp.clip(at + 1, 0, source_blocks - 1) * LANES, LANES)
-            place = jnp.broadcast_to(places_ref[pl.ds(first_place + block, 1), :], (8, LANES))
-            inner = place & (LANES - 1)
-            hit = ((place >= 0) & (place < LANES) & inside_low) | ((place >= LANES) & inside_high)
-            from_low = lane >= split
-            for row in range(0, columns, 8):
-                rows = slice(row, row + 8)
-                merged = jnp.where(
-                    from_low, source_ref[rows, pl.ds(low_at, LANES)], source_ref[rows, pl.ds(high_at, LANES)]
-                )
-                gained[j, row] = jnp.where(hit, jnp.take_along_axis(merged, inner, axis=1), 0.0)
-        for j in members:
-            here = slice(j * LANES, (j + 1) * LANES)
-            for row in range(0, columns, 8):
-                rows = slice(row, row + 8)
-                value = front_ref[..., rows, here].reshape(8, LANES) + gained[j, row]
-                out_ref[0, rows, here] = value
-                if piece_refs:
-                    piece_refs[row // 8][0, :, here] = value
-
-
-def extend_add(front, source, places, first_place, starts, offset, map_blocks, steps, width, columns=None, part=0, pieces=0):
+    for j in range(groups * per_group):
+        block = step * groups * per_group + j
+        start = scalars[block]
+        at = jnp.minimum(start // LANES, map_blocks - 1)
+        split = jnp.where(start // LANES < map_blocks, start & (LANES - 1), LANES)
+        at = at - offset
+        inside_low = (at >= 0) & (at < source_blocks)
+        inside_high = (at + 1 >= 0) & (at + 1 < source_blocks)
+        low_at = pl.multiple_of(jnp.clip(at, 0, source_blocks - 1) * LANES, LANES)
+        high_at = pl.multiple_of(jnp.clip(at + 1, 0, source_blocks - 1) * LANES, LANES)
+        place = jnp.broadcast_to(places_ref[pl.ds(first_place + block, 1), :], (8, LANES))
+        inner = place & (LANES - 1)
+        hit = ((place >= 0) & (place < LANES) & inside_low) | ((place >= LANES) & inside_high)
+        from_low = lane >= split
+        group = j // per_group
+        here = slice(j % per_group * LANES, (j % per_group + 1) * LANES)
+        for row in range(0, columns, 8):
+            rows = slice(row, row + 8)
+            merged = jnp.where(from_low, source_ref[rows, pl.ds(low_at, LANES)], source_ref[rows, pl.ds(high_at, LANES)])
+            gained = jnp.where(hit, jnp.take_along_axis(merged, inner, axis=1), 0.0)
+            if len(front_ref.shape) == 2:
+                value = front_ref[rows, j * LANES : (j + 1) * LANES] + gained
+            else:
+                value = front_ref[group, rows, here] + gained
+            out_ref[group, rows, here] = value
+            if piece_refs:
+                piece_refs[row // 8][group, :, here] = value
+
+
+def extend_add(front, source, places, first_place, starts, offset, map_blocks, groups, width, columns=None, part=0, pieces=0):
     columns = source.shape[0] if columns is None else columns
+    steps = 2 if groups % 2 == 0 else 1
+    per_step = groups // steps
     if front.ndim == 2:
-        front_spec = pl.BlockSpec((columns, width), lambda i, _: (part, i))
+        front_spec = pl.BlockSpec((columns, per_step * width), lambda i, _: (part, i))
     else:
-        front_spec = pl.BlockSpec((1, columns, width), lambda i, _: (i, 0, 0))
-    source_width = min(source.shape[1], map_blocks * LANES if steps > 1 else width)
+        front_spec = pl.BlockSpec((per_step, columns, width), lambda i, _: (i, part, 0))
+    source_part = part if source.shape[0] > columns else 0
+    source_width = min(source.shape[1], map_blocks * LANES if groups > 1 else width)
     scalars = jnp.concatenate([starts, offset.reshape(1)]).astype(jnp.int32)
     whole = lambda shape, row=0: pl.BlockSpec(shape, lambda i, _: (row, 0), pipeline_mode=pl.Buffered(1))
     sizes = [columns] + [8] * pieces
     outs = pl.pallas_call(
         functools.partial(extend_kernel, first_place, map_blocks),
-        out_shape=[jax.ShapeDtypeStruct((steps, size, width), jnp.float32) for size in sizes],
+        out_shape=[jax.ShapeDtypeStruct((groups, size, width), jnp.float32) for size in sizes],
         grid_spec=pltpu.PrefetchScalarGridSpec(
             num_scalar_prefetch=1,
             grid=(steps,),
-            in_specs=[whole(places.shape), front_spec, whole((columns, source_width), part)],
-            out_specs=[pl.BlockSpec((1, size, width), lambda i, _: (i, 0, 0)) for size in sizes],
+            in_specs=[whole(places.shape), front_spec, whole((columns, source_width), source_part)],
+            out_specs=[pl.BlockSpec((per_step, size, width), lambda i, _: (i, 0, 0)) for size in sizes],
         ),
         compiler_params=pltpu.CompilerParams(vmem_limit_bytes=VMEM_BYTES),
     )(scalars, places, front, source)
@@ -238,9 +236,11 @@
 
     window = -(-(child_rows * 13 // 24) // LANES) * LANES
     rest = child_rows - window
-    tail = thin // 4
-    parts = [(thin - tail, thin), (0, thin - tail)]
-    received = [exchange(jnp.where(side == 0, own[a:b, rest:], own[a:b, :window])) for a, b in parts]
+    parts = [(thin // 2, thin), (0, thin // 2)]
+    first_sent, last_sent = [jnp.where(side == 0, own[a:b, rest:], own[a:b, :window]) for a, b in parts]
+    received = [exchange(first_sent)]
+    last_sent, received[0] = lax.optimization_barrier((last_sent, received[0]))
+    received.append(exchange(last_sent))
 
     map_blocks = child_rows // LANES
     blocks = half_rows // LANES
@@ -258,9 +258,48 @@
     prefix = own[:, :pivot_rows]
     base = strip_add(front, own, 0)
     got = exchange(jnp.concatenate([jnp.where(side == 0, base, prefix), mask_rows]))
-    got, received[0] = lax.optimization_barrier((got, received[0]))
+
+    first_row = (side * half_rows).astype(jnp.int32)
+    own_map = lax.dynamic_index_in_dim(row_maps, side, 0, keepdims=False)
+    other_map = lax.dynamic_index_in_dim(row_maps, 1 - side, 0, keepdims=False)
+    starts = count(jnp.stack([own_map, other_map]), first_row + edges)
+    places = search(
+        maps,
+        [side.astype(jnp.int32), (1 - side).astype(jnp.int32)],
+        [first_row, first_row],
+        [starts[0], starts[1]],
+    )
+    lower = jnp.sum((row_maps < half_rows).astype(jnp.int32), axis=1)
+    spill = (child_rows - lower[0] > window) | (lower[1] > window)
+    window_at = jnp.where(side == 0, 0, rest // LANES).astype(jnp.int32)
+    rest_at = jnp.where(side == 0, window // LANES, 0).astype(jnp.int32)
+    add = functools.partial(extend_add, places=places, map_blocks=map_blocks, groups=grid_rows, width=row_count)
+    add_other = functools.partial(add, first_place=blocks, starts=starts[1])
+    base_sum = add(front, own, first_place=0, starts=starts[0], offset=zero)
+
+    def add_rest(base_sum):
+        more = exchange(jnp.where(side == 0, own[:, :rest], own[:, window:]))
+        return add_other(base_sum, more, offset=rest_at)
+
+    base_sum = lax.cond(spill, add_rest, lambda x: x, base_sum)
+
+    got, received[0], base_sum = lax.optimization_barrier((got, received[0], base_sum))
     strip = strip_add(jnp.where(side == 0, base, got[:thin]), jnp.where(side == 0, got[:thin], prefix), 1)
     first_masks = jnp.where(side == 0, mask_rows, got[thin:])
+
+    wholes, pieces = [], {}
+
+    def assemble(index):
+        a, b = parts[index]
+        size = b - a
+        whole, *chunk_list = add_other(
+            base_sum, received[index], offset=window_at, columns=size, part=a // size, pieces=size // 8
+        )
+        wholes.append(whole)
+        pieces.update({a // 8 + i: chunk for i, chunk in enumerate(chunk_list)})
+
+    assemble(0)
+    strip, wholes[0] = lax.optimization_barrier((strip, wholes[0]))
 
     cols = lax.axis_size("col")
     corner = jnp.where(place == 0, strip[:, PANEL:], strip[:, :PANEL])
@@ -278,42 +317,9 @@
     gathered = lax.all_gather(jnp.concatenate([strip, corner[:thin], first_masks]), "row", axis=0)
     kept = gathered[0, 2 * thin, 1] > 0.5
 
-    first_row = (side * half_rows).astype(jnp.int32)
-    own_map = lax.dynamic_index_in_dim(row_maps, side, 0, keepdims=False)
-    other_map = lax.dynamic_index_in_dim(row_maps, 1 - side, 0, keepdims=False)
-    starts = count(jnp.stack([own_map, other_map]), first_row + edges)
-    places = search(
-        maps,
-        [side.astype(jnp.int32), (1 - side).astype(jnp.int32)],
-        [first_row, first_row],
-        [starts[0], starts[1]],
-    )
-    lower = jnp.sum((row_maps < half_rows).astype(jnp.int32), axis=1)
-    spill = (child_rows - lower[0] > window) | (lower[1] > window)
-    window_at = jnp.where(side == 0, 0, rest // LANES).astype(jnp.int32)
-    rest_at = jnp.where(side == 0, window // LANES, 0).astype(jnp.int32)
-    add = functools.partial(extend_add, places=places, map_blocks=map_blocks, steps=grid_rows, width=row_count)
-    add_own = functools.partial(add, first_place=0, starts=starts[0], offset=zero)
-    add_other = functools.partial(add, first_place=blocks, starts=starts[1])
-    bases = [add_own(front, own, columns=b - a, part=a // (b - a)) for a, b in parts]
-
-    def add_rest(bases):
-        more = exchange(jnp.where(side == 0, own[:, :rest], own[:, window:]))
-        return tuple(
-            add_other(base, more, offset=rest_at, columns=b - a, part=a // (b - a)) for base, (a, b) in zip(bases, parts)
-        )
-
-    bases = lax.cond(spill, add_rest, lambda x: x, tuple(bases))
-
     across = lambda x: lax.all_to_all(x, "row", split_axis=0, concat_axis=0, tiled=True)
-    wholes, pieces = [], {}
-    for base, part, (a, b) in zip(bases, received, parts):
-        whole, *chunk_list = add_other(base, part, offset=window_at, pieces=(b - a) // 8)
-        wholes.append(whole)
-        pieces.update({a // 8 + i: chunk for i, chunk in enumerate(chunk_list)})
-    order = list(range(chunks))
-    middle = chunks // 2
-    order[middle : middle + 2], order[-2:] = order[-2:], order[middle : middle + 2]
+    assemble(1)
+    order = [0, 1] + list(range(chunks // 2, chunks)) + list(range(2, chunks // 2))
     mine = jnp.where(place // PANELS == 0, pieces[order[0]], 0.0)
     for chip in range(1, chunks):
         pairs = [(k, PANELS * chip + k) for k in range(PANELS)]

time: 254 us -> 260 us (1.024)
  waiting for transfers between devices: 100 us -> 119 us
  Pallas kernels: 59.8 us -> 47.2 us
    all_gather x1, waiting for transfers between devices: 0.01 us -> 20.9 us  [local(): lax.all_gather(mine.reshape(thin, row_count), 'col', axis=0, tiled=True)]
    ppermute x7, waiting for transfers between devices: 25.3 us -> 9.76 us  [local(): mine = mine + lax.ppermute(pieces[order[chip]], 'col', pairs)]
    pallas_call x6 -> x5, Pallas kernels: 32.7 us -> 20.1 us  [extend_add(): pl.pallas_call(functools.partial(extend_kernel, first_place, map_blocks),...]
    all_gather x1, waiting for transfers between devices: 0.01 us -> 10.7 us  [local(): lax.all_gather(jnp.concatenate([strip, corner[:thin], first_masks]), 'row...]
    all_to_all x2, waiting for transfers between devices: 41 us -> 50.2 us  [local(): lax.all_to_all(x, 'row', split_axis=0, concat_axis=0, tiled=True)]
    ppermute x3, waiting for transfers between devices: 20.6 us -> 16.1 us  [local(): corner = corner + lax.ppermute(corner, 'col', pairs)]
  transfers between devices with their start and end apart: 19 -> 19, of which waited for: 6 -> 8; matrix products, arithmetic and copies ran while one was open for 9% -> 8% of each run, Pallas kernels for 19% -> 14%
where the time goes in v5:
time: 260 us; the launch traced here: 258 us
  waiting for transfers between devices  119 us (46%)
  Pallas kernels  47.2 us (18%)
  starting transfers between devices  28.5 us (11%)
  blocking collectives  22.6 us (9%)
  other arithmetic  18.2 us (7%)
  between operations  15.3 us (6%)
  local copies, waits for them, and re-layouts  7.39 us (3%)
    all_to_all x2, waiting for transfers between devices, local(): lax.all_to_all(x, 'row', split_axis=0, concat_axis=0, tiled=True)  50.2 us
    all_to_all x1, blocking collectives, local(): lax.all_to_all(x, 'row', split_axis=0, concat_axis=0, tiled=True)  22.6 us
    all_gather x1, waiting for transfers between devices, local(): lax.all_gather(mine.reshape(thin, row_count), 'col', axis=0, tiled=True)  20.9 us
    pallas_call x5, Pallas kernels, extend_add(): pl.pallas_call(functools.partial(extend_kernel, first_place, map_blocks),...  20.1 us
    ppermute x3, waiting for transfers between devices, local(): corner = corner + lax.ppermute(corner, 'col', pairs)  16.1 us
    all_to_all x2, starting transfers between devices, local(): lax.all_to_all(x, 'row', split_axis=0, concat_axis=0, tiled=True)  12.1 us
    pallas_call x1, Pallas kernels, update(): pl.pallas_call(update_kernel, out_shape=jax.ShapeDtypeStruct((rows, PANEL...  10.9 us
    all_gather x1, waiting for transfers between devices, local(): lax.all_gather(jnp.concatenate([strip, corner[:thin], first_masks]), 'row...  10.7 us
  transfers between devices with their start and end apart: 19, of which 8 were waited for; matrix products, arithmetic and copies ran while one was open for 8% of the time, Pallas kernels for 14%

profile of v5, /device:TPU:10, one launch (start us, length us, event | category | flops | bytes accessed | tf_op | source)
XLA Modules:
  0.0 257.7 jit_solution(12657219090976704342)
XLA Ops:
  6.5 1.0 slice_bitcast_fusion.1
  7.5 0.7 pad_maximum_fusion.1
  9.0 1.2 convert_reduce_fusion.1
  10.2 1.5 copy.10
  13.1 2.9 %shard_map.55.places_ref = s32[16,128]{1,0:T(8,128)} custom-call(s32[20]{0:T(128)} %concatenate.40.scalars, s32[2,96,128]{2,1,0:T(8,128)} %bitcast.57), custom_call_target="tpu_custom_call" | custom-call | tf_op jit(solution)/shard_map/pallas_call | solution.py:53
  16.0 2.9 %shard_map.56 = f32[1,64,1024]{2,1,0:T(8,128)} custom-call(s32[9]{0:T(128)} %get-tuple-element.112.scalars, s32[16,128]{1,0:T(8,128)} %shard_map.55.places_ref, f32[64,12288]{1,0:T(8,128)} %bitcast.47, f32[64,12288]{1,0:T(8,128)} %bitcast.41), custom_call_target="tpu_custom_call" | custom-call | tf_op jit(solution)/shard_map/pallas_call | solution.py:116
  18.8 1.0 bitcast_select_fusion.1
  19.8 0.7 pad_maximum_fusion
  20.6 2.3 collective-permute-start.1
  22.9 1.4 slice_select_fusion.1
  24.3 1.2 collective-permute-start.2
  26.0 1.1 convert_reduce_fusion
  28.9 0.7 concatenate.44.scalars
  29.6 4.3 %shard_map.57.places_ref = s32[192,128]{1,0:T(8,128)S(1)} custom-call(s32[196]{0:T(256)} %concatenate.44.scalars, s32[2,96,128]{2,1,0:T(8,128)} %bitcast.58), custom_call_target="tpu_custom_call" | custom-call | tf_op jit(solution)/shard_map/pallas_call | solution.py:53
  34.5 4.8 %shard_map.58 = f32[8,64,1536]{2,1,0:T(8,128)} custom-call(s32[97]{0:T(128)} %get-tuple-element.114.scalars, s32[192,128]{1,0:T(8,128)S(1)} %shard_map.57.places_ref, f32[64,12288]{1,0:T(8,128)} %bitcast.48, f32[64,12288]{1,0:T(8,128)S(1)} %bitcast.44), custom_call_target="tpu_custom_call" | custom-call | tf_op jit(solution)/shard_map/pallas_call | solution.py:116
  39.4 10.0 %collective-permute-done.2.source_ref = f32[32,6656]{1,0:T(8,128)} collective-permute-done((f32[32,6656]{1,0:T(8,128)}, f32[32,6656]{1,0:T(8,128)}, u32[]{:S(2)}, u32[]{:S(2)}) %collective-permute-start.2) | collective-permute-done | bytes 852000 | tf_op jit(solution)/shard_map/ppermute | solution.py:233
  49.4 2.3 collective-permute-start.6
  51.7 1.8 slice_select_fusion.3
  53.6 2.6 shard_map.59
  56.1 5.1 %shard_map.60 = (f32[8,32,1536]{2,1,0:T(8,128)}, f32[8,8,1536]{2,1,0:T(8,128)}, f32[8,8,1536]{2,1,0:T(8,128)}, f32[8,8,1536]{2,1,0:T(8,128)}, f32[8,8,1536]{2,1,0:T(8,128)}) custom-call(s32[97]{0:T(128)} %get-tuple-element.115.scalars, s32[192,128]{1,0:T(8,128)S(1)} %shard_map.57.places_ref, f32[8,64,1536]{2,1,0:T(8,128)} %get-tuple-element.116.front_ref, ...), custom_call_target="tpu_custom_call" | custom-call | tf_op jit(solution)/shard_map/pallas_call | solution.py:116
  62.0 0.8 collective-permute-start.4
  62.8 0.7 add.94
  63.5 1.3 collective-permute-start.5
  64.8 16.1 %collective-permute-done.5 = f32[72,512]{1,0:T(8,128)} collective-permute-done((f32[72,512]{1,0:T(8,128)}, f32[72,512]{1,0:T(8,128)}, u32[]{:S(2)}, u32[]{:S(2)}) %collective-permute-start.5) | collective-permute-done | bytes 147488 | tf_op jit(solution)/shard_map/ppermute | solution.py:310
  80.9 1.7 add.95
  82.6 0.8 slice_select_fusion.5
  83.3 0.8 collective-permute-done.7
  84.2 0.9 broadcast_select_fusion
  85.8 0.9 fusion.1
  86.6 8.5 %all-to-all-start = ((f32[8,32,1536]{2,1,0:T(8,128)}), f32[8,32,1536]{2,1,0:T(8,128)}, u32[]{:S(2)}, u32[]{:S(2)}) async-start(f32[8,32,1536]{2,1,0:T(8,128)} %get-tuple-element.86), calls=%async_computation | async-start | bytes 3145728 | tf_op jit(solution)/shard_map/all_to_all | solution.py:320
  95.2 1.4 collective-permute-start.9
  96.6 1.3 collective-permute-start.10
  97.9 1.6 collective-permute-start.11
  99.5 1.4 collective-permute-start.12
  100.9 4.7 %shard_map.61 = (f32[8,32,1536]{2,1,0:T(8,128)}, f32[8,8,1536]{2,1,0:T(8,128)}, f32[8,8,1536]{2,1,0:T(8,128)}, f32[8,8,1536]{2,1,0:T(8,128)}, f32[8,8,1536]{2,1,0:T(8,128)}) custom-call(s32[97]{0:T(128)} %get-tuple-element.115.scalars, s32[192,128]{1,0:T(8,128)S(1)} %shard_map.57.places_ref, f32[8,64,1536]{2,1,0:T(8,128)S(1)} %copy-done.2, ...), custom_call_target="tpu_custom_call" | custom-call | tf_op jit(solution)/shard_map/pallas_call | solution.py:116
  106.4 0.7 collective-permute-start.13
  107.0 9.7 %collective-permute-done.10 = f32[8,8,1536]{2,1,0:T(8,128)} collective-permute-done((f32[8,8,1536]{2,1,0:T(8,128)}, f32[8,8,1536]{2,1,0:T(8,128)}, u32[]{:S(2)}, u32[]{:S(2)}) %collective-permute-start.10) | collective-permute-done | bytes 393248 | tf_op jit(solution)/shard_map/ppermute | solution.py:326
  117.6 1.6 add_add_fusion
  119.1 32.0 %all-to-all-done.refs_1_ = f32[8,32,1536]{2,1,0:T(8,128)} async-done(((f32[8,32,1536]{2,1,0:T(8,128)}), f32[8,32,1536]{2,1,0:T(8,128)}, u32[]{:S(2)}, u32[]{:S(2)}) %all-to-all-start) | async-done | bytes 1572896 | tf_op jit(solution)/shard_map/all_to_all | solution.py:320
  151.1 22.6 %all_to_all.15 = f32[8,8,1536]{2,1,0:T(8,128)} all-to-all(f32[8,8,1536]{2,1,0:T(8,128)S(1)} %add_add_fusion), channel_id=1, replica_groups=mesh['subcube'=2,'row'=8,'col'=16] {'row'}, dimensions={0} | all-to-all | bytes 786432 | tf_op jit(solution)/shard_map/all_to_all | solution.py:320
  173.8 3.6 %all-to-all-start.2 = ((f32[8,32,1536]{2,1,0:T(8,128)}), f32[8,32,1536]{2,1,0:T(8,128)S(1)}, u32[]{:S(2)}, u32[]{:S(2)}) async-start(f32[8,32,1536]{2,1,0:T(8,128)} %get-tuple-element.88), calls=%async_computation.2 | async-start | bytes 3145728 | tf_op jit(solution)/shard_map/all_to_all | solution.py:320
  177.4 0.7 fusion.5
  178.9 10.7 %all-gather.10.cloned.1.call-done = f32[1088,1024]{1,0:T(8,128)} async-done(((f32[136,1024]{1,0:T(8,128)}), f32[1088,1024]{1,0:T(8,128)}) %all-gather.10.cloned.1.call-update) | async-done | bytes 4456464 | tf_op jit(solution)/shard_map/all_gather | solution.py:317
  189.5 1.3 slice.121
  192.2 9.0 %shard_map.62 = (f32[512,512]{1,0:T(8,128)}, f32[512,512]{1,0:T(8,128)}, f32[512,512]{1,0:T(8,128)}) custom-call(s32[2]{0:T(128)} %pad_add_fusion.6.flags, f32[8,136,1024]{2,1,0:T(8,128)} %bitcast.51, f32[8,64,1024]{2,1,0:T(8,128)} %bitcast.54), custom_call_target="tpu_custom_call" | custom-call | tf_op jit(solution)/shard_map/pallas_call | solution.py:170
  201.2 18.2 %all-to-all-done.2.refs_0_ = f32[8,32,1536]{2,1,0:T(8,128)S(1)} async-done(((f32[8,32,1536]{2,1,0:T(8,128)}), f32[8,32,1536]{2,1,0:T(8,128)S(1)}, u32[]{:S(2)}, u32[]{:S(2)}) %all-to-all-start.2) | async-done | bytes 1572896 | tf_op jit(solution)/shard_map/all_to_all | solution.py:320
  219.4 20.9 %all-gather.6.cloned.1.call-done = f32[1024,1536]{1,0:T(8,128)} async-done(((f32[64,1536]{1,0:T(8,128)}), f32[1024,1536]{1,0:T(8,128)}) %all-gather.6.cloned.1.call-update) | async-done | bytes 6291472 | tf_op jit(solution)/shard_map/all_gather | solution.py:330
  240.3 10.9 %shard_map.63 = f32[1536,512]{1,0:T(8,128)} custom-call(s32[12]{0:T(128)} %reshape.125.flags, f32[8,32,1536]{2,1,0:T(8,128)} %copy-done.3, f32[8,32,1536]{2,1,0:T(8,128)} %all-to-all-done.refs_1_, f32[8,2,64,1536]{3,2,1,0:T(8,128)} %bitcast.49, f32[512,512]{1,0:T(8,128)} %get-tuple-element.91.refs_3_, f32[512,512]{1,0:T(8,128)} %get-tuple-element.92.refs_4_, ...), custom_call_target="tpu_custom_call" | custom-call | tf_op jit(solution)/shard_map/pallas_call | solution.py:201
  (62 shorter events, 8.0 us)
Async XLA Ops:
  6.5 76.0 %all-gather.8.cloned.1.call-start = ((), (), s32[]{:S(2)}) async-start(), calls=%async_computation.4 | async-start | bytes 2359296 | tf_op jit(solution)/shard_map/all_gather | solution.py:235
  8.3 181.2 %all-gather.10.cloned.1.call-start = ((), (), s32[]{:S(2)}) async-start(), calls=%async_computation.5 | async-start | bytes 5013504 | tf_op jit(solution)/shard_map/all_gather | solution.py:317
  16.0 2.9 %copy-start = (f32[1,1,1,64,12288]{4,3,2,1,0:T(8,128)S(1)}, f32[1,1,1,64,12288]{4,3,2,1,0:T(8,128)}, u32[]{:S(2)}) copy-start(f32[1,1,1,64,12288]{4,3,2,1,0:T(8,128)} %param.10) | copy-start | bytes 9437188
  18.8 6.7 %copy-start.6 = (s32[2,12288]{1,0:T(2,128)S(1)}, s32[2,12288]{1,0:T(2,128)}, u32[]{:S(2)}) copy-start(s32[2,12288]{1,0:T(2,128)} %param.11) | copy-start | bytes 294916
  20.6 31.1 %collective-permute-start.1 = (f32[72,1024]{1,0:T(8,128)}, f32[72,1024]{1,0:T(8,128)}, u32[]{:S(2)}, u32[]{:S(2)}) collective-permute-start(f32[72,1024]{1,0:T(8,128)} %pad_maximum_fusion), channel_id=1, source_target_pairs={{0,128},{128,0},{1,129},{129,1},{2,130},{130,2},{3,131},{131,3},{4... | collective-permute-start | bytes 884744 | tf_op jit(solution)/shard_map/ppermute | solution.py:233
  24.3 25.1 %collective-permute-start.2 = (f32[32,6656]{1,0:T(8,128)}, f32[32,6656]{1,0:T(8,128)}, u32[]{:S(2)}, u32[]{:S(2)}) collective-permute-start(f32[32,6656]{1,0:T(8,128)} %get-tuple-element.94), channel_id=1, source_target_pairs={{0,128},{128,0},{1,129},{129,1},{2,130},{130,2},{3,131},{131,3},{4... | collective-permute-start | bytes 2555912 | tf_op jit(solution)/shard_map/ppermute | solution.py:233
  39.4 12.4 %copy-start.5 = (f32[1,64,1024]{2,1,0:T(8,128)S(1)}, f32[1,64,1024]{2,1,0:T(8,128)}, u32[]{:S(2)}) copy-start(f32[1,64,1024]{2,1,0:T(8,128)} %shard_map.56) | copy-start | bytes 786436
  49.4 33.2 %collective-permute-start.6 = (f32[32,6656]{1,0:T(8,128)}, f32[32,6656]{1,0:T(8,128)}, u32[]{:S(2)}, u32[]{:S(2)}) collective-permute-start(f32[32,6656]{1,0:T(8,128)} %get-tuple-element.74), channel_id=1, source_target_pairs={{0,128},{128,0},{1,129},{129,1},{2,130},{130,2},{3,131},{131,3},{4... | collective-permute-start | bytes 2555912 | tf_op jit(solution)/shard_map/ppermute | solution.py:233
  56.1 5.1 %copy-start.4 = (f32[1,64,1024]{2,1,0:T(8,128)S(1)}, f32[1,64,1024]{2,1,0:T(8,128)}, u32[]{:S(2)}) copy-start(f32[1,64,1024]{2,1,0:T(8,128)} %shard_map.59) | copy-start | bytes 786436
  61.2 0.7 collective-permute-start.3
  62.0 39.0 %copy-start.2 = (f32[8,64,1536]{2,1,0:T(8,128)S(1)}, f32[8,64,1536]{2,1,0:T(8,128)}, u32[]{:S(2)}) copy-start(f32[8,64,1536]{2,1,0:T(8,128)} %get-tuple-element.116.front_ref) | copy-start | bytes 9437188
  62.0 0.8 collective-permute-start.4
  63.5 17.4 %collective-permute-start.5 = (f32[72,512]{1,0:T(8,128)}, f32[72,512]{1,0:T(8,128)}, u32[]{:S(2)}, u32[]{:S(2)}) collective-permute-start(f32[72,512]{1,0:T(8,128)} %add.94), channel_id=1, source_target_pairs={{0,2},{1,3},{4,6},{5,7},{8,10},{9,11},{12,14},{13,15},{16,18},{17,... | collective-permute-start | bytes 442376 | tf_op jit(solution)/shard_map/ppermute | solution.py:310
  82.6 1.6 collective-permute-start.7
  85.1 0.7 copy-start.7
  86.6 64.5 %all-to-all-start = ((f32[8,32,1536]{2,1,0:T(8,128)}), f32[8,32,1536]{2,1,0:T(8,128)}, u32[]{:S(2)}, u32[]{:S(2)}) async-start(f32[8,32,1536]{2,1,0:T(8,128)} %get-tuple-element.86), calls=%async_computation | async-start | bytes 3145728 | tf_op jit(solution)/shard_map/all_to_all | solution.py:320
  95.1 145.2 %all-gather.6.cloned.1.call-start = ((), (), s32[]{:S(2)}) async-start(), calls=%async_computation.3 | async-start | bytes 6684672 | tf_op jit(solution)/shard_map/all_gather | solution.py:330
  95.2 11.2 %collective-permute-start.9 = (f32[8,8,1536]{2,1,0:T(8,128)}, f32[8,8,1536]{2,1,0:T(8,128)}, u32[]{:S(2)}, u32[]{:S(2)}) collective-permute-start(f32[8,8,1536]{2,1,0:T(8,128)} %get-tuple-element.80), channel_id=1, source_target_pairs={{0,4},{1,5},{16,20},{17,21},{32,36},{33,37},{48,52},{49,53},{64,68... | collective-permute-start | bytes 1179656 | tf_op jit(solution)/shard_map/ppermute | solution.py:326
  96.6 20.2 %collective-permute-start.10 = (f32[8,8,1536]{2,1,0:T(8,128)}, f32[8,8,1536]{2,1,0:T(8,128)}, u32[]{:S(2)}, u32[]{:S(2)}) collective-permute-start(f32[8,8,1536]{2,1,0:T(8,128)} %get-tuple-element.81), channel_id=1, source_target_pairs={{0,6},{1,7},{16,22},{17,23},{32,38},{33,39},{48,54},{49,55},{64,70... | collective-permute-start | bytes 1179656 | tf_op jit(solution)/shard_map/ppermute | solution.py:326
  97.9 19.6 %collective-permute-start.11 = (f32[8,8,1536]{2,1,0:T(8,128)}, f32[8,8,1536]{2,1,0:T(8,128)}, u32[]{:S(2)}, u32[]{:S(2)}) collective-permute-start(f32[8,8,1536]{2,1,0:T(8,128)} %get-tuple-element.82), channel_id=1, source_target_pairs={{0,8},{1,9},{16,24},{17,25},{32,40},{33,41},{48,56},{49,57},{64,72... | collective-permute-start | bytes 1179656 | tf_op jit(solution)/shard_map/ppermute | solution.py:326
  99.5 18.0 %collective-permute-start.12 = (f32[8,8,1536]{2,1,0:T(8,128)}, f32[8,8,1536]{2,1,0:T(8,128)}, u32[]{:S(2)}, u32[]{:S(2)}) collective-permute-start(f32[8,8,1536]{2,1,0:T(8,128)} %get-tuple-element.83), channel_id=1, source_target_pairs={{0,10},{1,11},{16,26},{17,27},{32,42},{33,43},{48,58},{49,59},{64,... | collective-permute-start | bytes 1179656 | tf_op jit(solution)/shard_map/ppermute | solution.py:326
  105.7 11.9 %collective-permute-start.8 = (f32[8,8,1536]{2,1,0:T(8,128)}, f32[8,8,1536]{2,1,0:T(8,128)S(1)}, u32[]{:S(2)}, u32[]{:S(2)}) collective-permute-start(f32[8,8,1536]{2,1,0:T(8,128)} %get-tuple-element.79), channel_id=1, source_target_pairs={{0,2},{1,3},{16,18},{17,19},{32,34},{33,35},{48,50},{49,51},{64,66... | collective-permute-start | bytes 1179656 | tf_op jit(solution)/shard_map/ppermute | solution.py:326
  106.4 11.2 %collective-permute-start.13 = (f32[8,8,1536]{2,1,0:T(8,128)}, f32[8,8,1536]{2,1,0:T(8,128)S(1)}, u32[]{:S(2)}, u32[]{:S(2)}) collective-permute-start(f32[8,8,1536]{2,1,0:T(8,128)} %get-tuple-element.84), channel_id=1, source_target_pairs={{0,12},{1,13},{16,28},{17,29},{32,44},{33,45},{48,60},{49,61},{64,... | collective-permute-start | bytes 1179656 | tf_op jit(solution)/shard_map/ppermute | solution.py:326
  116.8 0.7 collective-permute-start.14
  117.5 59.8 %copy-start.8 = (s32[3,1]{0,1:T(1,128)S(1)}, s32[3,1]{0,1:T(1,128)}, u32[]{:S(2)}) copy-start(s32[3,1]{0,1:T(1,128)} %param.13) | copy-start | bytes 40
  173.8 45.6 %all-to-all-start.2 = ((f32[8,32,1536]{2,1,0:T(8,128)}), f32[8,32,1536]{2,1,0:T(8,128)S(1)}, u32[]{:S(2)}, u32[]{:S(2)}) async-start(f32[8,32,1536]{2,1,0:T(8,128)} %get-tuple-element.88), calls=%async_computation.2 | async-start | bytes 3145728 | tf_op jit(solution)/shard_map/all_to_all | solution.py:320
  219.4 20.9 %copy-start.3 = (f32[8,32,1536]{2,1,0:T(8,128)}, f32[8,32,1536]{2,1,0:T(8,128)S(1)}, u32[]{:S(2)}) copy-start(f32[8,32,1536]{2,1,0:T(8,128)S(1)} %all-to-all-done.2.refs_0_) | copy-start | bytes 4718596
Sparse Core Ops, SparseCore 0:
  9.1 44.1 all-gather.7
  86.8 102.7 all-gather.9
  191.4 48.8 all-gather.5

commit v6 on v5

--- a/solution.py
+++ b/solution.py
@@ -64,7 +64,8 @@
     )(scalars, maps)
 
 
-def extend_kernel(first_place, map_blocks, scalars, places_ref, front_ref, source_ref, out_ref, *piece_refs):
+def extend_kernel(first_place, map_blocks, scalars, places_ref, front_ref, source_ref, *refs):
+    tail_ref, out_ref, piece_refs = (refs[0], refs[1], refs[2:]) if len(refs) > 1 else (None, refs[0], ())
     step = pl.program_id(0)
     groups, columns, width = out_ref.shape
     per_group = width // LANES
@@ -98,9 +99,14 @@
             out_ref[group, rows, here] = value
             if piece_refs:
                 piece_refs[row // 8][group, :, here] = value
-
-
-def extend_add(front, source, places, first_place, starts, offset, map_blocks, groups, width, columns=None, part=0, pieces=0):
+    for index, piece_ref in enumerate(piece_refs):
+        rows = slice(8 * index, 8 * index + 8)
+        for group in range(groups):
+            lanes = pl.ds(pl.multiple_of((step * groups + group) * LANES, LANES), LANES)
+            piece_ref[group, :, width:] = tail_ref[rows, lanes]
+
+
+def extend_add(front, source, places, first_place, starts, offset, map_blocks, groups, width, columns=None, part=0, tail=None):
     columns = source.shape[0] if columns is None else columns
     steps = 2 if groups % 2 == 0 else 1
     per_step = groups // steps
@@ -112,19 +118,24 @@
     source_width = min(source.shape[1], map_blocks * LANES if groups > 1 else width)
     scalars = jnp.concatenate([starts, offset.reshape(1)]).astype(jnp.int32)
     whole = lambda shape, row=0: pl.BlockSpec(shape, lambda i, _: (row, 0), pipeline_mode=pl.Buffered(1))
-    sizes = [columns] + [8] * pieces
+    shapes = [(columns, width)]
+    inputs, in_specs = [places, front, source], [whole(places.shape), front_spec, whole((columns, source_width), source_part)]
+    if tail is not None:
+        shapes += [(8, width + LANES)] * (columns // 8)
+        inputs.append(tail)
+        in_specs.append(whole((columns, tail.shape[1]), part))
     outs = pl.pallas_call(
         functools.partial(extend_kernel, first_place, map_blocks),
-        out_shape=[jax.ShapeDtypeStruct((groups, size, width), jnp.float32) for size in sizes],
+        out_shape=[jax.ShapeDtypeStruct((groups,) + shape, jnp.float32) for shape in shapes],
         grid_spec=pltpu.PrefetchScalarGridSpec(
             num_scalar_prefetch=1,
             grid=(steps,),
-            in_specs=[whole(places.shape), front_spec, whole((columns, source_width), source_part)],
-            out_specs=[pl.BlockSpec((per_step, size, width), lambda i, _: (i, 0, 0)) for size in sizes],
+            in_specs=in_specs,
+            out_specs=[pl.BlockSpec((per_step,) + shape, lambda i, _: (i, 0, 0)) for shape in shapes],
         ),
         compiler_params=pltpu.CompilerParams(vmem_limit_bytes=VMEM_BYTES),
-    )(scalars, places, front, source)
-    return outs if pieces else outs[0]
+    )(scalars, *inputs)
+    return outs[0] if tail is None else outs
 
 
 def halves(x):
@@ -143,16 +154,16 @@
 CROSS = ((1,), (1,))
 
 
-def factor_kernel(order, flags, gathered_ref, inverse_ref, first_ref, second_ref, fixed_ref):
+def factor_kernel(order, flags, gathered_ref, inverse_ref, corner_ref, first_ref, second_ref, fixed_ref):
     place, kept = flags[0], flags[1]
     thin = inverse_ref.shape[1]
     by_chip = lambda x: jnp.concatenate([x[:, 8 * q : 8 * q + 8].reshape(-1, x.shape[2]) for q in order])
     strip = gathered_ref[:, :thin].reshape(PANEL, 2 * PANEL)
-    corner = by_chip(gathered_ref[:, thin : 2 * thin])
     inverse = by_chip(inverse_ref[...])
     inverse0, inverse1 = inverse[:, :PANEL], inverse[:, PANEL:]
     halves0, halves1 = halves(inverse0), halves(inverse1)
-    corner10, corner01 = halves(corner[:, :PANEL]), halves(corner[:, PANEL:])
+    corner = corner_ref[...]
+    corner10, corner01 = (halves(corner[:, k].reshape(PANEL, PANEL)) for k in range(PANELS))
     first = product(halves(strip[:, :PANEL]), halves0, CROSS)
     lowered = product(halves(first), corner10, PLAIN)
     pivot1 = strip[:, PANEL:] - jnp.where(kept == 1, lowered, 0.0)
@@ -165,7 +176,7 @@
     fixed_ref[...] = fixed
 
 
-def factor(order, flags, gathered, inverse):
+def factor(order, flags, gathered, inverse, panels):
     square = jax.ShapeDtypeStruct((PANEL, PANEL), jnp.float32)
     return pl.pallas_call(
         functools.partial(factor_kernel, order),
@@ -173,11 +184,12 @@
         grid_spec=pltpu.PrefetchScalarGridSpec(
             num_scalar_prefetch=1,
             grid=(1,),
-            in_specs=[pl.BlockSpec(x.shape, lambda i, _: (0, 0, 0)) for x in (gathered, inverse)],
+            in_specs=[pl.BlockSpec(x.shape, lambda i, _: (0, 0, 0)) for x in (gathered, inverse)]
+            + [pl.BlockSpec(panels.shape[:3] + (PANEL,), lambda i, _: (0, 0, 0, panels.shape[3] // PANEL - 1))],
             out_specs=[pl.BlockSpec((PANEL, PANEL), lambda i, _: (0, 0))] * 3,
         ),
         compiler_params=pltpu.CompilerParams(vmem_limit_bytes=VMEM_BYTES),
-    )(flags, gathered, inverse)
+    )(flags, gathered, inverse, panels)
 
 
 def update_kernel(flags, *refs):
@@ -196,7 +208,7 @@
 
 
 def update(flags, parts, panels, first, second, fixed):
-    rows = panels.shape[3]
+    rows = parts[0].shape[2]
     square = pl.BlockSpec((PANEL, PANEL), lambda i, _: (0, 0))
     return pl.pallas_call(
         update_kernel,
@@ -287,53 +299,41 @@
     strip = strip_add(jnp.where(side == 0, base, got[:thin]), jnp.where(side == 0, got[:thin], prefix), 1)
     first_masks = jnp.where(side == 0, mask_rows, got[thin:])
 
+    strip, inverse = lax.optimization_barrier((strip, inverse))
+    gathered = lax.all_gather(jnp.concatenate([strip, first_masks]), "row", axis=0)
+    kept = gathered[0, thin, 1] > 0.5
+
+    corner = jnp.where(place == 0, strip[:, PANEL:], strip[:, :PANEL])
+    tail = jnp.concatenate([corner, jnp.broadcast_to(mask_rows[:1, :PANEL], (thin, PANEL))], axis=1)
     wholes, pieces = [], {}
-
-    def assemble(index):
-        a, b = parts[index]
+    for (a, b), part in zip(parts, received):
         size = b - a
-        whole, *chunk_list = add_other(
-            base_sum, received[index], offset=window_at, columns=size, part=a // size, pieces=size // 8
-        )
+        whole, *chunk_list = add_other(base_sum, part, offset=window_at, columns=size, part=a // size, tail=tail)
         wholes.append(whole)
         pieces.update({a // 8 + i: chunk for i, chunk in enumerate(chunk_list)})
 
-    assemble(0)
-    strip, wholes[0] = lax.optimization_barrier((strip, wholes[0]))
-
-    cols = lax.axis_size("col")
-    corner = jnp.where(place == 0, strip[:, PANEL:], strip[:, :PANEL])
-    corner = jnp.where(place < PANELS, jnp.concatenate([corner, mask_rows[:, :PANEL]]), 0.0)
-    reach = cols // 2
-    while reach >= PANELS:
-        pairs = [(c, c + reach) for c in range(cols) if c % (2 * reach) < PANELS]
-        corner = corner + lax.ppermute(corner, "col", pairs)
-        reach //= 2
-    corner, received[1], inverse = lax.optimization_barrier((corner, received[1], inverse))
-    other = lax.ppermute(corner, "col", [(c, c ^ 1) for c in range(cols)])
-    core0 = place % PANELS == 0
-    corner = jnp.concatenate([jnp.where(core0, corner, other), jnp.where(core0, other, corner)], axis=1)
-    cross_mask = corner[thin, PANEL : PANEL + tile_mask.shape[0]] > 0.5
-    gathered = lax.all_gather(jnp.concatenate([strip, corner[:thin], first_masks]), "row", axis=0)
-    kept = gathered[0, 2 * thin, 1] > 0.5
-
     across = lambda x: lax.all_to_all(x, "row", split_axis=0, concat_axis=0, tiled=True)
-    assemble(1)
     order = [0, 1] + list(range(chunks // 2, chunks)) + list(range(2, chunks // 2))
     mine = jnp.where(place // PANELS == 0, pieces[order[0]], 0.0)
     for chip in range(1, chunks):
         pairs = [(k, PANELS * chip + k) for k in range(PANELS)]
         mine = mine + lax.ppermute(pieces[order[chip]], "col", pairs)
+    tails = mine[:, :, row_count:]
+    core0 = place % PANELS == 0
+    masks_there = lax.ppermute(tails[PANEL // LANES], "col", [(c, c ^ 1) for c in range(lax.axis_size("col"))])
+    cross_mask = jnp.where(core0, masks_there, tails[PANEL // LANES])[0, : tile_mask.shape[0]] > 0.5
+    corner = tails[: PANEL // LANES].transpose(1, 0, 2).reshape(1, 8, PANEL)
+    mine = jnp.concatenate([mine[:, :, :row_count], jnp.broadcast_to(corner, (grid_rows, 8, PANEL))], axis=2)
     moved = [across(wholes[0])]
     mine, moved[0] = lax.optimization_barrier((mine, moved[0]))
     mine = across(mine)
-    panels = lax.all_gather(mine.reshape(thin, row_count), "col", axis=0, tiled=True)
-    panels = panels.reshape(chunks, PANELS, thin, row_count)
+    panels = lax.all_gather(mine.reshape(thin, -1), "col", axis=0, tiled=True)
+    panels = panels.reshape(chunks, PANELS, thin, -1)
     last, mine = lax.optimization_barrier((wholes[1], mine))
     moved.append(across(last))
 
     first, second, fixed = factor(
-        order, jnp.stack([place, kept.astype(place.dtype)]).astype(jnp.int32), gathered, inverse
+        order, jnp.stack([place, kept.astype(place.dtype)]).astype(jnp.int32), gathered, inverse, panels
     )
 
     tiles = row_count // PANEL

time: 260 us -> 228 us (0.88)
  waiting for transfers between devices: 119 us -> 92.2 us
  blocking collectives: 22.6 us -> 19 us
  starting transfers between devices: 28.5 us -> 25.8 us
    all_to_all x2, waiting for transfers between devices: 50.2 us -> 25.9 us  [local(): lax.all_to_all(x, 'row', split_axis=0, concat_axis=0, tiled=True)]
    ppermute x4 -> x1, waiting for transfers between devices: 16.9 us -> 1.12 us  [local(): lax.ppermute(tails[PANEL // LANES], 'col', [(c, c ^ 1) for c in range(lax...]
    ppermute x3, waiting for transfers between devices: 10 us -> 22.5 us  [local(): exchange = lambda x: lax.ppermute(x, 'subcube', [(0, 1), (1, 0)])]
    all_gather x2, waiting for transfers between devices: 31.6 us -> 42.5 us  [the longest x1 42.5 us: local(): panels = lax.all_gather(mine.reshape(thin, -1), 'col', axis=0, tiled=True)]
    ppermute x7, waiting for transfers between devices: 9.76 us -> 0.02 us  [local(): mine = mine + lax.ppermute(pieces[order[chip]], 'col', pairs)]
    all_to_all x1, blocking collectives: 22.6 us -> 19 us  [local(): lax.all_to_all(x, 'row', split_axis=0, concat_axis=0, tiled=True)]
    ppermute x4 -> x1, starting transfers between devices: 2.75 us -> 0.09 us  [local(): lax.ppermute(tails[PANEL // LANES], 'col', [(c, c ^ 1) for c in range(lax...]
  transfers between devices with their start and end apart: 19 -> 16, of which waited for: 8 -> 5; matrix products, arithmetic and copies ran while one was open for 8% -> 9% of each run, Pallas kernels for 14% -> 16%
where the time goes in v6:
time: 228 us; the launch traced here: 226 us
  waiting for transfers between devices  92.2 us (40%)
  Pallas kernels  47.4 us (21%)
  starting transfers between devices  25.8 us (11%)
  blocking collectives  19 us (8%)
  other arithmetic  17.4 us (8%)
  between operations  15.4 us (7%)
  local copies, waits for them, and re-layouts  8.7 us (4%)
    all_gather x1, waiting for transfers between devices, local(): panels = lax.all_gather(mine.reshape(thin, -1), 'col', axis=0, tiled=True)  42.5 us
    all_to_all x2, waiting for transfers between devices, local(): lax.all_to_all(x, 'row', split_axis=0, concat_axis=0, tiled=True)  25.9 us
    ppermute x3, waiting for transfers between devices, local(): exchange = lambda x: lax.ppermute(x, 'subcube', [(0, 1), (1, 0)])  22.5 us
    pallas_call x5, Pallas kernels, extend_add(): pl.pallas_call(functools.partial(extend_kernel, first_place, map_blocks),...  20.3 us
    all_to_all x1, blocking collectives, local(): lax.all_to_all(x, 'row', split_axis=0, concat_axis=0, tiled=True)  19 us
    all_to_all x2, starting transfers between devices, local(): lax.all_to_all(x, 'row', split_axis=0, concat_axis=0, tiled=True)  12.1 us
    pallas_call x1, Pallas kernels, update(): pl.pallas_call(update_kernel, out_shape=jax.ShapeDtypeStruct((rows, PANEL...  10.9 us
    pallas_call x1, Pallas kernels, factor(): pl.pallas_call(functools.partial(factor_kernel, order), out_shape=(square...  8.98 us
  transfers between devices with their start and end apart: 16, of which 5 were waited for; matrix products, arithmetic and copies ran while one was open for 9% of the time, Pallas kernels for 16%

profile of v6, /device:TPU:10, one launch (start us, length us, event | category | flops | bytes accessed | tf_op | source)
XLA Modules:
  0.0 225.9 jit_solution(6079053305100323839)
XLA Ops:
  6.5 1.0 slice_bitcast_fusion.1
  7.5 0.7 pad_maximum_fusion.3
  9.0 1.2 convert_reduce_fusion.1
  10.2 1.5 copy.10
  11.7 0.7 pad_add_fusion.2
  13.0 2.9 %shard_map.56.places_ref = s32[16,128]{1,0:T(8,128)} custom-call(s32[20]{0:T(128)} %concatenate.42.scalars, s32[2,96,128]{2,1,0:T(8,128)} %bitcast.67), custom_call_target="tpu_custom_call" | custom-call | tf_op jit(solution)/shard_map/pallas_call | solution.py:53
  15.9 2.8 %shard_map.57 = f32[1,64,1024]{2,1,0:T(8,128)} custom-call(s32[9]{0:T(128)} %get-tuple-element.105.scalars, s32[16,128]{1,0:T(8,128)} %shard_map.56.places_ref, f32[64,12288]{1,0:T(8,128)} %bitcast.58, f32[64,12288]{1,0:T(8,128)} %bitcast.50), custom_call_target="tpu_custom_call" | custom-call | tf_op jit(solution)/shard_map/pallas_call | solution.py:127
  18.8 1.0 bitcast_select_fusion.1
  19.8 0.7 pad_maximum_fusion.1
  20.5 2.3 %collective-permute-start.1 = (f32[72,1024]{1,0:T(8,128)}, f32[72,1024]{1,0:T(8,128)}, u32[]{:S(2)}, u32[]{:S(2)}) collective-permute-start(f32[72,1024]{1,0:T(8,128)} %pad_maximum_fusion.1), channel_id=1, source_target_pairs={{0,128},{128,0},{1,129},{129,1},{2,130},{130,2},{3,131},{131,3},{4... | collective-permute-start | bytes 884744 | tf_op jit(solution)/shard_map/ppermute | solution.py:245
  22.8 1.4 slice_select_fusion.1
  24.2 1.2 collective-permute-start.2
  27.9 1.1 convert_reduce_fusion
  29.0 0.7 concatenate.40.scalars
  29.7 4.3 %shard_map.55.places_ref = s32[192,128]{1,0:T(8,128)S(1)} custom-call(s32[196]{0:T(256)} %concatenate.40.scalars, s32[2,96,128]{2,1,0:T(8,128)} %bitcast.68), custom_call_target="tpu_custom_call" | custom-call | tf_op jit(solution)/shard_map/pallas_call | solution.py:53
  33.9 0.7 pad_add_fusion.5.scalars
  34.6 4.8 %shard_map.58 = f32[8,64,1536]{2,1,0:T(8,128)} custom-call(s32[97]{0:T(128)} %pad_add_fusion.5.scalars, s32[192,128]{1,0:T(8,128)S(1)} %shard_map.55.places_ref, f32[64,12288]{1,0:T(8,128)} %bitcast.59, f32[64,12288]{1,0:T(8,128)S(1)} %bitcast.53), custom_call_target="tpu_custom_call" | custom-call | tf_op jit(solution)/shard_map/pallas_call | solution.py:127
  39.5 0.7 pad_add_fusion.4.scalars
  40.2 9.2 %collective-permute-done.2.source_ref = f32[32,6656]{1,0:T(8,128)} collective-permute-done((f32[32,6656]{1,0:T(8,128)}, f32[32,6656]{1,0:T(8,128)}, u32[]{:S(2)}, u32[]{:S(2)}) %collective-permute-start.2) | collective-permute-done | bytes 852000 | tf_op jit(solution)/shard_map/ppermute | solution.py:245
  49.3 1.8 slice_select_fusion.3
  51.2 2.6 %shard_map.59 = f32[1,64,1024]{2,1,0:T(8,128)} custom-call(s32[9]{0:T(128)} %get-tuple-element.104.scalars, s32[16,128]{1,0:T(8,128)} %shard_map.56.places_ref, f32[64,1024]{1,0:T(8,128)} %get-tuple-element.91.front_ref, f32[64,1024]{1,0:T(8,128)} %get-tuple-element.90.source_ref), custom_call_target="tpu_custom_call" | custom-call | tf_op jit(solution)/shard_map/pallas_call | solution.py:127
  53.8 0.8 slice_select_fusion.5
  54.5 1.7 pad_maximum_fusion.2
  56.2 1.0 slice_select_fusion.4
  57.2 0.7 pad_maximum_fusion.4.refs_0_
  58.0 5.3 %shard_map.61 = (f32[8,32,1536]{2,1,0:T(8,128)}, f32[8,8,1664]{2,1,0:T(8,128)}, f32[8,8,1664]{2,1,0:T(8,128)}, f32[8,8,1664]{2,1,0:T(8,128)}, f32[8,8,1664]{2,1,0:T(8,128)}) custom-call(s32[97]{0:T(128)} %pad_add_fusion.4.scalars, s32[192,128]{1,0:T(8,128)S(1)} %shard_map.55.places_ref, f32[8,64,1536]{2,1,0:T(8,128)} %get-tuple-element.106.front_ref, ...), custom_call_target="tpu_custom_call" | custom-call | tf_op jit(solution)/shard_map/pallas_call | solution.py:127
  63.2 8.5 %all-to-all-start = ((f32[8,32,1536]{2,1,0:T(8,128)}), f32[8,32,1536]{2,1,0:T(8,128)}, u32[]{:S(2)}, u32[]{:S(2)}) async-start(f32[8,32,1536]{2,1,0:T(8,128)} %get-tuple-element.80), calls=%async_computation | async-start | bytes 3145728 | tf_op jit(solution)/shard_map/all_to_all | solution.py:315
  71.7 2.4 %collective-permute-start.3 = (f32[32,6656]{1,0:T(8,128)}, f32[32,6656]{1,0:T(8,128)S(1)}, u32[]{:S(2)}, u32[]{:S(2)}) collective-permute-start(f32[32,6656]{1,0:T(8,128)} %get-tuple-element.67), channel_id=1, source_target_pairs={{0,128},{128,0},{1,129},{129,1},{2,130},{130,2},{3,131},{131,3},{4... | collective-permute-start | bytes 2555912 | tf_op jit(solution)/shard_map/ppermute | solution.py:245
  74.1 1.4 collective-permute-start.5
  75.6 1.3 collective-permute-start.6
  76.8 1.5 collective-permute-start.7
  78.3 1.4 collective-permute-start.8
  79.7 13.4 %collective-permute-done.3.source_ref = f32[32,6656]{1,0:T(8,128)S(1)} collective-permute-done((f32[32,6656]{1,0:T(8,128)}, f32[32,6656]{1,0:T(8,128)S(1)}, u32[]{:S(2)}, u32[]{:S(2)}) %collective-permute-start.3) | collective-permute-done | bytes 852000 | tf_op jit(solution)/shard_map/ppermute | solution.py:245
  93.1 0.9 copy-done.6
  94.0 4.8 %shard_map.60 = (f32[8,32,1536]{2,1,0:T(8,128)}, f32[8,8,1664]{2,1,0:T(8,128)}, f32[8,8,1664]{2,1,0:T(8,128)}, f32[8,8,1664]{2,1,0:T(8,128)}, f32[8,8,1664]{2,1,0:T(8,128)}) custom-call(s32[97]{0:T(128)} %pad_add_fusion.4.scalars, s32[192,128]{1,0:T(8,128)S(1)} %shard_map.55.places_ref, f32[8,64,1536]{2,1,0:T(8,128)S(1)} %copy-done.2, f32[32,6656]{1,0:T(8,128)} %copy-done.6, ...), custom_call_target="tpu_custom_call" | custom-call | tf_op jit(solution)/shard_map/pallas_call | solution.py:127
  98.7 0.7 collective-permute-start.4
  99.4 0.7 collective-permute-start.9
  100.1 0.7 collective-permute-start.10
  100.9 1.6 add_add_fusion
  102.6 25.9 %all-to-all-done.refs_1_ = f32[8,32,1536]{2,1,0:T(8,128)} async-done(((f32[8,32,1536]{2,1,0:T(8,128)}), f32[8,32,1536]{2,1,0:T(8,128)}, u32[]{:S(2)}, u32[]{:S(2)}) %all-to-all-start) | async-done | bytes 1572896 | tf_op jit(solution)/shard_map/all_to_all | solution.py:315
  128.5 19.0 %all_to_all.15 = f32[8,8,2048]{2,1,0:T(8,128)} all-to-all(f32[8,8,2048]{2,1,0:T(8,128)S(1)} %pad_maximum_fusion), channel_id=1, replica_groups=mesh['subcube'=2,'row'=8,'col'=16] {'row'}, dimensions={0} | all-to-all | bytes 1048576 | tf_op jit(solution)/shard_map/all_to_all | solution.py:315
  147.6 3.6 %all-to-all-start.2 = ((f32[8,32,1536]{2,1,0:T(8,128)}), f32[8,32,1536]{2,1,0:T(8,128)S(1)}, u32[]{:S(2)}, u32[]{:S(2)}) async-start(f32[8,32,1536]{2,1,0:T(8,128)} %get-tuple-element.82), calls=%async_computation.2 | async-start | bytes 3145728 | tf_op jit(solution)/shard_map/all_to_all | solution.py:315
  151.4 1.1 collective-permute-done.11
  153.2 1.3 slice.135
  155.7 42.5 %all-gather.6.cloned.1.call-done = f32[1024,2048]{1,0:T(8,128)} async-done(((f32[64,2048]{1,0:T(8,128)}), f32[1024,2048]{1,0:T(8,128)}) %all-gather.6.cloned.1.call-update) | async-done | bytes 8388624 | tf_op jit(solution)/shard_map/all_gather | solution.py:330
  198.3 9.0 %shard_map.62 = (f32[512,512]{1,0:T(8,128)}, f32[512,512]{1,0:T(8,128)}, f32[512,512]{1,0:T(8,128)}) custom-call(s32[2]{0:T(128)} %pad_add_fusion.6.flags, f32[8,72,1024]{2,1,0:T(8,128)} %bitcast.61, f32[8,64,1024]{2,1,0:T(8,128)} %bitcast.64, f32[8,2,64,2048]{3,2,1,0:T(8,128)} %bitcast.56), custom_call_target="tpu_custom_call" | custom-call | tf_op jit(solution)/shard_map/pallas_call | solution.py:181
  207.2 1.2 copy-done.3
  208.4 10.9 %shard_map.63 = f32[1536,512]{1,0:T(8,128)} custom-call(s32[12]{0:T(128)} %reshape.127.flags, f32[8,32,1536]{2,1,0:T(8,128)} %copy-done.3, f32[8,32,1536]{2,1,0:T(8,128)} %all-to-all-done.refs_1_, f32[8,2,64,2048]{3,2,1,0:T(8,128)} %bitcast.57, f32[512,512]{1,0:T(8,128)} %get-tuple-element.85.refs_3_, f32[512,512]{1,0:T(8,128)} %get-tuple-element.86.refs_4_, ...), custom_call_target="tpu_custom_call" | custom-call | tf_op jit(solution)/shard_map/pallas_call | solution.py:213
  (58 shorter events, 4.1 us)
Async XLA Ops:
  6.5 48.0 %all-gather.8.cloned.1.call-start = ((), (), s32[]{:S(2)}) async-start(), calls=%async_computation.4 | async-start | bytes 2359296 | tf_op jit(solution)/shard_map/all_gather | solution.py:247
  8.3 144.9 %all-gather.10.cloned.1.call-start = ((), (), s32[]{:S(2)}) async-start(), calls=%async_computation.5 | async-start | bytes 2654208 | tf_op jit(solution)/shard_map/all_gather | solution.py:303
  15.9 2.9 %copy-start = (f32[1,1,1,64,12288]{4,3,2,1,0:T(8,128)S(1)}, f32[1,1,1,64,12288]{4,3,2,1,0:T(8,128)}, u32[]{:S(2)}) copy-start(f32[1,1,1,64,12288]{4,3,2,1,0:T(8,128)} %param.10) | copy-start | bytes 9437188
  18.8 6.7 %copy-start.5 = (s32[2,12288]{1,0:T(2,128)S(1)}, s32[2,12288]{1,0:T(2,128)}, u32[]{:S(2)}) copy-start(s32[2,12288]{1,0:T(2,128)} %param.11) | copy-start | bytes 294916
  20.5 28.8 %collective-permute-start.1 = (f32[72,1024]{1,0:T(8,128)}, f32[72,1024]{1,0:T(8,128)}, u32[]{:S(2)}, u32[]{:S(2)}) collective-permute-start(f32[72,1024]{1,0:T(8,128)} %pad_maximum_fusion.1), channel_id=1, source_target_pairs={{0,128},{128,0},{1,129},{129,1},{2,130},{130,2},{3,131},{131,3},{4... | collective-permute-start | bytes 884744 | tf_op jit(solution)/shard_map/ppermute | solution.py:245
  24.2 25.1 %collective-permute-start.2 = (f32[32,6656]{1,0:T(8,128)}, f32[32,6656]{1,0:T(8,128)}, u32[]{:S(2)}, u32[]{:S(2)}) collective-permute-start(f32[32,6656]{1,0:T(8,128)} %get-tuple-element.88), channel_id=1, source_target_pairs={{0,128},{128,0},{1,129},{129,1},{2,130},{130,2},{3,131},{131,3},{4... | collective-permute-start | bytes 2555912 | tf_op jit(solution)/shard_map/ppermute | solution.py:245
  39.5 9.9 %copy-start.4 = (f32[1,64,1024]{2,1,0:T(8,128)S(1)}, f32[1,64,1024]{2,1,0:T(8,128)}, u32[]{:S(2)}) copy-start(f32[1,64,1024]{2,1,0:T(8,128)} %shard_map.57) | copy-start | bytes 786436
  58.0 36.0 %copy-start.2 = (f32[8,64,1536]{2,1,0:T(8,128)S(1)}, f32[8,64,1536]{2,1,0:T(8,128)}, u32[]{:S(2)}) copy-start(f32[8,64,1536]{2,1,0:T(8,128)} %get-tuple-element.106.front_ref) | copy-start | bytes 9437188
  63.2 65.3 %all-to-all-start = ((f32[8,32,1536]{2,1,0:T(8,128)}), f32[8,32,1536]{2,1,0:T(8,128)}, u32[]{:S(2)}, u32[]{:S(2)}) async-start(f32[8,32,1536]{2,1,0:T(8,128)} %get-tuple-element.80), calls=%async_computation | async-start | bytes 3145728 | tf_op jit(solution)/shard_map/all_to_all | solution.py:315
  71.7 126.6 %all-gather.6.cloned.1.call-start = ((), (), s32[]{:S(2)}) async-start(), calls=%async_computation.3 | async-start | bytes 8912896 | tf_op jit(solution)/shard_map/all_gather | solution.py:330
  71.7 21.3 %collective-permute-start.3 = (f32[32,6656]{1,0:T(8,128)}, f32[32,6656]{1,0:T(8,128)S(1)}, u32[]{:S(2)}, u32[]{:S(2)}) collective-permute-start(f32[32,6656]{1,0:T(8,128)} %get-tuple-element.67), channel_id=1, source_target_pairs={{0,128},{128,0},{1,129},{129,1},{2,130},{130,2},{3,131},{131,3},{4... | collective-permute-start | bytes 2555912 | tf_op jit(solution)/shard_map/ppermute | solution.py:245
  74.1 25.3 %collective-permute-start.5 = (f32[8,8,1664]{2,1,0:T(8,128)}, f32[8,8,1664]{2,1,0:T(8,128)}, u32[]{:S(2)}, u32[]{:S(2)}) collective-permute-start(f32[8,8,1664]{2,1,0:T(8,128)} %get-tuple-element.73), channel_id=1, source_target_pairs={{0,4},{1,5},{16,20},{17,21},{32,36},{33,37},{48,52},{49,53},{64,68... | collective-permute-start | bytes 1277960 | tf_op jit(solution)/shard_map/ppermute | solution.py:320
  75.6 24.6 %collective-permute-start.6 = (f32[8,8,1664]{2,1,0:T(8,128)}, f32[8,8,1664]{2,1,0:T(8,128)}, u32[]{:S(2)}, u32[]{:S(2)}) collective-permute-start(f32[8,8,1664]{2,1,0:T(8,128)} %get-tuple-element.74), channel_id=1, source_target_pairs={{0,6},{1,7},{16,22},{17,23},{32,38},{33,39},{48,54},{49,55},{64,70... | collective-permute-start | bytes 1277960 | tf_op jit(solution)/shard_map/ppermute | solution.py:320
  76.8 24.0 %collective-permute-start.7 = (f32[8,8,1664]{2,1,0:T(8,128)}, f32[8,8,1664]{2,1,0:T(8,128)}, u32[]{:S(2)}, u32[]{:S(2)}) collective-permute-start(f32[8,8,1664]{2,1,0:T(8,128)} %get-tuple-element.75), channel_id=1, source_target_pairs={{0,8},{1,9},{16,24},{17,25},{32,40},{33,41},{48,56},{49,57},{64,72... | collective-permute-start | bytes 1277960 | tf_op jit(solution)/shard_map/ppermute | solution.py:320
  78.3 22.6 %collective-permute-start.8 = (f32[8,8,1664]{2,1,0:T(8,128)}, f32[8,8,1664]{2,1,0:T(8,128)}, u32[]{:S(2)}, u32[]{:S(2)}) collective-permute-start(f32[8,8,1664]{2,1,0:T(8,128)} %get-tuple-element.76), channel_id=1, source_target_pairs={{0,10},{1,11},{16,26},{17,27},{32,42},{33,43},{48,58},{49,59},{64,... | collective-permute-start | bytes 1277960 | tf_op jit(solution)/shard_map/ppermute | solution.py:320
  93.1 0.9 copy-start.6
  98.7 2.1 collective-permute-start.4
  99.4 1.5 collective-permute-start.9
  100.1 0.8 collective-permute-start.10
  102.5 48.7 %copy-start.7 = (s32[3,1]{0,1:T(1,128)S(1)}, s32[3,1]{0,1:T(1,128)}, u32[]{:S(2)}) copy-start(s32[3,1]{0,1:T(1,128)} %param.13) | copy-start | bytes 40
  147.6 59.7 %all-to-all-start.2 = ((f32[8,32,1536]{2,1,0:T(8,128)}), f32[8,32,1536]{2,1,0:T(8,128)S(1)}, u32[]{:S(2)}, u32[]{:S(2)}) async-start(f32[8,32,1536]{2,1,0:T(8,128)} %get-tuple-element.82), calls=%async_computation.2 | async-start | bytes 3145728 | tf_op jit(solution)/shard_map/all_to_all | solution.py:315
  151.2 1.3 collective-permute-start.11
  207.2 1.2 copy-start.3
Sparse Core Ops, SparseCore 0:
  9.1 44.1 all-gather.7
  56.4 74.5 all-gather.9
  147.7 50.5 all-gather.5

commit v7 on v6

--- a/solution.py
+++ b/solution.py
@@ -156,11 +156,10 @@
 
 def factor_kernel(order, flags, gathered_ref, inverse_ref, corner_ref, first_ref, second_ref, fixed_ref):
     place, kept = flags[0], flags[1]
-    thin = inverse_ref.shape[1]
+    thin = inverse_ref.shape[2]
     by_chip = lambda x: jnp.concatenate([x[:, 8 * q : 8 * q + 8].reshape(-1, x.shape[2]) for q in order])
     strip = gathered_ref[:, :thin].reshape(PANEL, 2 * PANEL)
-    inverse = by_chip(inverse_ref[...])
-    inverse0, inverse1 = inverse[:, :PANEL], inverse[:, PANEL:]
+    inverse0, inverse1 = (by_chip(inverse_ref[:, k]) for k in range(PANELS))
     halves0, halves1 = halves(inverse0), halves(inverse1)
     corner = corner_ref[...]
     corner10, corner01 = (halves(corner[:, k].reshape(PANEL, PANEL)) for k in range(PANELS))
@@ -184,7 +183,10 @@
         grid_spec=pltpu.PrefetchScalarGridSpec(
             num_scalar_prefetch=1,
             grid=(1,),
-            in_specs=[pl.BlockSpec(x.shape, lambda i, _: (0, 0, 0)) for x in (gathered, inverse)]
+            in_specs=[
+                pl.BlockSpec(gathered.shape, lambda i, _: (0, 0, 0)),
+                pl.BlockSpec(inverse.shape, lambda i, _: (0, 0, 0, 0)),
+            ]
             + [pl.BlockSpec(panels.shape[:3] + (PANEL,), lambda i, _: (0, 0, 0, panels.shape[3] // PANEL - 1))],
             out_specs=[pl.BlockSpec((PANEL, PANEL), lambda i, _: (0, 0))] * 3,
         ),
@@ -192,9 +194,9 @@
     )(flags, gathered, inverse, panels)
 
 
-def update_kernel(flags, *refs):
-    part_refs, (panels_ref, first_ref, second_ref, fixed_ref, out_ref) = refs[:-5], refs[-5:]
-    tile = pl.program_id(0)
+def update_kernel(first_tile, flags, *refs):
+    part_refs, (panels_ref, first_ref, second_ref, fixed_ref), out_ref = refs[:2], refs[2:6], refs[-1]
+    tile = first_tile + pl.program_id(0)
     keep, use_first, use_fixed, use_second = (flags[4 * tile + i] == 1 for i in range(4))
     left0 = first_ref[...] - jnp.where(use_fixed, fixed_ref[...], 0.0)
     left0 = halves(jnp.where(use_first, left0, 0.0))
@@ -207,26 +209,29 @@
     out_ref[...] = (jnp.where(keep, block, 0.0) - update).T
 
 
-def update(flags, parts, panels, first, second, fixed):
+def update(flags, parts, panels, squares, first_tile, tiles, earlier=None):
     rows = parts[0].shape[2]
     square = pl.BlockSpec((PANEL, PANEL), lambda i, _: (0, 0))
+    inputs = [*parts, panels, *squares]
+    in_specs = [pl.BlockSpec(part.shape[:2] + (PANEL,), lambda i, _: (0, 0, first_tile + i)) for part in parts]
+    in_specs += [pl.BlockSpec(panels.shape[:3] + (PANEL,), lambda i, _: (0, 0, 0, i)), square, square, square]
+    aliases = {}
+    if earlier is not None:
+        inputs.append(earlier)
+        in_specs.append(pl.BlockSpec(memory_space=pl.ANY))
+        aliases = {len(inputs): 0}
     return pl.pallas_call(
-        update_kernel,
+        functools.partial(update_kernel, first_tile),
         out_shape=jax.ShapeDtypeStruct((rows, PANEL), jnp.float32),
         grid_spec=pltpu.PrefetchScalarGridSpec(
             num_scalar_prefetch=1,
-            grid=(rows // PANEL,),
-            in_specs=[pl.BlockSpec(part.shape[:2] + (PANEL,), lambda i, _: (0, 0, i)) for part in parts]
-            + [
-                pl.BlockSpec(panels.shape[:3] + (PANEL,), lambda i, _: (0, 0, 0, i)),
-                square,
-                square,
-                square,
-            ],
-            out_specs=pl.BlockSpec((PANEL, PANEL), lambda i, _: (i, 0)),
-        ),
+            grid=(tiles,),
+            in_specs=in_specs,
+            out_specs=pl.BlockSpec((PANEL, PANEL), lambda i, _: (first_tile + i, 0)),
+        ),
+        input_output_aliases=aliases,
         compiler_params=pltpu.CompilerParams(vmem_limit_bytes=VMEM_BYTES),
-    )(flags, *parts, panels, first, second, fixed)
+    )(flags, *inputs)
 
 
 def local(front_entries, child_blocks, row_maps, pivot_inverses, tile_mask):
@@ -244,15 +249,13 @@
     zero = jnp.zeros((), jnp.int32)
     exchange = lambda x: lax.ppermute(x, "subcube", [(0, 1), (1, 0)])
 
-    inverse = lax.all_gather(jnp.concatenate([pivot_inverses[k] for k in range(PANELS)], axis=1), "row", axis=0)
+    inverse = lax.all_gather(pivot_inverses, "row", axis=0)
 
     window = -(-(child_rows * 13 // 24) // LANES) * LANES
     rest = child_rows - window
     parts = [(thin // 2, thin), (0, thin // 2)]
     first_sent, last_sent = [jnp.where(side == 0, own[a:b, rest:], own[a:b, :window]) for a, b in parts]
     received = [exchange(first_sent)]
-    last_sent, received[0] = lax.optimization_barrier((last_sent, received[0]))
-    received.append(exchange(last_sent))
 
     map_blocks = child_rows // LANES
     blocks = half_rows // LANES
@@ -295,22 +298,33 @@
 
     base_sum = lax.cond(spill, add_rest, lambda x: x, base_sum)
 
-    got, received[0], base_sum = lax.optimization_barrier((got, received[0], base_sum))
+    got, received[0], base_sum, last_sent = lax.optimization_barrier((got, received[0], base_sum, last_sent))
+    received.append(exchange(last_sent))
     strip = strip_add(jnp.where(side == 0, base, got[:thin]), jnp.where(side == 0, got[:thin], prefix), 1)
     first_masks = jnp.where(side == 0, mask_rows, got[thin:])
-
-    strip, inverse = lax.optimization_barrier((strip, inverse))
-    gathered = lax.all_gather(jnp.concatenate([strip, first_masks]), "row", axis=0)
-    kept = gathered[0, thin, 1] > 0.5
 
     corner = jnp.where(place == 0, strip[:, PANEL:], strip[:, :PANEL])
     tail = jnp.concatenate([corner, jnp.broadcast_to(mask_rows[:1, :PANEL], (thin, PANEL))], axis=1)
     wholes, pieces = [], {}
-    for (a, b), part in zip(parts, received):
+
+    def assemble(index):
+        a, b = parts[index]
         size = b - a
-        whole, *chunk_list = add_other(base_sum, part, offset=window_at, columns=size, part=a // size, tail=tail)
+        whole, *chunk_list = add_other(
+            base_sum, received[index], offset=window_at, columns=size, part=a // size, tail=tail
+        )
         wholes.append(whole)
         pieces.update({a // 8 + i: chunk for i, chunk in enumerate(chunk_list)})
+
+    assemble(0)
+    to_gather = jnp.concatenate([strip, first_masks])
+    to_gather, inverse, received[1], wholes[0] = lax.optimization_barrier(
+        (to_gather, inverse, received[1], wholes[0])
+    )
+    gathered = lax.all_gather(to_gather, "row", axis=0)
+    kept = gathered[0, thin, 1] > 0.5
+
+    assemble(1)
 
     across = lambda x: lax.all_to_all(x, "row", split_axis=0, concat_axis=0, tiled=True)
     order = [0, 1] + list(range(chunks // 2, chunks)) + list(range(2, chunks // 2))
@@ -323,12 +337,16 @@
     masks_there = lax.ppermute(tails[PANEL // LANES], "col", [(c, c ^ 1) for c in range(lax.axis_size("col"))])
     cross_mask = jnp.where(core0, masks_there, tails[PANEL // LANES])[0, : tile_mask.shape[0]] > 0.5
     corner = tails[: PANEL // LANES].transpose(1, 0, 2).reshape(1, 8, PANEL)
-    mine = jnp.concatenate([mine[:, :, :row_count], jnp.broadcast_to(corner, (grid_rows, 8, PANEL))], axis=2)
+    corner = jnp.broadcast_to(corner, (grid_rows, 8, PANEL))
+    cut = row_count - PANEL
+    mine = jnp.concatenate([mine[:, :, :cut], corner, mine[:, :, cut:row_count]], axis=2)
     moved = [across(wholes[0])]
     mine, moved[0] = lax.optimization_barrier((mine, moved[0]))
     mine = across(mine)
-    panels = lax.all_gather(mine.reshape(thin, -1), "col", axis=0, tiled=True)
-    panels = panels.reshape(chunks, PANELS, thin, -1)
+    mine_flat = mine.reshape(thin, -1)
+    gather_panels = lambda x: lax.all_gather(x, "col", axis=0, tiled=True).reshape(chunks, PANELS, thin, -1)
+    panels = gather_panels(mine_flat[:, :row_count])
+    last_panels = gather_panels(mine_flat[:, row_count:])
     last, mine = lax.optimization_barrier((wholes[1], mine))
     moved.append(across(last))
 
@@ -345,7 +363,9 @@
     use_fixed = jnp.where(is0, False, cross_mask & (tile_ids >= jnp.where(is1, 1, 2)))
     use_second = jnp.where(is0, False, jnp.where(is1, tile_ids >= 1, own_mask & (tile_ids >= 2)))
     flags = jnp.stack([keep, use_first, use_fixed, use_second], axis=1).astype(jnp.int32).reshape(-1)
-    return update(flags, moved[::-1], panels, first, second, fixed)
+    squares = [first, second, fixed]
+    begun = update(flags, moved[::-1], panels, squares, 0, tiles - 1)
+    return update(flags, moved[::-1], last_panels, squares, tiles - 1, 1, begun)
 
 
 def solution(mesh):

time: 228 us -> 248 us (1.088)
  waiting for transfers between devices: 92.2 us -> 108 us
  Pallas kernels: 47.4 us -> 51.4 us
    ppermute x7, waiting for transfers between devices: 0.02 us -> 12.3 us  [local(): mine = mine + lax.ppermute(pieces[order[chip]], 'col', pairs)]
    all_gather x3 -> x4, waiting for transfers between devices: 42.5 us -> 52.7 us  [the longest x2 52.7 us: local(): lax.all_gather(x, 'col', axis=0, tiled=True)]
    ppermute x3, waiting for transfers between devices: 22.5 us -> 15.5 us  [local(): exchange = lambda x: lax.ppermute(x, 'subcube', [(0, 1), (1, 0)])]
    pallas_call x1 -> x2, Pallas kernels: 10.9 us -> 15.1 us  [update(): pl.pallas_call(functools.partial(update_kernel, first_tile), out_shape=ja...]
  transfers between devices with their start and end apart: 16 -> 17, of which waited for: 5 -> 7; matrix products, arithmetic and copies ran while one was open for 9% -> 9% of each run, Pallas kernels for 16% -> 18%
where the time goes in v7:
time: 248 us; the launch traced here: 245 us
  waiting for transfers between devices  108 us (44%)
  Pallas kernels  51.4 us (21%)
  starting transfers between devices  25.7 us (10%)
  blocking collectives  19.9 us (8%)
  other arithmetic  16 us (6%)
  between operations  15.5 us (6%)
  local copies, waits for them, and re-layouts  8.36 us (3%)
    all_gather x2, waiting for transfers between devices, local(): lax.all_gather(x, 'col', axis=0, tiled=True)  52.7 us
    all_to_all x2, waiting for transfers between devices, local(): lax.all_to_all(x, 'row', split_axis=0, concat_axis=0, tiled=True)  25.5 us
    pallas_call x5, Pallas kernels, extend_add(): pl.pallas_call(functools.partial(extend_kernel, first_place, map_blocks),...  20.2 us
    all_to_all x1, blocking collectives, local(): lax.all_to_all(x, 'row', split_axis=0, concat_axis=0, tiled=True)  19.9 us
    ppermute x3, waiting for transfers between devices, local(): exchange = lambda x: lax.ppermute(x, 'subcube', [(0, 1), (1, 0)])  15.5 us
    pallas_call x2, Pallas kernels, update(): pl.pallas_call(functools.partial(update_kernel, first_tile), out_shape=ja...  15.1 us
    ppermute x7, waiting for transfers between devices, local(): mine = mine + lax.ppermute(pieces[order[chip]], 'col', pairs)  12.3 us
    all_to_all x2, starting transfers between devices, local(): lax.all_to_all(x, 'row', split_axis=0, concat_axis=0, tiled=True)  12.1 us
  transfers between devices with their start and end apart: 17, of which 7 were waited for; matrix products, arithmetic and copies ran while one was open for 9% of the time, Pallas kernels for 18%

profile of v7, /device:TPU:10, one launch (start us, length us, event | category | flops | bytes accessed | tf_op | source)
XLA Modules:
  0.0 244.6 jit_solution(3965975365044031390)
XLA Ops:
  6.5 0.7 all-gather.11.cloned.1.call-update
  8.0 1.2 convert_reduce_fusion.1
  9.2 1.5 copy.12
  12.1 2.9 %shard_map.56.places_ref = s32[16,128]{1,0:T(8,128)} custom-call(s32[20]{0:T(128)} %concatenate.39.scalars, s32[2,96,128]{2,1,0:T(8,128)} %bitcast.66), custom_call_target="tpu_custom_call" | custom-call | tf_op jit(solution)/shard_map/pallas_call | solution.py:53
  14.9 2.9 %shard_map.57 = f32[1,64,1024]{2,1,0:T(8,128)} custom-call(s32[9]{0:T(128)} %pad_add_fusion.3.scalars, s32[16,128]{1,0:T(8,128)} %shard_map.56.places_ref, f32[64,12288]{1,0:T(8,128)} %bitcast.55, f32[64,12288]{1,0:T(8,128)} %bitcast.47), custom_call_target="tpu_custom_call" | custom-call | tf_op jit(solution)/shard_map/pallas_call | solution.py:127
  17.8 1.0 bitcast_select_fusion.1
  18.8 0.7 pad_maximum_fusion.1
  19.5 2.3 collective-permute-start.1
  21.8 1.5 slice_select_fusion.1
  23.3 1.2 collective-permute-start.2
  27.0 1.1 convert_reduce_fusion
  28.1 0.7 concatenate.37.scalars
  28.8 4.3 %shard_map.55.places_ref = s32[192,128]{1,0:T(8,128)S(1)} custom-call(s32[196]{0:T(256)} %concatenate.37.scalars, s32[2,96,128]{2,1,0:T(8,128)} %bitcast.67), custom_call_target="tpu_custom_call" | custom-call | tf_op jit(solution)/shard_map/pallas_call | solution.py:53
  33.1 0.7 pad_add_fusion.4
  33.8 4.8 %shard_map.58 = f32[8,64,1536]{2,1,0:T(8,128)} custom-call(s32[97]{0:T(128)} %get-tuple-element.105.scalars, s32[192,128]{1,0:T(8,128)S(1)} %shard_map.55.places_ref, f32[64,12288]{1,0:T(8,128)} %bitcast.56, f32[64,12288]{1,0:T(8,128)S(1)} %bitcast.50), custom_call_target="tpu_custom_call" | custom-call | tf_op jit(solution)/shard_map/pallas_call | solution.py:127
  39.3 9.1 %collective-permute-done.2.source_ref = f32[32,6656]{1,0:T(8,128)} collective-permute-done((f32[32,6656]{1,0:T(8,128)}, f32[32,6656]{1,0:T(8,128)}, u32[]{:S(2)}, u32[]{:S(2)}) %collective-permute-start.2) | collective-permute-done | bytes 852000 | tf_op jit(solution)/shard_map/ppermute | solution.py:250
  48.4 2.3 collective-permute-start.3
  50.7 1.8 slice_select_fusion.3
  52.5 2.6 %shard_map.59 = f32[1,64,1024]{2,1,0:T(8,128)} custom-call(s32[9]{0:T(128)} %pad_add_fusion.2.scalars, s32[16,128]{1,0:T(8,128)} %shard_map.56.places_ref, f32[64,1024]{1,0:T(8,128)} %get-tuple-element.93.front_ref, f32[64,1024]{1,0:T(8,128)} %get-tuple-element.92.source_ref), custom_call_target="tpu_custom_call" | custom-call | tf_op jit(solution)/shard_map/pallas_call | solution.py:127
  55.1 1.0 slice_select_fusion.4
  56.1 0.7 pad_maximum_fusion.3.refs_0_
  56.9 5.1 %shard_map.60 = (f32[8,32,1536]{2,1,0:T(8,128)}, f32[8,8,1664]{2,1,0:T(8,128)}, f32[8,8,1664]{2,1,0:T(8,128)}, f32[8,8,1664]{2,1,0:T(8,128)}, f32[8,8,1664]{2,1,0:T(8,128)}) custom-call(s32[97]{0:T(128)} %get-tuple-element.104.scalars, s32[192,128]{1,0:T(8,128)S(1)} %shard_map.55.places_ref, f32[8,64,1536]{2,1,0:T(8,128)} %get-tuple-element.106.front_ref, ...), custom_call_target="tpu_custom_call" | custom-call | tf_op jit(solution)/shard_map/pallas_call | solution.py:127
  61.9 0.9 slice_select_fusion.5
  62.9 0.7 pad_maximum_fusion.2
  63.6 6.4 %collective-permute-done.3.source_ref = f32[32,6656]{1,0:T(8,128)} collective-permute-done((f32[32,6656]{1,0:T(8,128)}, f32[32,6656]{1,0:T(8,128)}, u32[]{:S(2)}, u32[]{:S(2)}) %collective-permute-start.3) | collective-permute-done | bytes 852000 | tf_op jit(solution)/shard_map/ppermute | solution.py:250
  70.0 8.5 %all-to-all-start = ((f32[8,32,1536]{2,1,0:T(8,128)}), f32[8,32,1536]{2,1,0:T(8,128)}, u32[]{:S(2)}, u32[]{:S(2)}) async-start(f32[8,32,1536]{2,1,0:T(8,128)} %get-tuple-element.81), calls=%async_computation | async-start | bytes 3145728 | tf_op jit(solution)/shard_map/all_to_all | solution.py:329
  78.6 1.4 collective-permute-start.5
  80.0 1.3 collective-permute-start.6
  81.3 1.4 collective-permute-start.7
  82.7 1.4 collective-permute-start.8
  84.1 4.8 %shard_map.61 = (f32[8,32,1536]{2,1,0:T(8,128)}, f32[8,8,1664]{2,1,0:T(8,128)}, f32[8,8,1664]{2,1,0:T(8,128)}, f32[8,8,1664]{2,1,0:T(8,128)}, f32[8,8,1664]{2,1,0:T(8,128)}) custom-call(s32[97]{0:T(128)} %get-tuple-element.104.scalars, s32[192,128]{1,0:T(8,128)S(1)} %shard_map.55.places_ref, f32[8,64,1536]{2,1,0:T(8,128)S(1)} %copy-done.2, ...), custom_call_target="tpu_custom_call" | custom-call | tf_op jit(solution)/shard_map/pallas_call | solution.py:127
  88.9 0.7 collective-permute-start.4
  89.6 0.7 collective-permute-start.9
  90.3 12.2 %collective-permute-done.6 = f32[8,8,1664]{2,1,0:T(8,128)} collective-permute-done((f32[8,8,1664]{2,1,0:T(8,128)}, f32[8,8,1664]{2,1,0:T(8,128)}, u32[]{:S(2)}, u32[]{:S(2)}) %collective-permute-start.6) | collective-permute-done | bytes 426016 | tf_op jit(solution)/shard_map/ppermute | solution.py:334
  102.5 0.7 collective-permute-start.10
  103.3 1.6 add_add_fusion
  105.0 25.4 %all-to-all-done.refs_1_ = f32[8,32,1536]{2,1,0:T(8,128)} async-done(((f32[8,32,1536]{2,1,0:T(8,128)}), f32[8,32,1536]{2,1,0:T(8,128)}, u32[]{:S(2)}, u32[]{:S(2)}) %all-to-all-start) | async-done | bytes 1572896 | tf_op jit(solution)/shard_map/all_to_all | solution.py:329
  130.4 19.9 %all_to_all.15 = f32[8,8,2048]{2,1,0:T(8,128)S(1)} all-to-all(f32[8,8,2048]{2,1,0:T(8,128)S(1)} %pad_maximum_fusion), channel_id=1, replica_groups=mesh['subcube'=2,'row'=8,'col'=16] {'row'}, dimensions={0} | all-to-all | bytes 1048576 | tf_op jit(solution)/shard_map/all_to_all | solution.py:329
  150.4 0.8 slice.144
  151.9 3.6 %all-to-all-start.2 = ((f32[8,32,1536]{2,1,0:T(8,128)}), f32[8,32,1536]{2,1,0:T(8,128)S(1)}, u32[]{:S(2)}, u32[]{:S(2)}) async-start(f32[8,32,1536]{2,1,0:T(8,128)} %get-tuple-element.83), calls=%async_computation.2 | async-start | bytes 3145728 | tf_op jit(solution)/shard_map/all_to_all | solution.py:329
  155.7 1.1 collective-permute-done.11
  157.6 1.3 slice.143
  160.1 33.4 %all-gather.9.cloned.1.call-done = f32[1024,1536]{1,0:T(8,128)} async-done(((f32[64,1536]{1,0:T(8,128)}), f32[1024,1536]{1,0:T(8,128)}) %all-gather.9.cloned.1.call-update) | async-done | bytes 6291472 | tf_op jit(solution)/shard_map/all_gather | solution.py:347
  193.5 9.0 %shard_map.62 = (f32[512,512]{1,0:T(8,128)}, f32[512,512]{1,0:T(8,128)}, f32[512,512]{1,0:T(8,128)}) custom-call(s32[2]{0:T(128)} %pad_add_fusion.6.flags, f32[8,72,1024]{2,1,0:T(8,128)} %bitcast.60, f32[8,2,64,512]{3,2,1,0:T(8,128)} %bitcast.63, f32[8,2,64,1536]{3,2,1,0:T(8,128)} %bitcast.53), custom_call_target="tpu_custom_call" | custom-call | tf_op jit(solution)/shard_map/pallas_call | solution.py:180
  202.5 1.2 copy-done.3
  203.7 8.7 %shard_map.63.refs_6_ = f32[1536,512]{1,0:T(8,128)} custom-call(s32[12]{0:T(128)} %reshape.131.flags, f32[8,32,1536]{2,1,0:T(8,128)} %copy-done.3, f32[8,32,1536]{2,1,0:T(8,128)} %all-to-all-done.refs_1_, f32[8,2,64,1536]{3,2,1,0:T(8,128)} %bitcast.54, f32[512,512]{1,0:T(8,128)} %get-tuple-element.87.refs_3_, f32[512,512]{1,0:T(8,128)} %get-tuple-element.88.refs_4_, ...), custom_call_target="tpu_custom_call" | custom-call | tf_op jit(solution)/shard_map/pallas_call | solution.py:223
  212.4 19.3 %all-gather.7.cloned.1.call-done = f32[1024,512]{1,0:T(8,128)} async-done(((f32[64,512]{1,0:T(8,128)}), f32[1024,512]{1,0:T(8,128)}) %all-gather.7.cloned.1.call-update) | async-done | bytes 2097168 | tf_op jit(solution)/shard_map/all_gather | solution.py:347
  231.7 6.4 %shard_map.64 = f32[1536,512]{1,0:T(8,128)} custom-call(s32[12]{0:T(128)} %reshape.131.flags, f32[8,32,1536]{2,1,0:T(8,128)} %copy-done.3, f32[8,32,1536]{2,1,0:T(8,128)} %all-to-all-done.refs_1_, f32[8,2,64,512]{3,2,1,0:T(8,128)} %bitcast.64, f32[512,512]{1,0:T(8,128)} %get-tuple-element.87.refs_3_, ...), custom_call_target="tpu_custom_call", output_to_operand_aliasing={{}: (7, {})} | custom-call | tf_op jit(solution)/shard_map/pallas_call | solution.py:223
  (63 shorter events, 6.2 us)
Async XLA Ops:
  6.5 63.5 %all-gather.11.cloned.1.call-start = ((), (), s32[]{:S(2)}) async-start(), calls=%async_computation.5 | async-start | bytes 2359296 | tf_op jit(solution)/shard_map/all_gather | solution.py:252
  7.3 150.3 %all-gather.13.cloned.1.call-start = ((), (), s32[]{:S(2)}) async-start(), calls=%async_computation.6 | async-start | bytes 2654208 | tf_op jit(solution)/shard_map/all_gather | solution.py:324
  14.9 2.9 %copy-start = (f32[1,1,1,64,12288]{4,3,2,1,0:T(8,128)S(1)}, f32[1,1,1,64,12288]{4,3,2,1,0:T(8,128)}, u32[]{:S(2)}) copy-start(f32[1,1,1,64,12288]{4,3,2,1,0:T(8,128)} %param.10) | copy-start | bytes 9437188
  17.8 6.7 %copy-start.6 = (s32[2,12288]{1,0:T(2,128)S(1)}, s32[2,12288]{1,0:T(2,128)}, u32[]{:S(2)}) copy-start(s32[2,12288]{1,0:T(2,128)} %param.11) | copy-start | bytes 294916
  19.5 19.7 %collective-permute-start.1 = (f32[72,1024]{1,0:T(8,128)}, f32[72,1024]{1,0:T(8,128)}, u32[]{:S(2)}, u32[]{:S(2)}) collective-permute-start(f32[72,1024]{1,0:T(8,128)} %pad_maximum_fusion.1), channel_id=1, source_target_pairs={{0,128},{128,0},{1,129},{129,1},{2,130},{130,2},{3,131},{131,3},{4... | collective-permute-start | bytes 884744 | tf_op jit(solution)/shard_map/ppermute | solution.py:250
  23.3 25.1 %collective-permute-start.2 = (f32[32,6656]{1,0:T(8,128)}, f32[32,6656]{1,0:T(8,128)}, u32[]{:S(2)}, u32[]{:S(2)}) collective-permute-start(f32[32,6656]{1,0:T(8,128)} %get-tuple-element.91), channel_id=1, source_target_pairs={{0,128},{128,0},{1,129},{129,1},{2,130},{130,2},{3,131},{131,3},{4... | collective-permute-start | bytes 2555912 | tf_op jit(solution)/shard_map/ppermute | solution.py:250
  38.6 12.1 %copy-start.5 = (f32[1,64,1024]{2,1,0:T(8,128)S(1)}, f32[1,64,1024]{2,1,0:T(8,128)}, u32[]{:S(2)}) copy-start(f32[1,64,1024]{2,1,0:T(8,128)} %shard_map.57) | copy-start | bytes 786436
  48.4 21.6 %collective-permute-start.3 = (f32[32,6656]{1,0:T(8,128)}, f32[32,6656]{1,0:T(8,128)}, u32[]{:S(2)}, u32[]{:S(2)}) collective-permute-start(f32[32,6656]{1,0:T(8,128)} %get-tuple-element.68), channel_id=1, source_target_pairs={{0,128},{128,0},{1,129},{129,1},{2,130},{130,2},{3,131},{131,3},{4... | collective-permute-start | bytes 2555912 | tf_op jit(solution)/shard_map/ppermute | solution.py:250
  55.1 7.7 %copy-start.4 = (f32[1,64,1024]{2,1,0:T(8,128)S(1)}, f32[1,64,1024]{2,1,0:T(8,128)}, u32[]{:S(2)}) copy-start(f32[1,64,1024]{2,1,0:T(8,128)} %shard_map.59) | copy-start | bytes 786436
  61.9 22.2 %copy-start.2 = (f32[8,64,1536]{2,1,0:T(8,128)S(1)}, f32[8,64,1536]{2,1,0:T(8,128)}, u32[]{:S(2)}) copy-start(f32[8,64,1536]{2,1,0:T(8,128)} %get-tuple-element.106.front_ref) | copy-start | bytes 9437188
  70.0 60.4 %all-to-all-start = ((f32[8,32,1536]{2,1,0:T(8,128)}), f32[8,32,1536]{2,1,0:T(8,128)}, u32[]{:S(2)}, u32[]{:S(2)}) async-start(f32[8,32,1536]{2,1,0:T(8,128)} %get-tuple-element.81), calls=%async_computation | async-start | bytes 3145728 | tf_op jit(solution)/shard_map/all_to_all | solution.py:329
  78.5 115.0 %all-gather.9.cloned.1.call-start = ((), (), s32[]{:S(2)}) async-start(), calls=%async_computation.4 | async-start | bytes 6684672 | tf_op jit(solution)/shard_map/all_gather | solution.py:347
  78.6 11.0 %collective-permute-start.5 = (f32[8,8,1664]{2,1,0:T(8,128)}, f32[8,8,1664]{2,1,0:T(8,128)}, u32[]{:S(2)}, u32[]{:S(2)}) collective-permute-start(f32[8,8,1664]{2,1,0:T(8,128)} %get-tuple-element.74), channel_id=1, source_target_pairs={{0,4},{1,5},{16,20},{17,21},{32,36},{33,37},{48,52},{49,53},{64,68... | collective-permute-start | bytes 1277960 | tf_op jit(solution)/shard_map/ppermute | solution.py:334
  80.0 22.6 %collective-permute-start.6 = (f32[8,8,1664]{2,1,0:T(8,128)}, f32[8,8,1664]{2,1,0:T(8,128)}, u32[]{:S(2)}, u32[]{:S(2)}) collective-permute-start(f32[8,8,1664]{2,1,0:T(8,128)} %get-tuple-element.75), channel_id=1, source_target_pairs={{0,6},{1,7},{16,22},{17,23},{32,38},{33,39},{48,54},{49,55},{64,70... | collective-permute-start | bytes 1277960 | tf_op jit(solution)/shard_map/ppermute | solution.py:334
  81.3 22.0 %collective-permute-start.7 = (f32[8,8,1664]{2,1,0:T(8,128)}, f32[8,8,1664]{2,1,0:T(8,128)}, u32[]{:S(2)}, u32[]{:S(2)}) collective-permute-start(f32[8,8,1664]{2,1,0:T(8,128)} %get-tuple-element.76), channel_id=1, source_target_pairs={{0,8},{1,9},{16,24},{17,25},{32,40},{33,41},{48,56},{49,57},{64,72... | collective-permute-start | bytes 1277960 | tf_op jit(solution)/shard_map/ppermute | solution.py:334
  82.7 20.6 %collective-permute-start.8 = (f32[8,8,1664]{2,1,0:T(8,128)}, f32[8,8,1664]{2,1,0:T(8,128)}, u32[]{:S(2)}, u32[]{:S(2)}) collective-permute-start(f32[8,8,1664]{2,1,0:T(8,128)} %get-tuple-element.77), channel_id=1, source_target_pairs={{0,10},{1,11},{16,26},{17,27},{32,42},{33,43},{48,58},{49,59},{64,... | collective-permute-start | bytes 1277960 | tf_op jit(solution)/shard_map/ppermute | solution.py:334
  88.9 14.4 %collective-permute-start.4 = (f32[8,8,1664]{2,1,0:T(8,128)}, f32[8,8,1664]{2,1,0:T(8,128)S(1)}, u32[]{:S(2)}, u32[]{:S(2)}) collective-permute-start(f32[8,8,1664]{2,1,0:T(8,128)} %get-tuple-element.73), channel_id=1, source_target_pairs={{0,2},{1,3},{16,18},{17,19},{32,34},{33,35},{48,50},{49,51},{64,66... | collective-permute-start | bytes 1277960 | tf_op jit(solution)/shard_map/ppermute | solution.py:334
  89.6 13.7 %collective-permute-start.9 = (f32[8,8,1664]{2,1,0:T(8,128)}, f32[8,8,1664]{2,1,0:T(8,128)S(1)}, u32[]{:S(2)}, u32[]{:S(2)}) collective-permute-start(f32[8,8,1664]{2,1,0:T(8,128)} %get-tuple-element.78), channel_id=1, source_target_pairs={{0,12},{1,13},{16,28},{17,29},{32,44},{33,45},{48,60},{49,61},{64,... | collective-permute-start | bytes 1277960 | tf_op jit(solution)/shard_map/ppermute | solution.py:334
  102.5 0.7 collective-permute-start.10
  105.0 50.5 %copy-start.7 = (s32[3,1]{0,1:T(1,128)S(1)}, s32[3,1]{0,1:T(1,128)}, u32[]{:S(2)}) copy-start(s32[3,1]{0,1:T(1,128)} %param.13) | copy-start | bytes 40
  151.2 80.5 %all-gather.7.cloned.1.call-start = ((), (), s32[]{:S(2)}) async-start(), calls=%async_computation.3 | async-start | bytes 2228224 | tf_op jit(solution)/shard_map/all_gather | solution.py:347
  151.9 50.6 %all-to-all-start.2 = ((f32[8,32,1536]{2,1,0:T(8,128)}), f32[8,32,1536]{2,1,0:T(8,128)S(1)}, u32[]{:S(2)}, u32[]{:S(2)}) async-start(f32[8,32,1536]{2,1,0:T(8,128)} %get-tuple-element.83), calls=%async_computation.2 | async-start | bytes 3145728 | tf_op jit(solution)/shard_map/all_to_all | solution.py:329
  155.6 1.3 collective-permute-start.11
  202.5 1.2 copy-start.3
Sparse Core Ops, SparseCore 0:
  9.1 44.1 all-gather.10
  70.2 68.8 all-gather.12
  151.3 42.1 all-gather.8
  195.2 36.4 all-gather.6

commit v8 on v6

--- a/solution.py
+++ b/solution.py
@@ -156,11 +156,10 @@
 
 def factor_kernel(order, flags, gathered_ref, inverse_ref, corner_ref, first_ref, second_ref, fixed_ref):
     place, kept = flags[0], flags[1]
-    thin = inverse_ref.shape[1]
+    thin = inverse_ref.shape[2]
     by_chip = lambda x: jnp.concatenate([x[:, 8 * q : 8 * q + 8].reshape(-1, x.shape[2]) for q in order])
     strip = gathered_ref[:, :thin].reshape(PANEL, 2 * PANEL)
-    inverse = by_chip(inverse_ref[...])
-    inverse0, inverse1 = inverse[:, :PANEL], inverse[:, PANEL:]
+    inverse0, inverse1 = (by_chip(inverse_ref[:, k]) for k in range(PANELS))
     halves0, halves1 = halves(inverse0), halves(inverse1)
     corner = corner_ref[...]
     corner10, corner01 = (halves(corner[:, k].reshape(PANEL, PANEL)) for k in range(PANELS))
@@ -184,7 +183,10 @@
         grid_spec=pltpu.PrefetchScalarGridSpec(
             num_scalar_prefetch=1,
             grid=(1,),
-            in_specs=[pl.BlockSpec(x.shape, lambda i, _: (0, 0, 0)) for x in (gathered, inverse)]
+            in_specs=[
+                pl.BlockSpec(gathered.shape, lambda i, _: (0, 0, 0)),
+                pl.BlockSpec(inverse.shape, lambda i, _: (0, 0, 0, 0)),
+            ]
             + [pl.BlockSpec(panels.shape[:3] + (PANEL,), lambda i, _: (0, 0, 0, panels.shape[3] // PANEL - 1))],
             out_specs=[pl.BlockSpec((PANEL, PANEL), lambda i, _: (0, 0))] * 3,
         ),
@@ -244,15 +246,14 @@
     zero = jnp.zeros((), jnp.int32)
     exchange = lambda x: lax.ppermute(x, "subcube", [(0, 1), (1, 0)])
 
-    inverse = lax.all_gather(jnp.concatenate([pivot_inverses[k] for k in range(PANELS)], axis=1), "row", axis=0)
+    inverse = lax.all_gather(pivot_inverses, "row", axis=0)
 
     window = -(-(child_rows * 13 // 24) // LANES) * LANES
     rest = child_rows - window
-    parts = [(thin // 2, thin), (0, thin // 2)]
+    share = thin // 4
+    parts = [(thin - share, thin), (0, thin - share)]
     first_sent, last_sent = [jnp.where(side == 0, own[a:b, rest:], own[a:b, :window]) for a, b in parts]
     received = [exchange(first_sent)]
-    last_sent, received[0] = lax.optimization_barrier((last_sent, received[0]))
-    received.append(exchange(last_sent))
 
     map_blocks = child_rows // LANES
     blocks = half_rows // LANES
@@ -295,25 +296,38 @@
 
     base_sum = lax.cond(spill, add_rest, lambda x: x, base_sum)
 
-    got, received[0], base_sum = lax.optimization_barrier((got, received[0], base_sum))
+    got, received[0], base_sum, last_sent = lax.optimization_barrier((got, received[0], base_sum, last_sent))
+    received.append(exchange(last_sent))
     strip = strip_add(jnp.where(side == 0, base, got[:thin]), jnp.where(side == 0, got[:thin], prefix), 1)
     first_masks = jnp.where(side == 0, mask_rows, got[thin:])
-
-    strip, inverse = lax.optimization_barrier((strip, inverse))
-    gathered = lax.all_gather(jnp.concatenate([strip, first_masks]), "row", axis=0)
-    kept = gathered[0, thin, 1] > 0.5
 
     corner = jnp.where(place == 0, strip[:, PANEL:], strip[:, :PANEL])
     tail = jnp.concatenate([corner, jnp.broadcast_to(mask_rows[:1, :PANEL], (thin, PANEL))], axis=1)
     wholes, pieces = [], {}
-    for (a, b), part in zip(parts, received):
+
+    def assemble(index):
+        a, b = parts[index]
         size = b - a
-        whole, *chunk_list = add_other(base_sum, part, offset=window_at, columns=size, part=a // size, tail=tail)
+        whole, *chunk_list = add_other(
+            base_sum, received[index], offset=window_at, columns=size, part=a // size, tail=tail
+        )
         wholes.append(whole)
         pieces.update({a // 8 + i: chunk for i, chunk in enumerate(chunk_list)})
 
+    assemble(0)
+    to_gather = jnp.concatenate([strip, first_masks])
+    to_gather, inverse, received[1], wholes[0] = lax.optimization_barrier(
+        (to_gather, inverse, received[1], wholes[0])
+    )
+    gathered = lax.all_gather(to_gather, "row", axis=0)
+    kept = gathered[0, thin, 1] > 0.5
+
+    assemble(1)
+
     across = lambda x: lax.all_to_all(x, "row", split_axis=0, concat_axis=0, tiled=True)
-    order = [0, 1] + list(range(chunks // 2, chunks)) + list(range(2, chunks // 2))
+    order = list(range(chunks))
+    middle = chunks // 2
+    order[middle : middle + 2], order[-2:] = order[-2:], order[middle : middle + 2]
     mine = jnp.where(place // PANELS == 0, pieces[order[0]], 0.0)
     for chip in range(1, chunks):
         pairs = [(k, PANELS * chip + k) for k in range(PANELS)]

time: 228 us -> 229 us (level)
  waiting for transfers between devices: 92.2 us -> 95.3 us
    ppermute x7, waiting for transfers between devices: 0.02 us -> 19.8 us  [local(): mine = mine + lax.ppermute(pieces[order[chip]], 'col', pairs)]
    all_to_all x2, waiting for transfers between devices: 25.9 us -> 8.87 us  [local(): lax.all_to_all(x, 'row', split_axis=0, concat_axis=0, tiled=True)]
    ppermute x3, waiting for transfers between devices: 22.5 us -> 15.9 us  [local(): exchange = lambda x: lax.ppermute(x, 'subcube', [(0, 1), (1, 0)])]
    all_gather x1, waiting for transfers between devices: 42.5 us -> 48.8 us  [local(): panels = lax.all_gather(mine.reshape(thin, -1), 'col', axis=0, tiled=True)]
  transfers between devices with their start and end apart: 16 -> 16, of which waited for: 5 -> 6; matrix products, arithmetic and copies ran while one was open for 9% -> 10% of each run, Pallas kernels for 16% -> 16%
where the time goes in v8:
time: 229 us; the launch traced here: 227 us
  waiting for transfers between devices  95.3 us (42%)
  Pallas kernels  47.2 us (21%)
  starting transfers between devices  25.2 us (11%)
  blocking collectives  18.9 us (8%)
  other arithmetic  16.6 us (7%)
  between operations  15.3 us (7%)
  local copies, waits for them, and re-layouts  8.54 us (4%)
    all_gather x1, waiting for transfers between devices, local(): panels = lax.all_gather(mine.reshape(thin, -1), 'col', axis=0, tiled=True)  48.8 us
    pallas_call x5, Pallas kernels, extend_add(): pl.pallas_call(functools.partial(extend_kernel, first_place, map_blocks),...  20.2 us
    ppermute x7, waiting for transfers between devices, local(): mine = mine + lax.ppermute(pieces[order[chip]], 'col', pairs)  19.8 us
    all_to_all x1, blocking collectives, local(): lax.all_to_all(x, 'row', split_axis=0, concat_axis=0, tiled=True)  18.9 us
    ppermute x3, waiting for transfers between devices, local(): exchange = lambda x: lax.ppermute(x, 'subcube', [(0, 1), (1, 0)])  15.9 us
    all_to_all x2, starting transfers between devices, local(): lax.all_to_all(x, 'row', split_axis=0, concat_axis=0, tiled=True)  12.2 us
    pallas_call x1, Pallas kernels, update(): pl.pallas_call(update_kernel, out_shape=jax.ShapeDtypeStruct((rows, PANEL...  10.9 us
    pallas_call x1, Pallas kernels, factor(): pl.pallas_call(functools.partial(factor_kernel, order), out_shape=(square...  8.96 us
  transfers between devices with their start and end apart: 16, of which 6 were waited for; matrix products, arithmetic and copies ran while one was open for 10% of the time, Pallas kernels for 16%

profile of v8, /device:TPU:10, one launch (start us, length us, event | category | flops | bytes accessed | tf_op | source)
XLA Modules:
  0.0 227.0 jit_solution(13802898049165126302)
XLA Ops:
  6.5 0.7 all-gather.8.cloned.1.call-update
  8.0 1.2 convert_reduce_fusion.1
  9.2 1.5 copy.11
  11.3 0.7 concatenate.39.scalars
  12.0 2.9 %shard_map.56.places_ref = s32[16,128]{1,0:T(8,128)} custom-call(s32[20]{0:T(128)} %concatenate.39.scalars, s32[2,96,128]{2,1,0:T(8,128)} %bitcast.64), custom_call_target="tpu_custom_call" | custom-call | tf_op jit(solution)/shard_map/pallas_call | solution.py:53
  14.9 2.9 %shard_map.57 = f32[1,64,1024]{2,1,0:T(8,128)} custom-call(s32[9]{0:T(128)} %pad_add_fusion.3.scalars, s32[16,128]{1,0:T(8,128)} %shard_map.56.places_ref, f32[64,12288]{1,0:T(8,128)} %bitcast.55, f32[64,12288]{1,0:T(8,128)} %bitcast.46), custom_call_target="tpu_custom_call" | custom-call | tf_op jit(solution)/shard_map/pallas_call | solution.py:127
  17.8 1.0 bitcast_select_fusion.1
  18.7 0.8 pad_maximum_fusion.1
  19.5 2.3 %collective-permute-start.1 = (f32[72,1024]{1,0:T(8,128)}, f32[72,1024]{1,0:T(8,128)}, u32[]{:S(2)}, u32[]{:S(2)}) collective-permute-start(f32[72,1024]{1,0:T(8,128)} %pad_maximum_fusion.1), channel_id=1, source_target_pairs={{0,128},{128,0},{1,129},{129,1},{2,130},{130,2},{3,131},{131,3},{4... | collective-permute-start | bytes 884744 | tf_op jit(solution)/shard_map/ppermute | solution.py:247
  21.8 0.8 slice_select_fusion.2
  22.6 1.2 collective-permute-start.2
  24.3 1.1 convert_reduce_fusion
  25.4 1.2 slice_select_fusion.1
  29.0 4.3 %shard_map.55.places_ref = s32[192,128]{1,0:T(8,128)S(1)} custom-call(s32[196]{0:T(256)} %concatenate.37.scalars, s32[2,96,128]{2,1,0:T(8,128)} %bitcast.65), custom_call_target="tpu_custom_call" | custom-call | tf_op jit(solution)/shard_map/pallas_call | solution.py:53
  33.3 0.7 pad_add_fusion.4
  33.9 4.8 %shard_map.58 = f32[8,64,1536]{2,1,0:T(8,128)} custom-call(s32[97]{0:T(128)} %get-tuple-element.103.scalars, s32[192,128]{1,0:T(8,128)S(1)} %shard_map.55.places_ref, f32[64,12288]{1,0:T(8,128)} %bitcast.56, f32[64,12288]{1,0:T(8,128)S(1)} %bitcast.50), custom_call_target="tpu_custom_call" | custom-call | tf_op jit(solution)/shard_map/pallas_call | solution.py:127
  39.2 2.3 %collective-permute-start.3 = (f32[48,6656]{1,0:T(8,128)}, f32[48,6656]{1,0:T(8,128)}, u32[]{:S(2)}, u32[]{:S(2)}) collective-permute-start(f32[48,6656]{1,0:T(8,128)} %slice_select_fusion.1), channel_id=1, source_target_pairs={{0,128},{128,0},{1,129},{129,1},{2,130},{130,2},{3,131},{131,3},{4... | collective-permute-start | bytes 3833864 | tf_op jit(solution)/shard_map/ppermute | solution.py:247
  42.1 1.8 slice_select_fusion.3
  44.0 2.9 %shard_map.59 = f32[1,64,1024]{2,1,0:T(8,128)} custom-call(s32[9]{0:T(128)} %pad_add_fusion.2.scalars, s32[16,128]{1,0:T(8,128)} %shard_map.56.places_ref, f32[64,1024]{1,0:T(8,128)} %get-tuple-element.91.front_ref, f32[64,1024]{1,0:T(8,128)} %get-tuple-element.90.source_ref), custom_call_target="tpu_custom_call" | custom-call | tf_op jit(solution)/shard_map/pallas_call | solution.py:127
  46.9 1.0 slice_select_fusion.4
  47.9 0.7 pad_maximum_fusion.3.refs_0_
  48.6 4.4 %shard_map.60 = (f32[8,16,1536]{2,1,0:T(8,128)}, f32[8,8,1664]{2,1,0:T(8,128)}, f32[8,8,1664]{2,1,0:T(8,128)}) custom-call(s32[97]{0:T(128)} %get-tuple-element.102.scalars, s32[192,128]{1,0:T(8,128)S(1)} %shard_map.55.places_ref, f32[8,64,1536]{2,1,0:T(8,128)} %get-tuple-element.104.front_ref, f32[16,6656]{1,0:T(8,128)} %collective-permute-done.2.source_ref, ...), custom_call_target="tpu_custom_call" | custom-call | tf_op jit(solution)/shard_map/pallas_call | solution.py:127
  53.0 0.8 slice_select_fusion.5
  53.8 0.7 pad_maximum_fusion.2
  54.5 15.5 %collective-permute-done.3.source_ref = f32[48,6656]{1,0:T(8,128)} collective-permute-done((f32[48,6656]{1,0:T(8,128)}, f32[48,6656]{1,0:T(8,128)}, u32[]{:S(2)}, u32[]{:S(2)}) %collective-permute-start.3) | collective-permute-done | bytes 1277984 | tf_op jit(solution)/shard_map/ppermute | solution.py:247
  70.0 1.4 collective-permute-start.7
  71.4 1.4 collective-permute-start.8
  72.9 5.2 %shard_map.61 = (f32[8,48,1536]{2,1,0:T(8,128)}, f32[8,8,1664]{2,1,0:T(8,128)}, f32[8,8,1664]{2,1,0:T(8,128)}, f32[8,8,1664]{2,1,0:T(8,128)}, f32[8,8,1664]{2,1,...) custom-call(s32[97]{0:T(128)} %get-tuple-element.102.scalars, s32[192,128]{1,0:T(8,128)S(1)} %shard_map.55.places_ref, ...), custom_call_target="tpu_custom_call" | custom-call | tf_op jit(solution)/shard_map/pallas_call | solution.py:127
  78.1 0.7 collective-permute-start.4
  78.8 0.7 collective-permute-start.5
  79.5 1.5 collective-permute-start.6
  81.0 0.7 collective-permute-start.9
  81.7 0.7 collective-permute-start.10
  82.4 8.5 %all-to-all-start = ((f32[8,16,1536]{2,1,0:T(8,128)}), f32[8,16,1536]{2,1,0:T(8,128)S(1)}, u32[]{:S(2)}, u32[]{:S(2)}) async-start(f32[8,16,1536]{2,1,0:T(8,128)} %get-tuple-element.81), calls=%async_computation | async-start | bytes 1572864 | tf_op jit(solution)/shard_map/all_to_all | solution.py:327
  90.9 19.8 %collective-permute-done.6 = f32[8,8,1664]{2,1,0:T(8,128)S(1)} collective-permute-done((f32[8,8,1664]{2,1,0:T(8,128)}, f32[8,8,1664]{2,1,0:T(8,128)S(1)}, u32[]{:S(2)}, u32[]{:S(2)}) %collective-permute-start.6) | collective-permute-done | bytes 426016 | tf_op jit(solution)/shard_map/ppermute | solution.py:334
  110.7 1.3 add_add_fusion
  112.1 0.7 copy-done.7
  112.8 8.9 %all-to-all-done.refs_1_ = f32[8,16,1536]{2,1,0:T(8,128)S(1)} async-done(((f32[8,16,1536]{2,1,0:T(8,128)}), f32[8,16,1536]{2,1,0:T(8,128)S(1)}, u32[]{:S(2)}, u32[]{:S(2)}) %all-to-all-start) | async-done | bytes 786464 | tf_op jit(solution)/shard_map/all_to_all | solution.py:327
  121.7 18.9 %all_to_all.15 = f32[8,8,2048]{2,1,0:T(8,128)} all-to-all(f32[8,8,2048]{2,1,0:T(8,128)S(1)} %pad_maximum_fusion), channel_id=1, replica_groups=mesh['subcube'=2,'row'=8,'col'=16] {'row'}, dimensions={0} | all-to-all | bytes 1048576 | tf_op jit(solution)/shard_map/all_to_all | solution.py:327
  140.6 3.7 %all-to-all-start.2 = ((f32[8,48,1536]{2,1,0:T(8,128)}), f32[8,48,1536]{2,1,0:T(8,128)S(1)}, u32[]{:S(2)}, u32[]{:S(2)}) async-start(f32[8,48,1536]{2,1,0:T(8,128)} %get-tuple-element.83), calls=%async_computation.2 | async-start | bytes 4718592 | tf_op jit(solution)/shard_map/all_to_all | solution.py:327
  144.3 0.7 slice_bitcast_fusion.1
  145.1 1.1 collective-permute-done.11
  146.2 0.7 broadcast_select_fusion
  147.7 1.3 slice.129
  150.3 48.8 %all-gather.6.cloned.1.call-done = f32[1024,2048]{1,0:T(8,128)} async-done(((f32[64,2048]{1,0:T(8,128)}), f32[1024,2048]{1,0:T(8,128)}) %all-gather.6.cloned.1.call-update) | async-done | bytes 8388624 | tf_op jit(solution)/shard_map/all_gather | solution.py:344
  199.2 9.0 %shard_map.62 = (f32[512,512]{1,0:T(8,128)}, f32[512,512]{1,0:T(8,128)}, f32[512,512]{1,0:T(8,128)}) custom-call(s32[2]{0:T(128)} %pad_add_fusion.6.flags, f32[8,72,1024]{2,1,0:T(8,128)} %bitcast.58, f32[8,2,64,512]{3,2,1,0:T(8,128)} %bitcast.61, f32[8,2,64,2048]{3,2,1,0:T(8,128)} %bitcast.53), custom_call_target="tpu_custom_call" | custom-call | tf_op jit(solution)/shard_map/pallas_call | solution.py:180
  208.1 1.5 copy-done.3
  209.6 10.9 %shard_map.63 = f32[1536,512]{1,0:T(8,128)} custom-call(s32[12]{0:T(128)} %reshape.127.flags, f32[8,48,1536]{2,1,0:T(8,128)} %copy-done.3, f32[8,16,1536]{2,1,0:T(8,128)} %copy-done.4, f32[8,2,64,2048]{3,2,1,0:T(8,128)} %bitcast.54, f32[512,512]{1,0:T(8,128)} %get-tuple-element.87.refs_3_, f32[512,512]{1,0:T(8,128)} %get-tuple-element.88.refs_4_, ...), custom_call_target="tpu_custom_call" | custom-call | tf_op jit(solution)/shard_map/pallas_call | solution.py:215
  (61 shorter events, 5.6 us)
Async XLA Ops:
  6.5 63.4 %all-gather.8.cloned.1.call-start = ((), (), s32[]{:S(2)}) async-start(), calls=%async_computation.4 | async-start | bytes 2359296 | tf_op jit(solution)/shard_map/all_gather | solution.py:249
  7.3 140.4 %all-gather.10.cloned.1.call-start = ((), (), s32[]{:S(2)}) async-start(), calls=%async_computation.5 | async-start | bytes 2654208 | tf_op jit(solution)/shard_map/all_gather | solution.py:322
  14.9 2.9 %copy-start = (f32[1,1,1,64,12288]{4,3,2,1,0:T(8,128)S(1)}, f32[1,1,1,64,12288]{4,3,2,1,0:T(8,128)}, u32[]{:S(2)}) copy-start(f32[1,1,1,64,12288]{4,3,2,1,0:T(8,128)} %param.10) | copy-start | bytes 9437188
  14.9 9.0 %copy-start.8 = (s32[2,12288]{1,0:T(2,128)S(1)}, s32[2,12288]{1,0:T(2,128)}, u32[]{:S(2)}) copy-start(s32[2,12288]{1,0:T(2,128)} %param.11) | copy-start | bytes 294916
  19.5 19.2 %collective-permute-start.1 = (f32[72,1024]{1,0:T(8,128)}, f32[72,1024]{1,0:T(8,128)}, u32[]{:S(2)}, u32[]{:S(2)}) collective-permute-start(f32[72,1024]{1,0:T(8,128)} %pad_maximum_fusion.1), channel_id=1, source_target_pairs={{0,128},{128,0},{1,129},{129,1},{2,130},{130,2},{3,131},{131,3},{4... | collective-permute-start | bytes 884744 | tf_op jit(solution)/shard_map/ppermute | solution.py:247
  22.6 16.6 %collective-permute-start.2 = (f32[16,6656]{1,0:T(8,128)}, f32[16,6656]{1,0:T(8,128)}, u32[]{:S(2)}, u32[]{:S(2)}) collective-permute-start(f32[16,6656]{1,0:T(8,128)} %slice_select_fusion.2), channel_id=1, source_target_pairs={{0,128},{128,0},{1,129},{129,1},{2,130},{130,2},{3,131},{131,3},{4... | collective-permute-start | bytes 1277960 | tf_op jit(solution)/shard_map/ppermute | solution.py:247
  38.7 3.4 %copy-start.6 = (f32[1,64,1024]{2,1,0:T(8,128)S(1)}, f32[1,64,1024]{2,1,0:T(8,128)}, u32[]{:S(2)}) copy-start(f32[1,64,1024]{2,1,0:T(8,128)} %shard_map.57) | copy-start | bytes 786436
  39.2 30.8 %collective-permute-start.3 = (f32[48,6656]{1,0:T(8,128)}, f32[48,6656]{1,0:T(8,128)}, u32[]{:S(2)}, u32[]{:S(2)}) collective-permute-start(f32[48,6656]{1,0:T(8,128)} %slice_select_fusion.1), channel_id=1, source_target_pairs={{0,128},{128,0},{1,129},{129,1},{2,130},{130,2},{3,131},{131,3},{4... | collective-permute-start | bytes 3833864 | tf_op jit(solution)/shard_map/ppermute | solution.py:247
  44.0 28.9 %copy-start.2 = (f32[8,64,1536]{2,1,0:T(8,128)S(1)}, f32[8,64,1536]{2,1,0:T(8,128)}, u32[]{:S(2)}) copy-start(f32[8,64,1536]{2,1,0:T(8,128)} %get-tuple-element.104.front_ref) | copy-start | bytes 9437188
  46.9 6.9 %copy-start.5 = (f32[1,64,1024]{2,1,0:T(8,128)S(1)}, f32[1,64,1024]{2,1,0:T(8,128)}, u32[]{:S(2)}) copy-start(f32[1,64,1024]{2,1,0:T(8,128)} %shard_map.59) | copy-start | bytes 786436
  70.0 10.9 %collective-permute-start.7 = (f32[8,8,1664]{2,1,0:T(8,128)}, f32[8,8,1664]{2,1,0:T(8,128)}, u32[]{:S(2)}, u32[]{:S(2)}) collective-permute-start(f32[8,8,1664]{2,1,0:T(8,128)} %get-tuple-element.76), channel_id=1, source_target_pairs={{0,8},{1,9},{16,24},{17,25},{32,40},{33,41},{48,56},{49,57},{64,72... | collective-permute-start | bytes 1277960 | tf_op jit(solution)/shard_map/ppermute | solution.py:334
  71.4 10.2 %collective-permute-start.8 = (f32[8,8,1664]{2,1,0:T(8,128)}, f32[8,8,1664]{2,1,0:T(8,128)}, u32[]{:S(2)}, u32[]{:S(2)}) collective-permute-start(f32[8,8,1664]{2,1,0:T(8,128)} %get-tuple-element.77), channel_id=1, source_target_pairs={{0,10},{1,11},{16,26},{17,27},{32,42},{33,43},{48,58},{49,59},{64,... | collective-permute-start | bytes 1277960 | tf_op jit(solution)/shard_map/ppermute | solution.py:334
  78.1 12.8 %collective-permute-start.4 = (f32[8,8,1664]{2,1,0:T(8,128)}, f32[8,8,1664]{2,1,0:T(8,128)S(1)}, u32[]{:S(2)}, u32[]{:S(2)}) collective-permute-start(f32[8,8,1664]{2,1,0:T(8,128)} %get-tuple-element.73), channel_id=1, source_target_pairs={{0,2},{1,3},{16,18},{17,19},{32,34},{33,35},{48,50},{49,51},{64,66... | collective-permute-start | bytes 1277960 | tf_op jit(solution)/shard_map/ppermute | solution.py:334
  78.8 12.1 %collective-permute-start.5 = (f32[8,8,1664]{2,1,0:T(8,128)}, f32[8,8,1664]{2,1,0:T(8,128)S(1)}, u32[]{:S(2)}, u32[]{:S(2)}) collective-permute-start(f32[8,8,1664]{2,1,0:T(8,128)} %get-tuple-element.74), channel_id=1, source_target_pairs={{0,4},{1,5},{16,20},{17,21},{32,36},{33,37},{48,52},{49,53},{64,68... | collective-permute-start | bytes 1277960 | tf_op jit(solution)/shard_map/ppermute | solution.py:334
  79.5 31.2 %collective-permute-start.6 = (f32[8,8,1664]{2,1,0:T(8,128)}, f32[8,8,1664]{2,1,0:T(8,128)S(1)}, u32[]{:S(2)}, u32[]{:S(2)}) collective-permute-start(f32[8,8,1664]{2,1,0:T(8,128)} %get-tuple-element.75), channel_id=1, source_target_pairs={{0,6},{1,7},{16,22},{17,23},{32,38},{33,39},{48,54},{49,55},{64,70... | collective-permute-start | bytes 1277960 | tf_op jit(solution)/shard_map/ppermute | solution.py:334
  81.0 29.7 %collective-permute-start.9 = (f32[8,8,1664]{2,1,0:T(8,128)}, f32[8,8,1664]{2,1,0:T(8,128)S(1)}, u32[]{:S(2)}, u32[]{:S(2)}) collective-permute-start(f32[8,8,1664]{2,1,0:T(8,128)} %get-tuple-element.78), channel_id=1, source_target_pairs={{0,12},{1,13},{16,28},{17,29},{32,44},{33,45},{48,60},{49,61},{64,... | collective-permute-start | bytes 1277960 | tf_op jit(solution)/shard_map/ppermute | solution.py:334
  81.7 29.0 %collective-permute-start.10 = (f32[8,8,1664]{2,1,0:T(8,128)}, f32[8,8,1664]{2,1,0:T(8,128)S(1)}, u32[]{:S(2)}, u32[]{:S(2)}) collective-permute-start(f32[8,8,1664]{2,1,0:T(8,128)} %get-tuple-element.79), channel_id=1, source_target_pairs={{0,14},{1,15},{16,30},{17,31},{32,46},{33,47},{48,62},{49,63},{64,... | collective-permute-start | bytes 1277960 | tf_op jit(solution)/shard_map/ppermute | solution.py:334
  82.4 39.3 %all-to-all-start = ((f32[8,16,1536]{2,1,0:T(8,128)}), f32[8,16,1536]{2,1,0:T(8,128)S(1)}, u32[]{:S(2)}, u32[]{:S(2)}) async-start(f32[8,16,1536]{2,1,0:T(8,128)} %get-tuple-element.81), calls=%async_computation | async-start | bytes 1572864 | tf_op jit(solution)/shard_map/all_to_all | solution.py:327
  90.8 108.3 %all-gather.6.cloned.1.call-start = ((), (), s32[]{:S(2)}) async-start(), calls=%async_computation.3 | async-start | bytes 8912896 | tf_op jit(solution)/shard_map/all_gather | solution.py:344
  112.0 0.8 copy-start.7
  112.8 31.5 %copy-start.9 = (s32[3,1]{0,1:T(1,128)S(1)}, s32[3,1]{0,1:T(1,128)}, u32[]{:S(2)}) copy-start(s32[3,1]{0,1:T(1,128)} %param.13) | copy-start | bytes 40
  121.7 18.9 %copy-start.4 = (f32[8,16,1536]{2,1,0:T(8,128)}, f32[8,16,1536]{2,1,0:T(8,128)S(1)}, u32[]{:S(2)}) copy-start(f32[8,16,1536]{2,1,0:T(8,128)S(1)} %all-to-all-done.refs_1_) | copy-start | bytes 2359300
  140.6 67.5 %all-to-all-start.2 = ((f32[8,48,1536]{2,1,0:T(8,128)}), f32[8,48,1536]{2,1,0:T(8,128)S(1)}, u32[]{:S(2)}, u32[]{:S(2)}) async-start(f32[8,48,1536]{2,1,0:T(8,128)} %get-tuple-element.83), calls=%async_computation.2 | async-start | bytes 4718592 | tf_op jit(solution)/shard_map/all_to_all | solution.py:327
  145.0 1.2 collective-permute-start.11
  208.1 1.5 copy-start.3
Sparse Core Ops, SparseCore 0:
  9.1 44.1 all-gather.7
  70.1 61.4 all-gather.9
  140.7 58.4 all-gather.5

commit v9 on v8

--- a/solution.py
+++ b/solution.py
@@ -194,23 +194,19 @@
     )(flags, gathered, inverse, panels)
 
 
-def update_kernel(flags, *refs):
-    part_refs, (panels_ref, first_ref, second_ref, fixed_ref, out_ref) = refs[:-5], refs[-5:]
+def update_kernel(flags, panels_ref, first_ref, second_ref, fixed_ref, out_ref):
     tile = pl.program_id(0)
-    keep, use_first, use_fixed, use_second = (flags[4 * tile + i] == 1 for i in range(4))
+    use_first, use_fixed, use_second = (flags[4 * tile + i] == 1 for i in range(1, 4))
     left0 = first_ref[...] - jnp.where(use_fixed, fixed_ref[...], 0.0)
     left0 = halves(jnp.where(use_first, left0, 0.0))
     left1 = halves(jnp.where(use_second, second_ref[...], 0.0))
     panel = panels_ref[...]
     right0 = halves(panel[:, 0].reshape(PANEL, PANEL))
     right1 = halves(panel[:, 1].reshape(PANEL, PANEL))
-    update = product(left0, right0, PLAIN) + product(left1, right1, PLAIN)
-    block = jnp.concatenate([part[...] for part in part_refs], axis=1).reshape(PANEL, PANEL)
-    out_ref[...] = (jnp.where(keep, block, 0.0) - update).T
-
-
-def update(flags, parts, panels, first, second, fixed):
-    rows = parts[0].shape[2]
+    out_ref[...] = (product(left0, right0, PLAIN) + product(left1, right1, PLAIN)).T
+
+
+def update(flags, rows, panels, first, second, fixed):
     square = pl.BlockSpec((PANEL, PANEL), lambda i, _: (0, 0))
     return pl.pallas_call(
         update_kernel,
@@ -218,17 +214,31 @@
         grid_spec=pltpu.PrefetchScalarGridSpec(
             num_scalar_prefetch=1,
             grid=(rows // PANEL,),
-            in_specs=[pl.BlockSpec(part.shape[:2] + (PANEL,), lambda i, _: (0, 0, i)) for part in parts]
-            + [
-                pl.BlockSpec(panels.shape[:3] + (PANEL,), lambda i, _: (0, 0, 0, i)),
-                square,
-                square,
-                square,
-            ],
+            in_specs=[pl.BlockSpec(panels.shape[:3] + (PANEL,), lambda i, _: (0, 0, 0, i)), square, square, square],
             out_specs=pl.BlockSpec((PANEL, PANEL), lambda i, _: (i, 0)),
         ),
         compiler_params=pltpu.CompilerParams(vmem_limit_bytes=VMEM_BYTES),
-    )(flags, *parts, panels, first, second, fixed)
+    )(flags, panels, first, second, fixed)
+
+
+def finish_kernel(flags, block_ref, update_ref, out_ref):
+    keep = flags[4 * pl.program_id(0)] == 1
+    out_ref[...] = jnp.where(keep, block_ref[...], 0.0).T - update_ref[...]
+
+
+def finish(flags, block, lost):
+    tile = pl.BlockSpec((PANEL, PANEL), lambda i, _: (i, 0))
+    return pl.pallas_call(
+        finish_kernel,
+        out_shape=jax.ShapeDtypeStruct(lost.shape, jnp.float32),
+        grid_spec=pltpu.PrefetchScalarGridSpec(
+            num_scalar_prefetch=1,
+            grid=(lost.shape[0] // PANEL,),
+            in_specs=[pl.BlockSpec((PANEL, PANEL), lambda i, _: (0, i)), tile],
+            out_specs=tile,
+        ),
+        compiler_params=pltpu.CompilerParams(vmem_limit_bytes=VMEM_BYTES),
+    )(flags, block, lost)
 
 
 def local(front_entries, child_blocks, row_maps, pivot_inverses, tile_mask):
@@ -328,6 +338,8 @@
     order = list(range(chunks))
     middle = chunks // 2
     order[middle : middle + 2], order[-2:] = order[-2:], order[middle : middle + 2]
+    whole = jnp.concatenate(wholes[::-1], axis=1)
+    pieces[order[1]], whole = lax.optimization_barrier((pieces[order[1]], whole))
     mine = jnp.where(place // PANELS == 0, pieces[order[0]], 0.0)
     for chip in range(1, chunks):
         pairs = [(k, PANELS * chip + k) for k in range(PANELS)]
@@ -338,13 +350,11 @@
     cross_mask = jnp.where(core0, masks_there, tails[PANEL // LANES])[0, : tile_mask.shape[0]] > 0.5
     corner = tails[: PANEL // LANES].transpose(1, 0, 2).reshape(1, 8, PANEL)
     mine = jnp.concatenate([mine[:, :, :row_count], jnp.broadcast_to(corner, (grid_rows, 8, PANEL))], axis=2)
-    moved = [across(wholes[0])]
-    mine, moved[0] = lax.optimization_barrier((mine, moved[0]))
     mine = across(mine)
     panels = lax.all_gather(mine.reshape(thin, -1), "col", axis=0, tiled=True)
     panels = panels.reshape(chunks, PANELS, thin, -1)
-    last, mine = lax.optimization_barrier((wholes[1], mine))
-    moved.append(across(last))
+    whole, mine = lax.optimization_barrier((whole, mine))
+    block = across(whole).reshape(PANEL, row_count)
 
     first, second, fixed = factor(
         order, jnp.stack([place, kept.astype(place.dtype)]).astype(jnp.int32), gathered, inverse, panels
@@ -359,7 +369,8 @@
     use_fixed = jnp.where(is0, False, cross_mask & (tile_ids >= jnp.where(is1, 1, 2)))
     use_second = jnp.where(is0, False, jnp.where(is1, tile_ids >= 1, own_mask & (tile_ids >= 2)))
     flags = jnp.stack([keep, use_first, use_fixed, use_second], axis=1).astype(jnp.int32).reshape(-1)
-    return update(flags, moved[::-1], panels, first, second, fixed)
+    lost = update(flags, row_count, panels, first, second, fixed)
+    return finish(flags, block, lost)
 
 
 def solution(mesh):

time: 229 us -> 224 us (0.978)
  waiting for transfers between devices: 95.3 us -> 86.8 us
  starting transfers between devices: 25.2 us -> 16.8 us
  Pallas kernels: 47.2 us -> 52.8 us
  blocking collectives: 18.9 us -> 23.3 us
  other arithmetic: 16.6 us -> 20.2 us
    all_gather x1, waiting for transfers between devices: 48.8 us -> 39.9 us  [local(): panels = lax.all_gather(mine.reshape(thin, -1), 'col', axis=0, tiled=True)]
    all_to_all x2 -> x1, starting transfers between devices: 12.2 us -> 3.66 us  [local(): lax.all_to_all(x, 'row', split_axis=0, concat_axis=0, tiled=True)]
    pallas_call x0 -> x1, Pallas kernels: none -> 6.24 us  [finish(): pl.pallas_call(finish_kernel, out_shape=jax.ShapeDtypeStruct(lost.shape,...]
    ppermute x7, waiting for transfers between devices: 19.8 us -> 24.6 us  [local(): mine = mine + lax.ppermute(pieces[order[chip]], 'col', pairs)]
    all_to_all x2 -> x1, waiting for transfers between devices: 8.87 us -> 4.44 us  [local(): lax.all_to_all(x, 'row', split_axis=0, concat_axis=0, tiled=True)]
    all_to_all x1, blocking collectives: 18.9 us -> 23.3 us  [local(): lax.all_to_all(x, 'row', split_axis=0, concat_axis=0, tiled=True)]
    concatenate x0 -> x1, other arithmetic: none -> 3.63 us  [local(): whole = jnp.concatenate(wholes[::-1], axis=1)]
  transfers between devices with their start and end apart: 16 -> 15, of which waited for: 6 -> 6; matrix products, arithmetic and copies ran while one was open for 10% -> 12% of each run, Pallas kernels for 16% -> 21%
where the time goes in v9:
time: 224 us; the launch traced here: 223 us
  waiting for transfers between devices  86.8 us (39%)
  Pallas kernels  52.8 us (24%)
  blocking collectives  23.3 us (10%)
  other arithmetic  20.2 us (9%)
  starting transfers between devices  16.8 us (8%)
  between operations  15.3 us (7%)
  local copies, waits for them, and re-layouts  7.93 us (4%)
    all_gather x1, waiting for transfers between devices, local(): panels = lax.all_gather(mine.reshape(thin, -1), 'col', axis=0, tiled=True)  39.9 us
    ppermute x7, waiting for transfers between devices, local(): mine = mine + lax.ppermute(pieces[order[chip]], 'col', pairs)  24.6 us
    all_to_all x1, blocking collectives, local(): lax.all_to_all(x, 'row', split_axis=0, concat_axis=0, tiled=True)  23.3 us
    pallas_call x5, Pallas kernels, extend_add(): pl.pallas_call(functools.partial(extend_kernel, first_place, map_blocks),...  20.2 us
    ppermute x3, waiting for transfers between devices, local(): exchange = lambda x: lax.ppermute(x, 'subcube', [(0, 1), (1, 0)])  16 us
    pallas_call x1, Pallas kernels, update(): pl.pallas_call(update_kernel, out_shape=jax.ShapeDtypeStruct((rows, PANEL...  10.2 us
    pallas_call x1, Pallas kernels, factor(): pl.pallas_call(functools.partial(factor_kernel, order), out_shape=(square...  8.98 us
    ppermute x7, starting transfers between devices, local(): mine = mine + lax.ppermute(pieces[order[chip]], 'col', pairs)  7.2 us
  transfers between devices with their start and end apart: 15, of which 6 were waited for; matrix products, arithmetic and copies ran while one was open for 12% of the time, Pallas kernels for 21%

profile of v9, /device:TPU:10, one launch (start us, length us, event | category | flops | bytes accessed | tf_op | source)
XLA Modules:
  0.0 223.1 jit_solution(2434702568581127114)
XLA Ops:
  6.5 0.7 all-gather.8.cloned.1.call-update
  7.3 0.7 convert_bitcast_fusion
  8.0 1.2 convert_reduce_fusion.1
  9.2 1.5 copy.11
  12.0 2.9 %shard_map.56.places_ref = s32[16,128]{1,0:T(8,128)} custom-call(s32[20]{0:T(128)} %concatenate.42.scalars, s32[2,96,128]{2,1,0:T(8,128)} %bitcast.66), custom_call_target="tpu_custom_call" | custom-call | tf_op jit(solution)/shard_map/pallas_call | solution.py:53
  14.9 2.9 %shard_map.57 = f32[1,64,1024]{2,1,0:T(8,128)} custom-call(s32[9]{0:T(128)} %pad_add_fusion.3.scalars, s32[16,128]{1,0:T(8,128)} %shard_map.56.places_ref, f32[64,12288]{1,0:T(8,128)} %bitcast.57, f32[64,12288]{1,0:T(8,128)} %bitcast.47), custom_call_target="tpu_custom_call" | custom-call | tf_op jit(solution)/shard_map/pallas_call | solution.py:127
  17.8 1.0 bitcast_select_fusion.1
  18.8 0.8 pad_maximum_fusion.2
  19.5 2.3 %collective-permute-start.1 = (f32[72,1024]{1,0:T(8,128)}, f32[72,1024]{1,0:T(8,128)}, u32[]{:S(2)}, u32[]{:S(2)}) collective-permute-start(f32[72,1024]{1,0:T(8,128)} %pad_maximum_fusion.2), channel_id=1, source_target_pairs={{0,128},{128,0},{1,129},{129,1},{2,130},{130,2},{3,131},{131,3},{4... | collective-permute-start | bytes 884744 | tf_op jit(solution)/shard_map/ppermute | solution.py:257
  21.8 0.8 slice_select_fusion.2
  22.6 1.2 collective-permute-start.2
  24.3 1.1 convert_reduce_fusion
  25.4 1.2 slice_select_fusion.1
  29.0 4.3 %shard_map.55.places_ref = s32[192,128]{1,0:T(8,128)S(1)} custom-call(s32[196]{0:T(256)} %concatenate.40.scalars, s32[2,96,128]{2,1,0:T(8,128)} %bitcast.67), custom_call_target="tpu_custom_call" | custom-call | tf_op jit(solution)/shard_map/pallas_call | solution.py:53
  33.8 4.8 %shard_map.58 = f32[8,64,1536]{2,1,0:T(8,128)} custom-call(s32[97]{0:T(128)} %get-tuple-element.103.scalars, s32[192,128]{1,0:T(8,128)S(1)} %shard_map.55.places_ref, f32[64,12288]{1,0:T(8,128)} %bitcast.58, f32[64,12288]{1,0:T(8,128)S(1)} %bitcast.51), custom_call_target="tpu_custom_call" | custom-call | tf_op jit(solution)/shard_map/pallas_call | solution.py:127
  39.2 2.3 %collective-permute-start.3 = (f32[48,6656]{1,0:T(8,128)}, f32[48,6656]{1,0:T(8,128)}, u32[]{:S(2)}, u32[]{:S(2)}) collective-permute-start(f32[48,6656]{1,0:T(8,128)} %slice_select_fusion.1), channel_id=1, source_target_pairs={{0,128},{128,0},{1,129},{129,1},{2,130},{130,2},{3,131},{131,3},{4... | collective-permute-start | bytes 3833864 | tf_op jit(solution)/shard_map/ppermute | solution.py:257
  42.1 1.8 slice_select_fusion.3
  43.9 2.9 %shard_map.59 = f32[1,64,1024]{2,1,0:T(8,128)} custom-call(s32[9]{0:T(128)} %pad_add_fusion.2.scalars, s32[16,128]{1,0:T(8,128)} %shard_map.56.places_ref, f32[64,1024]{1,0:T(8,128)} %get-tuple-element.91.front_ref, f32[64,1024]{1,0:T(8,128)} %get-tuple-element.90.source_ref), custom_call_target="tpu_custom_call" | custom-call | tf_op jit(solution)/shard_map/pallas_call | solution.py:127
  46.8 1.0 slice_select_fusion.4
  47.9 0.7 pad_maximum_fusion.4.refs_0_
  48.6 4.4 %shard_map.60 = (f32[8,16,1536]{2,1,0:T(8,128)}, f32[8,8,1664]{2,1,0:T(8,128)}, f32[8,8,1664]{2,1,0:T(8,128)}) custom-call(s32[97]{0:T(128)} %get-tuple-element.102.scalars, s32[192,128]{1,0:T(8,128)S(1)} %shard_map.55.places_ref, f32[8,64,1536]{2,1,0:T(8,128)} %get-tuple-element.104.front_ref, f32[16,6656]{1,0:T(8,128)} %collective-permute-done.2.source_ref, ...), custom_call_target="tpu_custom_call" | custom-call | tf_op jit(solution)/shard_map/pallas_call | solution.py:127
  53.0 0.8 slice_select_fusion.5
  53.8 0.7 pad_maximum_fusion.3
  54.5 15.5 %collective-permute-done.3.source_ref = f32[48,6656]{1,0:T(8,128)} collective-permute-done((f32[48,6656]{1,0:T(8,128)}, f32[48,6656]{1,0:T(8,128)}, u32[]{:S(2)}, u32[]{:S(2)}) %collective-permute-start.3) | collective-permute-done | bytes 1277984 | tf_op jit(solution)/shard_map/ppermute | solution.py:257
  70.1 1.6 collective-permute-start.7
  71.6 1.4 collective-permute-start.8
  73.1 5.2 %shard_map.61 = (f32[8,48,1536]{2,1,0:T(8,128)}, f32[8,8,1664]{2,1,0:T(8,128)}, f32[8,8,1664]{2,1,0:T(8,128)}, f32[8,8,1664]{2,1,0:T(8,128)}, f32[8,8,1664]{2,1,...) custom-call(s32[97]{0:T(128)} %get-tuple-element.102.scalars, s32[192,128]{1,0:T(8,128)S(1)} %shard_map.55.places_ref, ...), custom_call_target="tpu_custom_call" | custom-call | tf_op jit(solution)/shard_map/pallas_call | solution.py:127
  78.3 0.7 collective-permute-start.5
  79.0 1.5 collective-permute-start.6
  80.4 0.7 collective-permute-start.9
  81.2 3.6 %pad_maximum_fusion = f32[8,64,1536]{2,1,0:T(8,128)} fusion(f32[8,16,1536]{2,1,0:T(8,128)S(1)} %copy-done.8, f32[8,48,1536]{2,1,0:T(8,128)} %get-tuple-element.74), kind=kLoop, calls=%fused_computation.3 | loop fusion | flops 786432 | bytes 6291456 | tf_op jit(solution)/shard_map/concatenate | solution.py:341
  84.8 0.7 collective-permute-start.10
  85.5 0.7 collective-permute-start.4
  86.2 24.6 %collective-permute-done.6 = f32[8,8,1664]{2,1,0:T(8,128)S(1)} collective-permute-done((f32[8,8,1664]{2,1,0:T(8,128)}, f32[8,8,1664]{2,1,0:T(8,128)S(1)}, u32[]{:S(2)}, u32[]{:S(2)}) %collective-permute-start.6) | collective-permute-done | bytes 426016 | tf_op jit(solution)/shard_map/ppermute | solution.py:346
  110.9 1.3 add_add_fusion
  112.3 23.3 %all_to_all.10 = f32[8,8,2048]{2,1,0:T(8,128)} all-to-all(f32[8,8,2048]{2,1,0:T(8,128)S(1)} %pad_maximum_fusion.1), channel_id=1, replica_groups=mesh['subcube'=2,'row'=8,'col'=16] {'row'}, dimensions={0} | all-to-all | bytes 1048576 | tf_op jit(solution)/shard_map/all_to_all | solution.py:337
  135.6 3.7 %all-to-all-start.1 = ((f32[8,64,1536]{2,1,0:T(8,128)}), f32[8,64,1536]{2,1,0:T(8,128)S(1)}, u32[]{:S(2)}, u32[]{:S(2)}) async-start(f32[8,64,1536]{2,1,0:T(8,128)} %pad_maximum_fusion), calls=%async_computation.1 | async-start | bytes 6291456 | tf_op jit(solution)/shard_map/all_to_all | solution.py:337
  139.3 0.7 slice_bitcast_fusion.1
  140.0 1.1 collective-permute-done.11
  141.1 0.7 broadcast_select_fusion
  141.9 0.7 reshape.131.flags
  142.6 1.3 slice.129
  145.2 39.9 %all-gather.6.cloned.1.call-done = f32[1024,2048]{1,0:T(8,128)} async-done(((f32[64,2048]{1,0:T(8,128)}), f32[1024,2048]{1,0:T(8,128)}) %all-gather.6.cloned.1.call-update) | async-done | bytes 8388624 | tf_op jit(solution)/shard_map/all_gather | solution.py:354
  185.1 9.0 %shard_map.62 = (f32[512,512]{1,0:T(8,128)}, f32[512,512]{1,0:T(8,128)}, f32[512,512]{1,0:T(8,128)}) custom-call(s32[2]{0:T(128)} %pad_add_fusion.6.flags, f32[8,72,1024]{2,1,0:T(8,128)} %bitcast.60, f32[8,2,64,512]{3,2,1,0:T(8,128)} %bitcast.63, f32[8,2,64,2048]{3,2,1,0:T(8,128)} %bitcast.54), custom_call_target="tpu_custom_call" | custom-call | tf_op jit(solution)/shard_map/pallas_call | solution.py:180
  194.1 10.2 %shard_map.63.update_ref = f32[1536,512]{1,0:T(8,128)} custom-call(s32[12]{0:T(128)} %reshape.131.flags, f32[8,2,64,2048]{3,2,1,0:T(8,128)} %bitcast.55, f32[512,512]{1,0:T(8,128)} %get-tuple-element.87.first_ref, f32[512,512]{1,0:T(8,128)} %get-tuple-element.88.second_ref, f32[512,512]{1,0:T(8,128)} %get-tuple-element.89.fixed_ref), custom_call_target="tpu_custom_call" | custom-call | tf_op jit(solution)/shard_map/pallas_call | solution.py:211
  204.2 4.4 %all-to-all-done.1 = f32[8,64,1536]{2,1,0:T(8,128)S(1)} async-done(((f32[8,64,1536]{2,1,0:T(8,128)}), f32[8,64,1536]{2,1,0:T(8,128)S(1)}, u32[]{:S(2)}, u32[]{:S(2)}) %all-to-all-start.1) | async-done | bytes 3145760 | tf_op jit(solution)/shard_map/all_to_all | solution.py:337
  208.7 1.6 copy-done.3
  210.3 6.2 %shard_map.64 = f32[1536,512]{1,0:T(8,128)} custom-call(s32[12]{0:T(128)} %reshape.131.flags, f32[512,1536]{1,0:T(8,128)} %bitcast.56, f32[1536,512]{1,0:T(8,128)} %shard_map.63.update_ref), custom_call_target="tpu_custom_call" | custom-call | tf_op jit(solution)/shard_map/pallas_call | solution.py:231
  (67 shorter events, 5.6 us)
Async XLA Ops:
  6.5 63.4 %all-gather.8.cloned.1.call-start = ((), (), s32[]{:S(2)}) async-start(), calls=%async_computation.3 | async-start | bytes 2359296 | tf_op jit(solution)/shard_map/all_gather | solution.py:259
  7.3 135.4 %all-gather.10.cloned.1.call-start = ((), (), s32[]{:S(2)}) async-start(), calls=%async_computation.4 | async-start | bytes 2654208 | tf_op jit(solution)/shard_map/all_gather | solution.py:332
  14.9 2.9 %copy-start = (f32[1,1,1,64,12288]{4,3,2,1,0:T(8,128)S(1)}, f32[1,1,1,64,12288]{4,3,2,1,0:T(8,128)}, u32[]{:S(2)}) copy-start(f32[1,1,1,64,12288]{4,3,2,1,0:T(8,128)} %param.10) | copy-start | bytes 9437188
  14.9 9.0 %copy-start.7 = (s32[2,12288]{1,0:T(2,128)S(1)}, s32[2,12288]{1,0:T(2,128)}, u32[]{:S(2)}) copy-start(s32[2,12288]{1,0:T(2,128)} %param.11) | copy-start | bytes 294916
  19.5 19.2 %collective-permute-start.1 = (f32[72,1024]{1,0:T(8,128)}, f32[72,1024]{1,0:T(8,128)}, u32[]{:S(2)}, u32[]{:S(2)}) collective-permute-start(f32[72,1024]{1,0:T(8,128)} %pad_maximum_fusion.2), channel_id=1, source_target_pairs={{0,128},{128,0},{1,129},{129,1},{2,130},{130,2},{3,131},{131,3},{4... | collective-permute-start | bytes 884744 | tf_op jit(solution)/shard_map/ppermute | solution.py:257
  22.6 16.6 %collective-permute-start.2 = (f32[16,6656]{1,0:T(8,128)}, f32[16,6656]{1,0:T(8,128)}, u32[]{:S(2)}, u32[]{:S(2)}) collective-permute-start(f32[16,6656]{1,0:T(8,128)} %slice_select_fusion.2), channel_id=1, source_target_pairs={{0,128},{128,0},{1,129},{129,1},{2,130},{130,2},{3,131},{131,3},{4... | collective-permute-start | bytes 1277960 | tf_op jit(solution)/shard_map/ppermute | solution.py:257
  38.7 3.4 %copy-start.5 = (f32[1,64,1024]{2,1,0:T(8,128)S(1)}, f32[1,64,1024]{2,1,0:T(8,128)}, u32[]{:S(2)}) copy-start(f32[1,64,1024]{2,1,0:T(8,128)} %shard_map.57) | copy-start | bytes 786436
  39.2 30.8 %collective-permute-start.3 = (f32[48,6656]{1,0:T(8,128)}, f32[48,6656]{1,0:T(8,128)}, u32[]{:S(2)}, u32[]{:S(2)}) collective-permute-start(f32[48,6656]{1,0:T(8,128)} %slice_select_fusion.1), channel_id=1, source_target_pairs={{0,128},{128,0},{1,129},{129,1},{2,130},{130,2},{3,131},{131,3},{4... | collective-permute-start | bytes 3833864 | tf_op jit(solution)/shard_map/ppermute | solution.py:257
  43.9 29.1 %copy-start.2 = (f32[8,64,1536]{2,1,0:T(8,128)S(1)}, f32[8,64,1536]{2,1,0:T(8,128)}, u32[]{:S(2)}) copy-start(f32[8,64,1536]{2,1,0:T(8,128)} %get-tuple-element.104.front_ref) | copy-start | bytes 9437188
  46.8 7.0 %copy-start.4 = (f32[1,64,1024]{2,1,0:T(8,128)S(1)}, f32[1,64,1024]{2,1,0:T(8,128)}, u32[]{:S(2)}) copy-start(f32[1,64,1024]{2,1,0:T(8,128)} %shard_map.59) | copy-start | bytes 786436
  70.0 115.1 %all-gather.6.cloned.1.call-start = ((), (), s32[]{:S(2)}) async-start(), calls=%async_computation.2 | async-start | bytes 8912896 | tf_op jit(solution)/shard_map/all_gather | solution.py:354
  70.0 11.1 %copy-start.8 = (f32[8,16,1536]{2,1,0:T(8,128)S(1)}, f32[8,16,1536]{2,1,0:T(8,128)}, u32[]{:S(2)}) copy-start(f32[8,16,1536]{2,1,0:T(8,128)} %get-tuple-element.75) | copy-start | bytes 2359300
  70.1 14.8 %collective-permute-start.7 = (f32[8,8,1664]{2,1,0:T(8,128)}, f32[8,8,1664]{2,1,0:T(8,128)}, u32[]{:S(2)}, u32[]{:S(2)}) collective-permute-start(f32[8,8,1664]{2,1,0:T(8,128)} %get-tuple-element.79), channel_id=1, source_target_pairs={{0,8},{1,9},{16,24},{17,25},{32,40},{33,41},{48,56},{49,57},{64,72... | collective-permute-start | bytes 1277960 | tf_op jit(solution)/shard_map/ppermute | solution.py:346
  71.6 13.9 %collective-permute-start.8 = (f32[8,8,1664]{2,1,0:T(8,128)}, f32[8,8,1664]{2,1,0:T(8,128)}, u32[]{:S(2)}, u32[]{:S(2)}) collective-permute-start(f32[8,8,1664]{2,1,0:T(8,128)} %get-tuple-element.80), channel_id=1, source_target_pairs={{0,10},{1,11},{16,26},{17,27},{32,42},{33,43},{48,58},{49,59},{64,... | collective-permute-start | bytes 1277960 | tf_op jit(solution)/shard_map/ppermute | solution.py:346
  78.3 8.0 %collective-permute-start.5 = (f32[8,8,1664]{2,1,0:T(8,128)}, f32[8,8,1664]{2,1,0:T(8,128)S(1)}, u32[]{:S(2)}, u32[]{:S(2)}) collective-permute-start(f32[8,8,1664]{2,1,0:T(8,128)} %get-tuple-element.77), channel_id=1, source_target_pairs={{0,4},{1,5},{16,20},{17,21},{32,36},{33,37},{48,52},{49,53},{64,68... | collective-permute-start | bytes 1277960 | tf_op jit(solution)/shard_map/ppermute | solution.py:346
  79.0 31.9 %collective-permute-start.6 = (f32[8,8,1664]{2,1,0:T(8,128)}, f32[8,8,1664]{2,1,0:T(8,128)S(1)}, u32[]{:S(2)}, u32[]{:S(2)}) collective-permute-start(f32[8,8,1664]{2,1,0:T(8,128)} %get-tuple-element.78), channel_id=1, source_target_pairs={{0,6},{1,7},{16,22},{17,23},{32,38},{33,39},{48,54},{49,55},{64,70... | collective-permute-start | bytes 1277960 | tf_op jit(solution)/shard_map/ppermute | solution.py:346
  80.4 30.4 %collective-permute-start.9 = (f32[8,8,1664]{2,1,0:T(8,128)}, f32[8,8,1664]{2,1,0:T(8,128)S(1)}, u32[]{:S(2)}, u32[]{:S(2)}) collective-permute-start(f32[8,8,1664]{2,1,0:T(8,128)} %get-tuple-element.81), channel_id=1, source_target_pairs={{0,12},{1,13},{16,28},{17,29},{32,44},{33,45},{48,60},{49,61},{64,... | collective-permute-start | bytes 1277960 | tf_op jit(solution)/shard_map/ppermute | solution.py:346
  81.2 3.7 %copy-start.12 = (f32[8,8,1664]{2,1,0:T(8,128)S(1)}, f32[8,8,1664]{2,1,0:T(8,128)}, u32[]{:S(2)}) copy-start(f32[8,8,1664]{2,1,0:T(8,128)} %get-tuple-element.82) | copy-start | bytes 1277956
  81.2 4.4 %copy-start.11 = (f32[8,8,1664]{2,1,0:T(8,128)S(1)}, f32[8,8,1664]{2,1,0:T(8,128)}, u32[]{:S(2)}) copy-start(f32[8,8,1664]{2,1,0:T(8,128)} %get-tuple-element.76) | copy-start | bytes 1277956
  81.2 29.7 %copy-start.9 = (f32[8,8,1664]{2,1,0:T(8,128)S(1)}, f32[8,8,1664]{2,1,0:T(8,128)}, u32[]{:S(2)}) copy-start(f32[8,8,1664]{2,1,0:T(8,128)} %get-tuple-element.72) | copy-start | bytes 1277956
  84.8 26.0 %collective-permute-start.10 = (f32[8,8,1664]{2,1,0:T(8,128)S(1)}, f32[8,8,1664]{2,1,0:T(8,128)S(1)}, u32[]{:S(2)}, u32[]{:S(2)}) collective-permute-start(f32[8,8,1664]{2,1,0:T(8,128)S(1)} %copy-done.12), channel_id=1, source_target_pairs={{0,14},{1,15},{16,30},{17,31},{32,46},{33,47},{48,62},{49,63},{64,... | collective-permute-start | bytes 1277960 | tf_op jit(solution)/shard_map/ppermute | solution.py:346
  85.5 25.3 %collective-permute-start.4 = (f32[8,8,1664]{2,1,0:T(8,128)S(1)}, f32[8,8,1664]{2,1,0:T(8,128)S(1)}, u32[]{:S(2)}, u32[]{:S(2)}) collective-permute-start(f32[8,8,1664]{2,1,0:T(8,128)S(1)} %copy-done.11), channel_id=1, source_target_pairs={{0,2},{1,3},{16,18},{17,19},{32,34},{33,35},{48,50},{49,51},{64,66... | collective-permute-start | bytes 1277960 | tf_op jit(solution)/shard_map/ppermute | solution.py:346
  112.2 23.4 %copy-start.6 = (f32[8,8,1664]{2,1,0:T(8,128)}, f32[8,8,1664]{2,1,0:T(8,128)S(1)}, u32[]{:S(2)}) copy-start(f32[8,8,1664]{2,1,0:T(8,128)S(1)} %add_add_fusion) | copy-start | bytes 1277956
  135.6 3.7 %copy-start.10 = (s32[3,1]{0,1:T(1,128)S(1)}, s32[3,1]{0,1:T(1,128)}, u32[]{:S(2)}) copy-start(s32[3,1]{0,1:T(1,128)} %param.13) | copy-start | bytes 40
  135.6 73.1 %all-to-all-start.1 = ((f32[8,64,1536]{2,1,0:T(8,128)}), f32[8,64,1536]{2,1,0:T(8,128)S(1)}, u32[]{:S(2)}, u32[]{:S(2)}) async-start(f32[8,64,1536]{2,1,0:T(8,128)} %pad_maximum_fusion), calls=%async_computation.1 | async-start | bytes 6291456 | tf_op jit(solution)/shard_map/all_to_all | solution.py:337
  140.0 1.2 collective-permute-start.11
  208.7 1.6 copy-start.3
Sparse Core Ops, SparseCore 0:
  9.1 43.9 all-gather.7
  70.1 44.5 all-gather.9
  135.7 49.3 all-gather.5

commit v10 on v9

--- a/solution.py
+++ b/solution.py
@@ -271,16 +271,10 @@
     maps = row_maps.reshape(2, map_blocks, LANES)
     count = lambda maps, edges: jnp.sum((maps[:, None, :] < edges[None, :, None]).astype(jnp.int32), axis=2)
     edges = LANES * jnp.arange(blocks, dtype=jnp.int32)
-    strip_starts = count(row_maps, edges[:strip_blocks])
-    strip_places = search(maps, [zero, zero + 1], [zero, zero], [strip_starts[0], strip_starts[1]])
-    strip_add = lambda base, child, t: extend_add(
-        base, child, strip_places, t * strip_blocks, strip_starts[t], zero, map_blocks, 1, pivot_rows
-    )[0]
+    strip_starts = count(row_maps[1:], edges[:strip_blocks])[0]
     mask_rows = jnp.zeros((8, pivot_rows), jnp.float32)
     mask_rows = mask_rows.at[0, : tile_mask.shape[0]].set(tile_mask.astype(jnp.float32)[:, 0])
     prefix = own[:, :pivot_rows]
-    base = strip_add(front, own, 0)
-    got = exchange(jnp.concatenate([jnp.where(side == 0, base, prefix), mask_rows]))
 
     first_row = (side * half_rows).astype(jnp.int32)
     own_map = lax.dynamic_index_in_dim(row_maps, side, 0, keepdims=False)
@@ -288,9 +282,9 @@
     starts = count(jnp.stack([own_map, other_map]), first_row + edges)
     places = search(
         maps,
-        [side.astype(jnp.int32), (1 - side).astype(jnp.int32)],
-        [first_row, first_row],
-        [starts[0], starts[1]],
+        [side.astype(jnp.int32), (1 - side).astype(jnp.int32), zero + 1],
+        [first_row, first_row, zero],
+        [starts[0], starts[1], strip_starts],
     )
     lower = jnp.sum((row_maps < half_rows).astype(jnp.int32), axis=1)
     spill = (child_rows - lower[0] > window) | (lower[1] > window)
@@ -304,11 +298,17 @@
         more = exchange(jnp.where(side == 0, own[:, :rest], own[:, window:]))
         return add_other(base_sum, more, offset=rest_at)
 
+    base = base_sum[0, :, :pivot_rows]
+    strip_sent = jnp.concatenate([jnp.where(side == 0, base, prefix), mask_rows])
+    strip_sent, received[0], last_sent = lax.optimization_barrier((strip_sent, received[0], last_sent))
+    got = exchange(strip_sent)
+    received.append(exchange(last_sent))
     base_sum = lax.cond(spill, add_rest, lambda x: x, base_sum)
 
-    got, received[0], base_sum, last_sent = lax.optimization_barrier((got, received[0], base_sum, last_sent))
-    received.append(exchange(last_sent))
-    strip = strip_add(jnp.where(side == 0, base, got[:thin]), jnp.where(side == 0, got[:thin], prefix), 1)
+    strip = extend_add(
+        jnp.where(side == 0, base, got[:thin]), jnp.where(side == 0, got[:thin], prefix),
+        places, 2 * blocks, strip_starts, zero, map_blocks, 1, pivot_rows,
+    )[0]
     first_masks = jnp.where(side == 0, mask_rows, got[thin:])
 
     corner = jnp.where(place == 0, strip[:, PANEL:], strip[:, :PANEL])

time: 224 us -> 225 us (level)
  Pallas kernels: 52.8 us -> 47.2 us
  waiting for transfers between devices: 86.8 us -> 90.7 us
    pallas_call x5 -> x4, Pallas kernels: 20.2 us -> 17.4 us  [extend_add(): pl.pallas_call(functools.partial(extend_kernel, first_place, map_blocks),...]
    select_n x2, other arithmetic: 1.99 us -> 4.82 us  [local(): jnp.where(side == 0, own[a:b, rest:], own[a:b, :window])]
    pallas_call x2 -> x1, Pallas kernels: 7.15 us -> 4.37 us  [search(): pl.pallas_call(functools.partial(search_kernel, sections), out_shape=jax....]
  transfers between devices with their start and end apart: 15 -> 15, of which waited for: 6 -> 6; matrix products, arithmetic and copies ran while one was open for 12% -> 13% of each run, Pallas kernels for 21% -> 18%
where the time goes in v10:
time: 225 us; the launch traced here: 224 us
  waiting for transfers between devices  90.7 us (40%)
  Pallas kernels  47.2 us (21%)
  blocking collectives  23.6 us (10%)
  other arithmetic  20.8 us (9%)
  starting transfers between devices  16.8 us (7%)
  between operations  15.3 us (7%)
  local copies, waits for them, and re-layouts  10 us (4%)
    all_gather x1, waiting for transfers between devices, local(): panels = lax.all_gather(mine.reshape(thin, -1), 'col', axis=0, tiled=True)  38.4 us
    ppermute x7, waiting for transfers between devices, local(): mine = mine + lax.ppermute(pieces[order[chip]], 'col', pairs)  26.2 us
    all_to_all x1, blocking collectives, local(): lax.all_to_all(x, 'row', split_axis=0, concat_axis=0, tiled=True)  23.6 us
    ppermute x3, waiting for transfers between devices, local(): exchange = lambda x: lax.ppermute(x, 'subcube', [(0, 1), (1, 0)])  17.7 us
    pallas_call x4, Pallas kernels, extend_add(): pl.pallas_call(functools.partial(extend_kernel, first_place, map_blocks),...  17.4 us
    pallas_call x1, Pallas kernels, update(): pl.pallas_call(update_kernel, out_shape=jax.ShapeDtypeStruct((rows, PANEL...  10.2 us
    pallas_call x1, Pallas kernels, factor(): pl.pallas_call(functools.partial(factor_kernel, order), out_shape=(square...  8.98 us
    ppermute x7, starting transfers between devices, local(): mine = mine + lax.ppermute(pieces[order[chip]], 'col', pairs)  7.18 us
  transfers between devices with their start and end apart: 15, of which 6 were waited for; matrix products, arithmetic and copies ran while one was open for 13% of the time, Pallas kernels for 18%

profile of v10, /device:TPU:10, one launch (start us, length us, event | category | flops | bytes accessed | tf_op | source)
XLA Modules:
  0.0 224.5 jit_solution(2301529003624834573)
XLA Ops:
  6.5 0.7 all-gather.8.cloned.1.call-update
  7.3 1.9 slice_select_fusion.2
  9.2 2.3 %collective-permute-start.1 = (f32[16,6656]{1,0:T(8,128)}, f32[16,6656]{1,0:T(8,128)}, u32[]{:S(2)}, u32[]{:S(2)}) collective-permute-start(f32[16,6656]{1,0:T(8,128)} %slice_select_fusion.2), channel_id=1, source_target_pairs={{0,128},{128,0},{1,129},{129,1},{2,130},{130,2},{3,131},{131,3},{4... | collective-permute-start | bytes 1277960 | tf_op jit(solution)/shard_map/ppermute | solution.py:257
  11.6 1.5 copy.11
  13.1 1.2 fusion.5
  14.4 1.1 convert_reduce_fusion
  15.8 0.7 pad_add_fusion.2
  17.1 4.4 %shard_map.55.places_ref = s32[200,128]{1,0:T(8,128)S(1)} custom-call(s32[206]{0:T(256)} %concatenate.34.scalars, s32[2,96,128]{2,1,0:T(8,128)} %bitcast.58), custom_call_target="tpu_custom_call" | custom-call | tf_op jit(solution)/shard_map/pallas_call | solution.py:53
  21.5 4.9 %shard_map.56 = f32[8,64,1536]{2,1,0:T(8,128)S(1)} custom-call(s32[97]{0:T(128)} %get-tuple-element.100.scalars, s32[200,128]{1,0:T(8,128)S(1)} %shard_map.55.places_ref, f32[64,12288]{1,0:T(8,128)} %bitcast.50, f32[64,12288]{1,0:T(8,128)} %bitcast.10.source_ref), custom_call_target="tpu_custom_call" | custom-call | tf_op jit(solution)/shard_map/pallas_call | solution.py:127
  26.4 2.9 %slice_select_fusion.1 = f32[48,6656]{1,0:T(8,128)} fusion(f32[64,12288]{1,0:T(8,128)} %bitcast.10.source_ref, pred[]{:T(512)} %eq.49), kind=kLoop, calls=%fused_computation.4 | loop fusion | flops 319488 | bytes 3833857 | tf_op jit(solution)/shard_map/jit(_where)/select_n | solution.py:265
  29.5 1.0 fusion.1
  30.5 0.7 pad_maximum_fusion.2
  31.2 1.2 collective-permute-start.2
  34.3 2.4 %collective-permute-start.3 = (f32[48,6656]{1,0:T(8,128)}, f32[48,6656]{1,0:T(8,128)}, u32[]{:S(2)}, u32[]{:S(2)}) collective-permute-start(f32[48,6656]{1,0:T(8,128)} %slice_select_fusion.1), channel_id=1, source_target_pairs={{0,128},{128,0},{1,129},{129,1},{2,130},{130,2},{3,131},{131,3},{4... | collective-permute-start | bytes 3833864 | tf_op jit(solution)/shard_map/ppermute | solution.py:257
  36.7 1.7 conditional.1
  36.7 1.7 copy.12
  38.4 1.3 pad_add_fusion.4.scalars
  39.7 3.2 %collective-permute-done.2 = f32[72,1024]{1,0:T(8,128)S(1)} collective-permute-done((f32[72,1024]{1,0:T(8,128)}, f32[72,1024]{1,0:T(8,128)S(1)}, u32[]{:S(2)}, u32[]{:S(2)}) %collective-permute-start.2) | collective-permute-done | bytes 294944 | tf_op jit(solution)/shard_map/ppermute | solution.py:257
  42.9 1.8 slice_select_fusion.3
  44.7 2.9 %shard_map.57 = f32[1,64,1024]{2,1,0:T(8,128)} custom-call(s32[9]{0:T(128)} %pad_add_fusion.4.scalars, s32[200,128]{1,0:T(8,128)S(1)} %shard_map.55.places_ref, f32[64,1024]{1,0:T(8,128)} %get-tuple-element.89.front_ref, f32[64,1024]{1,0:T(8,128)} %get-tuple-element.88.source_ref), custom_call_target="tpu_custom_call" | custom-call | tf_op jit(solution)/shard_map/pallas_call | solution.py:127
  47.5 1.0 slice_select_fusion.4
  48.6 0.7 pad_maximum_fusion.4.refs_0_
  49.3 4.4 %shard_map.58 = (f32[8,16,1536]{2,1,0:T(8,128)}, f32[8,8,1664]{2,1,0:T(8,128)}, f32[8,8,1664]{2,1,0:T(8,128)}) custom-call(s32[97]{0:T(128)} %get-tuple-element.99.scalars, s32[200,128]{1,0:T(8,128)S(1)} %shard_map.55.places_ref, f32[8,64,1536]{2,1,0:T(8,128)} %get-tuple-element.101.front_ref, f32[16,6656]{1,0:T(8,128)} %collective-permute-done.1.source_ref, ...), custom_call_target="tpu_custom_call" | custom-call | tf_op jit(solution)/shard_map/pallas_call | solution.py:127
  53.7 0.7 pad_maximum_fusion.3
  54.4 14.5 %collective-permute-done.3.source_ref = f32[48,6656]{1,0:T(8,128)} collective-permute-done((f32[48,6656]{1,0:T(8,128)}, f32[48,6656]{1,0:T(8,128)}, u32[]{:S(2)}, u32[]{:S(2)}) %collective-permute-start.3) | collective-permute-done | bytes 1277984 | tf_op jit(solution)/shard_map/ppermute | solution.py:257
  69.0 1.6 collective-permute-start.7
  70.5 1.4 collective-permute-start.8
  72.0 5.3 %shard_map.59 = (f32[8,48,1536]{2,1,0:T(8,128)}, f32[8,8,1664]{2,1,0:T(8,128)}, f32[8,8,1664]{2,1,0:T(8,128)}, f32[8,8,1664]{2,1,0:T(8,128)}, f32[8,8,1664]{2,1,...) custom-call(s32[97]{0:T(128)} %get-tuple-element.99.scalars, s32[200,128]{1,0:T(8,128)S(1)} %shard_map.55.places_ref, ...), custom_call_target="tpu_custom_call" | custom-call | tf_op jit(solution)/shard_map/pallas_call | solution.py:127
  77.2 0.7 collective-permute-start.5
  77.9 1.3 collective-permute-start.6
  79.2 0.9 collective-permute-start.9
  80.1 3.6 %pad_maximum_fusion = f32[8,64,1536]{2,1,0:T(8,128)} fusion(f32[8,16,1536]{2,1,0:T(8,128)S(1)} %copy-done.5, f32[8,48,1536]{2,1,0:T(8,128)} %get-tuple-element.72), kind=kLoop, calls=%fused_computation.3 | loop fusion | flops 786432 | bytes 6291456 | tf_op jit(solution)/shard_map/concatenate | solution.py:341
  83.8 0.7 collective-permute-start.10
  84.5 0.7 collective-permute-start.4
  85.2 26.2 %collective-permute-done.6 = f32[8,8,1664]{2,1,0:T(8,128)S(1)} collective-permute-done((f32[8,8,1664]{2,1,0:T(8,128)}, f32[8,8,1664]{2,1,0:T(8,128)S(1)}, u32[]{:S(2)}, u32[]{:S(2)}) %collective-permute-start.6) | collective-permute-done | bytes 426016 | tf_op jit(solution)/shard_map/ppermute | solution.py:346
  111.4 1.3 add_add_fusion
  112.8 23.6 %all_to_all.10 = f32[8,8,2048]{2,1,0:T(8,128)} all-to-all(f32[8,8,2048]{2,1,0:T(8,128)S(1)} %pad_maximum_fusion.1), channel_id=1, replica_groups=mesh['subcube'=2,'row'=8,'col'=16] {'row'}, dimensions={0} | all-to-all | bytes 1048576 | tf_op jit(solution)/shard_map/all_to_all | solution.py:337
  136.5 3.7 %all-to-all-start.1 = ((f32[8,64,1536]{2,1,0:T(8,128)}), f32[8,64,1536]{2,1,0:T(8,128)S(1)}, u32[]{:S(2)}, u32[]{:S(2)}) async-start(f32[8,64,1536]{2,1,0:T(8,128)} %pad_maximum_fusion), calls=%async_computation.1 | async-start | bytes 6291456 | tf_op jit(solution)/shard_map/all_to_all | solution.py:337
  140.2 0.7 slice_bitcast_fusion.2
  140.9 1.1 collective-permute-done.11
  142.1 0.7 broadcast_select_fusion
  143.5 1.2 slice.130
  146.0 38.4 %all-gather.6.cloned.1.call-done = f32[1024,2048]{1,0:T(8,128)} async-done(((f32[64,2048]{1,0:T(8,128)}), f32[1024,2048]{1,0:T(8,128)}) %all-gather.6.cloned.1.call-update) | async-done | bytes 8388624 | tf_op jit(solution)/shard_map/all_gather | solution.py:354
  184.4 9.0 %shard_map.60 = (f32[512,512]{1,0:T(8,128)}, f32[512,512]{1,0:T(8,128)}, f32[512,512]{1,0:T(8,128)}) custom-call(s32[2]{0:T(128)} %pad_add_fusion.5.flags, f32[8,72,1024]{2,1,0:T(8,128)} %bitcast.52, f32[8,2,64,512]{3,2,1,0:T(8,128)} %bitcast.55, f32[8,2,64,2048]{3,2,1,0:T(8,128)} %bitcast.47), custom_call_target="tpu_custom_call" | custom-call | tf_op jit(solution)/shard_map/pallas_call | solution.py:180
  193.3 10.2 %shard_map.61.update_ref = f32[1536,512]{1,0:T(8,128)} custom-call(s32[12]{0:T(128)} %reshape.186.flags, f32[8,2,64,2048]{3,2,1,0:T(8,128)} %bitcast.48, f32[512,512]{1,0:T(8,128)} %get-tuple-element.85.first_ref, f32[512,512]{1,0:T(8,128)} %get-tuple-element.86.second_ref, f32[512,512]{1,0:T(8,128)} %get-tuple-element.87.fixed_ref), custom_call_target="tpu_custom_call" | custom-call | tf_op jit(solution)/shard_map/pallas_call | solution.py:211
  203.5 6.5 %all-to-all-done.1 = f32[8,64,1536]{2,1,0:T(8,128)S(1)} async-done(((f32[8,64,1536]{2,1,0:T(8,128)}), f32[8,64,1536]{2,1,0:T(8,128)S(1)}, u32[]{:S(2)}, u32[]{:S(2)}) %all-to-all-start.1) | async-done | bytes 3145760 | tf_op jit(solution)/shard_map/all_to_all | solution.py:337
  210.0 1.6 copy-done.1
  211.7 6.2 %shard_map.62 = f32[1536,512]{1,0:T(8,128)} custom-call(s32[12]{0:T(128)} %reshape.186.flags, f32[512,1536]{1,0:T(8,128)} %bitcast.49, f32[1536,512]{1,0:T(8,128)} %shard_map.61.update_ref), custom_call_target="tpu_custom_call" | custom-call | tf_op jit(solution)/shard_map/pallas_call | solution.py:231
  (62 shorter events, 3.5 us)
Async XLA Ops:
  6.5 62.4 %all-gather.8.cloned.1.call-start = ((), (), s32[]{:S(2)}) async-start(), calls=%async_computation.3 | async-start | bytes 2359296 | tf_op jit(solution)/shard_map/all_gather | solution.py:259
  7.3 136.3 %all-gather.10.cloned.1.call-start = ((), (), s32[]{:S(2)}) async-start(), calls=%async_computation.4 | async-start | bytes 2654208 | tf_op jit(solution)/shard_map/all_gather | solution.py:332
  9.2 22.0 %collective-permute-start.1 = (f32[16,6656]{1,0:T(8,128)}, f32[16,6656]{1,0:T(8,128)}, u32[]{:S(2)}, u32[]{:S(2)}) collective-permute-start(f32[16,6656]{1,0:T(8,128)} %slice_select_fusion.2), channel_id=1, source_target_pairs={{0,128},{128,0},{1,129},{129,1},{2,130},{130,2},{3,131},{131,3},{4... | collective-permute-start | bytes 1277960 | tf_op jit(solution)/shard_map/ppermute | solution.py:257
  15.8 1.3 copy-start.7
  21.5 4.9 %copy-start.8 = (s32[3,1]{0,1:T(1,128)S(1)}, s32[3,1]{0,1:T(1,128)}, u32[]{:S(2)}) copy-start(s32[3,1]{0,1:T(1,128)} %param.13) | copy-start | bytes 40
  26.3 2.9 %copy-start.4 = (s32[2,12288]{1,0:T(2,128)S(1)}, s32[2,12288]{1,0:T(2,128)}, u32[]{:S(2)}) copy-start(s32[2,12288]{1,0:T(2,128)} %param.11) | copy-start | bytes 294916
  31.2 11.6 %collective-permute-start.2 = (f32[72,1024]{1,0:T(8,128)}, f32[72,1024]{1,0:T(8,128)S(1)}, u32[]{:S(2)}, u32[]{:S(2)}) collective-permute-start(f32[72,1024]{1,0:T(8,128)} %pad_maximum_fusion.2), channel_id=1, source_target_pairs={{0,128},{128,0},{1,129},{129,1},{2,130},{130,2},{3,131},{131,3},{4... | collective-permute-start | bytes 884744 | tf_op jit(solution)/shard_map/ppermute | solution.py:257
  34.3 34.6 %collective-permute-start.3 = (f32[48,6656]{1,0:T(8,128)}, f32[48,6656]{1,0:T(8,128)}, u32[]{:S(2)}, u32[]{:S(2)}) collective-permute-start(f32[48,6656]{1,0:T(8,128)} %slice_select_fusion.1), channel_id=1, source_target_pairs={{0,128},{128,0},{1,129},{129,1},{2,130},{130,2},{3,131},{131,3},{4... | collective-permute-start | bytes 3833864 | tf_op jit(solution)/shard_map/ppermute | solution.py:257
  44.7 27.3 %copy-start = (f32[8,64,1536]{2,1,0:T(8,128)S(1)}, f32[8,64,1536]{2,1,0:T(8,128)}, u32[]{:S(2)}) copy-start(f32[8,64,1536]{2,1,0:T(8,128)} %get-tuple-element.101.front_ref) | copy-start | bytes 9437188
  47.5 6.1 %copy-start.2 = (f32[1,64,1024]{2,1,0:T(8,128)S(1)}, f32[1,64,1024]{2,1,0:T(8,128)}, u32[]{:S(2)}) copy-start(f32[1,64,1024]{2,1,0:T(8,128)} %shard_map.57) | copy-start | bytes 786436
  68.9 115.4 %all-gather.6.cloned.1.call-start = ((), (), s32[]{:S(2)}) async-start(), calls=%async_computation.2 | async-start | bytes 8912896 | tf_op jit(solution)/shard_map/all_gather | solution.py:354
  69.0 11.1 %copy-start.5 = (f32[8,16,1536]{2,1,0:T(8,128)S(1)}, f32[8,16,1536]{2,1,0:T(8,128)}, u32[]{:S(2)}) copy-start(f32[8,16,1536]{2,1,0:T(8,128)} %get-tuple-element.73) | copy-start | bytes 2359300
  69.0 14.8 %collective-permute-start.7 = (f32[8,8,1664]{2,1,0:T(8,128)}, f32[8,8,1664]{2,1,0:T(8,128)}, u32[]{:S(2)}, u32[]{:S(2)}) collective-permute-start(f32[8,8,1664]{2,1,0:T(8,128)} %get-tuple-element.77), channel_id=1, source_target_pairs={{0,8},{1,9},{16,24},{17,25},{32,40},{33,41},{48,56},{49,57},{64,72... | collective-permute-start | bytes 1277960 | tf_op jit(solution)/shard_map/ppermute | solution.py:346
  70.5 13.9 %collective-permute-start.8 = (f32[8,8,1664]{2,1,0:T(8,128)}, f32[8,8,1664]{2,1,0:T(8,128)}, u32[]{:S(2)}, u32[]{:S(2)}) collective-permute-start(f32[8,8,1664]{2,1,0:T(8,128)} %get-tuple-element.78), channel_id=1, source_target_pairs={{0,10},{1,11},{16,26},{17,27},{32,42},{33,43},{48,58},{49,59},{64,... | collective-permute-start | bytes 1277960 | tf_op jit(solution)/shard_map/ppermute | solution.py:346
  77.2 8.0 %collective-permute-start.5 = (f32[8,8,1664]{2,1,0:T(8,128)}, f32[8,8,1664]{2,1,0:T(8,128)S(1)}, u32[]{:S(2)}, u32[]{:S(2)}) collective-permute-start(f32[8,8,1664]{2,1,0:T(8,128)} %get-tuple-element.75), channel_id=1, source_target_pairs={{0,4},{1,5},{16,20},{17,21},{32,36},{33,37},{48,52},{49,53},{64,68... | collective-permute-start | bytes 1277960 | tf_op jit(solution)/shard_map/ppermute | solution.py:346
  77.9 33.5 %collective-permute-start.6 = (f32[8,8,1664]{2,1,0:T(8,128)}, f32[8,8,1664]{2,1,0:T(8,128)S(1)}, u32[]{:S(2)}, u32[]{:S(2)}) collective-permute-start(f32[8,8,1664]{2,1,0:T(8,128)} %get-tuple-element.76), channel_id=1, source_target_pairs={{0,6},{1,7},{16,22},{17,23},{32,38},{33,39},{48,54},{49,55},{64,70... | collective-permute-start | bytes 1277960 | tf_op jit(solution)/shard_map/ppermute | solution.py:346
  79.2 32.2 %collective-permute-start.9 = (f32[8,8,1664]{2,1,0:T(8,128)}, f32[8,8,1664]{2,1,0:T(8,128)S(1)}, u32[]{:S(2)}, u32[]{:S(2)}) collective-permute-start(f32[8,8,1664]{2,1,0:T(8,128)} %get-tuple-element.79), channel_id=1, source_target_pairs={{0,12},{1,13},{16,28},{17,29},{32,44},{33,45},{48,60},{49,61},{64,... | collective-permute-start | bytes 1277960 | tf_op jit(solution)/shard_map/ppermute | solution.py:346
  80.1 3.7 %copy-start.11 = (f32[8,8,1664]{2,1,0:T(8,128)S(1)}, f32[8,8,1664]{2,1,0:T(8,128)}, u32[]{:S(2)}) copy-start(f32[8,8,1664]{2,1,0:T(8,128)} %get-tuple-element.80) | copy-start | bytes 1277956
  80.1 4.4 %copy-start.10 = (f32[8,8,1664]{2,1,0:T(8,128)S(1)}, f32[8,8,1664]{2,1,0:T(8,128)}, u32[]{:S(2)}) copy-start(f32[8,8,1664]{2,1,0:T(8,128)} %get-tuple-element.74) | copy-start | bytes 1277956
  80.1 31.3 %copy-start.6 = (f32[8,8,1664]{2,1,0:T(8,128)S(1)}, f32[8,8,1664]{2,1,0:T(8,128)}, u32[]{:S(2)}) copy-start(f32[8,8,1664]{2,1,0:T(8,128)} %get-tuple-element.70) | copy-start | bytes 1277956
  83.8 27.6 %collective-permute-start.10 = (f32[8,8,1664]{2,1,0:T(8,128)S(1)}, f32[8,8,1664]{2,1,0:T(8,128)S(1)}, u32[]{:S(2)}, u32[]{:S(2)}) collective-permute-start(f32[8,8,1664]{2,1,0:T(8,128)S(1)} %copy-done.11), channel_id=1, source_target_pairs={{0,14},{1,15},{16,30},{17,31},{32,46},{33,47},{48,62},{49,63},{64,... | collective-permute-start | bytes 1277960 | tf_op jit(solution)/shard_map/ppermute | solution.py:346
  84.5 26.9 %collective-permute-start.4 = (f32[8,8,1664]{2,1,0:T(8,128)S(1)}, f32[8,8,1664]{2,1,0:T(8,128)S(1)}, u32[]{:S(2)}, u32[]{:S(2)}) collective-permute-start(f32[8,8,1664]{2,1,0:T(8,128)S(1)} %copy-done.10), channel_id=1, source_target_pairs={{0,2},{1,3},{16,18},{17,19},{32,34},{33,35},{48,50},{49,51},{64,66... | collective-permute-start | bytes 1277960 | tf_op jit(solution)/shard_map/ppermute | solution.py:346
  112.7 23.8 %copy-start.3 = (f32[8,8,1664]{2,1,0:T(8,128)}, f32[8,8,1664]{2,1,0:T(8,128)S(1)}, u32[]{:S(2)}) copy-start(f32[8,8,1664]{2,1,0:T(8,128)S(1)} %add_add_fusion) | copy-start | bytes 1277956
  136.5 3.7 %copy-start.9 = (s32[3,1]{0,1:T(1,128)S(1)}, s32[3,1]{0,1:T(1,128)}, u32[]{:S(2)}) copy-start(s32[3,1]{0,1:T(1,128)} %param.13) | copy-start | bytes 40
  136.5 73.5 %all-to-all-start.1 = ((f32[8,64,1536]{2,1,0:T(8,128)}), f32[8,64,1536]{2,1,0:T(8,128)S(1)}, u32[]{:S(2)}, u32[]{:S(2)}) async-start(f32[8,64,1536]{2,1,0:T(8,128)} %pad_maximum_fusion), calls=%async_computation.1 | async-start | bytes 6291456 | tf_op jit(solution)/shard_map/all_to_all | solution.py:337
  140.9 1.2 collective-permute-start.11
  210.0 1.6 copy-start.1
Sparse Core Ops, SparseCore 0:
  9.1 43.9 all-gather.7
  69.0 43.3 all-gather.9
  136.6 47.7 all-gather.5

commit v11 on v10

--- a/solution.py
+++ b/solution.py
@@ -260,7 +260,7 @@
 
     window = -(-(child_rows * 13 // 24) // LANES) * LANES
     rest = child_rows - window
-    share = thin // 4
+    share = thin // 2
     parts = [(thin - share, thin), (0, thin - share)]
     first_sent, last_sent = [jnp.where(side == 0, own[a:b, rest:], own[a:b, :window]) for a, b in parts]
     received = [exchange(first_sent)]
@@ -335,9 +335,7 @@
     assemble(1)
 
     across = lambda x: lax.all_to_all(x, "row", split_axis=0, concat_axis=0, tiled=True)
-    order = list(range(chunks))
-    middle = chunks // 2
-    order[middle : middle + 2], order[-2:] = order[-2:], order[middle : middle + 2]
+    order = [0, 1] + list(range(chunks // 2, chunks)) + list(range(2, chunks // 2))
     whole = jnp.concatenate(wholes[::-1], axis=1)
     pieces[order[1]], whole = lax.optimization_barrier((pieces[order[1]], whole))
     mine = jnp.where(place // PANELS == 0, pieces[order[0]], 0.0)

time: 225 us -> 215 us (0.956); the launches traced: 224 us -> 210 us
  waiting for transfers between devices: 90.7 us -> 76.3 us
  blocking collectives: 23.6 us -> 26.4 us
    ppermute x7, waiting for transfers between devices: 26.2 us -> 9.54 us  [local(): mine = mine + lax.ppermute(pieces[order[chip]], 'col', pairs)]
    all_gather x1, waiting for transfers between devices: 38.4 us -> 52.2 us  [local(): panels = lax.all_gather(mine.reshape(thin, -1), 'col', axis=0, tiled=True)]
    all_to_all x1, waiting for transfers between devices: 6.51 us -> 0.01 us  [local(): lax.all_to_all(x, 'row', split_axis=0, concat_axis=0, tiled=True)]
    ppermute x3, waiting for transfers between devices: 17.7 us -> 12.7 us  [local(): exchange = lambda x: lax.ppermute(x, 'subcube', [(0, 1), (1, 0)])]
    all_to_all x1, blocking collectives: 23.6 us -> 26.4 us  [local(): lax.all_to_all(x, 'row', split_axis=0, concat_axis=0, tiled=True)]
    select_n x2 -> x1, other arithmetic: 4.82 us -> 3.3 us  [local(): jnp.where(side == 0, own[a:b, rest:], own[a:b, :window])]
  transfers between devices with their start and end apart: 15 -> 15, of which waited for: 6 -> 6; matrix products, arithmetic and copies ran while one was open for 13% -> 12% of each run, Pallas kernels for 18% -> 19%
where the time goes in v11:
time: 215 us; the launch traced here: 210 us
  waiting for transfers between devices  76.3 us (35%)
  Pallas kernels  47 us (22%)
  blocking collectives  26.4 us (12%)
  other arithmetic  19.6 us (9%)
  starting transfers between devices  17.7 us (8%)
  between operations  15.4 us (7%)
  local copies, waits for them, and re-layouts  8.15 us (4%)
    all_gather x1, waiting for transfers between devices, local(): panels = lax.all_gather(mine.reshape(thin, -1), 'col', axis=0, tiled=True)  52.2 us
    all_to_all x1, blocking collectives, local(): lax.all_to_all(x, 'row', split_axis=0, concat_axis=0, tiled=True)  26.4 us
    pallas_call x4, Pallas kernels, extend_add(): pl.pallas_call(functools.partial(extend_kernel, first_place, map_blocks),...  17.2 us
    ppermute x3, waiting for transfers between devices, local(): exchange = lambda x: lax.ppermute(x, 'subcube', [(0, 1), (1, 0)])  12.7 us
    pallas_call x1, Pallas kernels, update(): pl.pallas_call(update_kernel, out_shape=jax.ShapeDtypeStruct((rows, PANEL...  10.2 us
    ppermute x7, waiting for transfers between devices, local(): mine = mine + lax.ppermute(pieces[order[chip]], 'col', pairs)  9.54 us
    pallas_call x1, Pallas kernels, factor(): pl.pallas_call(functools.partial(factor_kernel, order), out_shape=(square...  8.98 us
    ppermute x7, starting transfers between devices, local(): mine = mine + lax.ppermute(pieces[order[chip]], 'col', pairs)  7.93 us
  transfers between devices with their start and end apart: 15, of which 6 were waited for; matrix products, arithmetic and copies ran while one was open for 12% of the time, Pallas kernels for 19%

profile of v11, /device:TPU:10, one launch (start us, length us, event | category | flops | bytes accessed | tf_op | source)
XLA Modules:
  0.0 210.4 jit_solution(17748149661289213524)
XLA Ops:
  6.5 0.7 all-gather.8.cloned.1.call-update
  7.3 3.3 %slice_select_fusion.1 = (f32[32,6656]{1,0:T(8,128)}, f32[32,6656]{1,0:T(8,128)}) fusion(f32[64,12288]{1,0:T(8,128)} %bitcast.10.source_ref, pred[]{:T(512)} %eq.49), kind=kLoop, calls=%fused_computation.4 | loop fusion | flops 425984 | bytes 5111809 | tf_op jit(solution)/shard_map/jit(_where)/select_n | solution.py:265
  10.6 2.3 %collective-permute-start.1 = (f32[32,6656]{1,0:T(8,128)}, f32[32,6656]{1,0:T(8,128)}, u32[]{:S(2)}, u32[]{:S(2)}) collective-permute-start(f32[32,6656]{1,0:T(8,128)} %get-tuple-element.89), channel_id=1, source_target_pairs={{0,128},{128,0},{1,129},{129,1},{2,130},{130,2},{3,131},{131,3},{4... | collective-permute-start | bytes 2555912 | tf_op jit(solution)/shard_map/ppermute | solution.py:257
  13.2 1.1 convert_reduce_fusion
  14.6 0.6 copy.11
  15.9 4.4 %shard_map.55.places_ref = s32[200,128]{1,0:T(8,128)S(1)} custom-call(s32[206]{0:T(256)} %concatenate.34.scalars, s32[2,96,128]{2,1,0:T(8,128)} %bitcast.58), custom_call_target="tpu_custom_call" | custom-call | tf_op jit(solution)/shard_map/pallas_call | solution.py:53
  20.2 0.7 pad_add_fusion.2
  20.9 4.8 %shard_map.56 = f32[8,64,1536]{2,1,0:T(8,128)S(1)} custom-call(s32[97]{0:T(128)} %get-tuple-element.102.scalars, s32[200,128]{1,0:T(8,128)S(1)} %shard_map.55.places_ref, f32[64,12288]{1,0:T(8,128)} %bitcast.50, f32[64,12288]{1,0:T(8,128)} %bitcast.10.source_ref), custom_call_target="tpu_custom_call" | custom-call | tf_op jit(solution)/shard_map/pallas_call | solution.py:127
  26.0 1.0 fusion.1
  27.0 0.7 pad_maximum_fusion.2
  27.7 5.4 %collective-permute-done.1.source_ref = f32[32,6656]{1,0:T(8,128)} collective-permute-done((f32[32,6656]{1,0:T(8,128)}, f32[32,6656]{1,0:T(8,128)}, u32[]{:S(2)}, u32[]{:S(2)}) %collective-permute-start.1) | collective-permute-done | bytes 852000 | tf_op jit(solution)/shard_map/ppermute | solution.py:257
  33.1 2.3 %collective-permute-start.2 = (f32[72,1024]{1,0:T(8,128)}, f32[72,1024]{1,0:T(8,128)}, u32[]{:S(2)}, u32[]{:S(2)}) collective-permute-start(f32[72,1024]{1,0:T(8,128)} %pad_maximum_fusion.2), channel_id=1, source_target_pairs={{0,128},{128,0},{1,129},{129,1},{2,130},{130,2},{3,131},{131,3},{4... | collective-permute-start | bytes 884744 | tf_op jit(solution)/shard_map/ppermute | solution.py:257
  37.4 1.7 conditional.1
  37.4 1.7 copy.12
  39.1 0.6 pad_add_fusion.4.scalars
  39.7 1.2 collective-permute-start.3
  40.9 1.9 collective-permute-done.2
  42.8 1.9 slice_select_fusion.3
  44.7 2.6 %shard_map.57 = f32[1,64,1024]{2,1,0:T(8,128)} custom-call(s32[9]{0:T(128)} %pad_add_fusion.4.scalars, s32[200,128]{1,0:T(8,128)S(1)} %shard_map.55.places_ref, f32[64,1024]{1,0:T(8,128)} %get-tuple-element.91.front_ref, f32[64,1024]{1,0:T(8,128)} %get-tuple-element.90.source_ref), custom_call_target="tpu_custom_call" | custom-call | tf_op jit(solution)/shard_map/pallas_call | solution.py:127
  47.3 1.1 slice_select_fusion.4
  48.4 0.7 pad_maximum_fusion.4.refs_0_
  49.2 5.0 %shard_map.58 = (f32[8,32,1536]{2,1,0:T(8,128)}, f32[8,8,1664]{2,1,0:T(8,128)}, f32[8,8,1664]{2,1,0:T(8,128)}, f32[8,8,1664]{2,1,0:T(8,128)}, f32[8,8,1664]{2,1,0:T(8,128)}) custom-call(s32[97]{0:T(128)} %get-tuple-element.101.scalars, s32[200,128]{1,0:T(8,128)S(1)} %shard_map.55.places_ref, f32[8,64,1536]{2,1,0:T(8,128)} %get-tuple-element.103.front_ref, ...), custom_call_target="tpu_custom_call" | custom-call | tf_op jit(solution)/shard_map/pallas_call | solution.py:127
  54.1 0.8 slice_select_fusion.5
  54.9 0.7 pad_maximum_fusion.3
  55.6 5.4 %collective-permute-done.3.source_ref = f32[32,6656]{1,0:T(8,128)} collective-permute-done((f32[32,6656]{1,0:T(8,128)}, f32[32,6656]{1,0:T(8,128)}, u32[]{:S(2)}, u32[]{:S(2)}) %collective-permute-start.3) | collective-permute-done | bytes 852000 | tf_op jit(solution)/shard_map/ppermute | solution.py:257
  61.2 1.6 collective-permute-start.5
  62.7 1.3 collective-permute-start.6
  64.0 1.4 collective-permute-start.7
  65.5 1.4 collective-permute-start.8
  66.9 4.8 %shard_map.59 = (f32[8,32,1536]{2,1,0:T(8,128)}, f32[8,8,1664]{2,1,0:T(8,128)}, f32[8,8,1664]{2,1,0:T(8,128)}, f32[8,8,1664]{2,1,0:T(8,128)}, f32[8,8,1664]{2,1,0:T(8,128)}) custom-call(s32[97]{0:T(128)} %get-tuple-element.101.scalars, s32[200,128]{1,0:T(8,128)S(1)} %shard_map.55.places_ref, f32[8,64,1536]{2,1,0:T(8,128)S(1)} %copy-done, ...), custom_call_target="tpu_custom_call" | custom-call | tf_op jit(solution)/shard_map/pallas_call | solution.py:127
  71.7 0.9 collective-permute-start.9
  72.6 3.4 %pad_maximum_fusion = f32[8,64,1536]{2,1,0:T(8,128)} fusion(f32[8,32,1536]{2,1,0:T(8,128)S(1)} %copy-done.4, f32[8,32,1536]{2,1,0:T(8,128)} %get-tuple-element.72), kind=kLoop, calls=%fused_computation.3 | loop fusion | flops 786432 | bytes 6291456 | tf_op jit(solution)/shard_map/concatenate | solution.py:339
  75.9 0.7 collective-permute-start.10
  76.6 9.5 %collective-permute-done.6 = f32[8,8,1664]{2,1,0:T(8,128)} collective-permute-done((f32[8,8,1664]{2,1,0:T(8,128)}, f32[8,8,1664]{2,1,0:T(8,128)}, u32[]{:S(2)}, u32[]{:S(2)}) %collective-permute-start.6) | collective-permute-done | bytes 426016 | tf_op jit(solution)/shard_map/ppermute | solution.py:344
  86.2 0.7 collective-permute-start.4
  86.9 1.6 add_add_fusion
  88.6 26.4 %all_to_all.10 = f32[8,8,2048]{2,1,0:T(8,128)} all-to-all(f32[8,8,2048]{2,1,0:T(8,128)S(1)} %pad_maximum_fusion.1), channel_id=1, replica_groups=mesh['subcube'=2,'row'=8,'col'=16] {'row'}, dimensions={0} | all-to-all | bytes 1048576 | tf_op jit(solution)/shard_map/all_to_all | solution.py:337
  115.0 3.8 %all-to-all-start.1 = ((f32[8,64,1536]{2,1,0:T(8,128)}), f32[8,64,1536]{2,1,0:T(8,128)S(1)}, u32[]{:S(2)}, u32[]{:S(2)}) async-start(f32[8,64,1536]{2,1,0:T(8,128)} %pad_maximum_fusion), calls=%async_computation.1 | async-start | bytes 6291456 | tf_op jit(solution)/shard_map/all_to_all | solution.py:337
  118.8 0.7 slice_bitcast_fusion.2
  119.5 1.1 collective-permute-done.11
  120.7 0.7 broadcast_select_fusion
  122.1 1.3 slice.130
  124.0 0.7 pad_add_fusion.5.flags
  124.7 52.2 %all-gather.6.cloned.1.call-done = f32[1024,2048]{1,0:T(8,128)} async-done(((f32[64,2048]{1,0:T(8,128)}), f32[1024,2048]{1,0:T(8,128)}) %all-gather.6.cloned.1.call-update) | async-done | bytes 8388624 | tf_op jit(solution)/shard_map/all_gather | solution.py:352
  176.9 9.0 %shard_map.60 = (f32[512,512]{1,0:T(8,128)}, f32[512,512]{1,0:T(8,128)}, f32[512,512]{1,0:T(8,128)}) custom-call(s32[2]{0:T(128)} %pad_add_fusion.5.flags, f32[8,72,1024]{2,1,0:T(8,128)} %bitcast.52, f32[8,2,64,512]{3,2,1,0:T(8,128)} %bitcast.55, f32[8,2,64,2048]{3,2,1,0:T(8,128)} %bitcast.47), custom_call_target="tpu_custom_call" | custom-call | tf_op jit(solution)/shard_map/pallas_call | solution.py:180
  185.8 10.2 %shard_map.61.update_ref = f32[1536,512]{1,0:T(8,128)} custom-call(s32[12]{0:T(128)} %reshape.186.flags, f32[8,2,64,2048]{3,2,1,0:T(8,128)} %bitcast.48, f32[512,512]{1,0:T(8,128)} %get-tuple-element.85.first_ref, f32[512,512]{1,0:T(8,128)} %get-tuple-element.86.second_ref, f32[512,512]{1,0:T(8,128)} %get-tuple-element.87.fixed_ref), custom_call_target="tpu_custom_call" | custom-call | tf_op jit(solution)/shard_map/pallas_call | solution.py:211
  196.0 1.6 copy-done.1
  197.7 6.2 %shard_map.62 = f32[1536,512]{1,0:T(8,128)} custom-call(s32[12]{0:T(128)} %reshape.186.flags, f32[512,1536]{1,0:T(8,128)} %bitcast.49, f32[1536,512]{1,0:T(8,128)} %shard_map.61.update_ref), custom_call_target="tpu_custom_call" | custom-call | tf_op jit(solution)/shard_map/pallas_call | solution.py:231
  (57 shorter events, 3.0 us)
Async XLA Ops:
  6.5 6.4 %copy-start.5 = (s32[2,12288]{1,0:T(2,128)S(1)}, s32[2,12288]{1,0:T(2,128)}, u32[]{:S(2)}) copy-start(s32[2,12288]{1,0:T(2,128)} %param.11) | copy-start | bytes 294916
  6.5 54.5 %all-gather.8.cloned.1.call-start = ((), (), s32[]{:S(2)}) async-start(), calls=%async_computation.3 | async-start | bytes 2359296 | tf_op jit(solution)/shard_map/all_gather | solution.py:259
  7.3 114.8 %all-gather.10.cloned.1.call-start = ((), (), s32[]{:S(2)}) async-start(), calls=%async_computation.4 | async-start | bytes 2654208 | tf_op jit(solution)/shard_map/all_gather | solution.py:332
  10.6 22.5 %collective-permute-start.1 = (f32[32,6656]{1,0:T(8,128)}, f32[32,6656]{1,0:T(8,128)}, u32[]{:S(2)}, u32[]{:S(2)}) collective-permute-start(f32[32,6656]{1,0:T(8,128)} %get-tuple-element.89), channel_id=1, source_target_pairs={{0,128},{128,0},{1,129},{129,1},{2,130},{130,2},{3,131},{131,3},{4... | collective-permute-start | bytes 2555912 | tf_op jit(solution)/shard_map/ppermute | solution.py:257
  20.9 4.9 %copy-start.7 = (s32[3,1]{0,1:T(1,128)S(1)}, s32[3,1]{0,1:T(1,128)}, u32[]{:S(2)}) copy-start(s32[3,1]{0,1:T(1,128)} %param.13) | copy-start | bytes 40
  33.1 9.7 %collective-permute-start.2 = (f32[72,1024]{1,0:T(8,128)}, f32[72,1024]{1,0:T(8,128)}, u32[]{:S(2)}, u32[]{:S(2)}) collective-permute-start(f32[72,1024]{1,0:T(8,128)} %pad_maximum_fusion.2), channel_id=1, source_target_pairs={{0,128},{128,0},{1,129},{129,1},{2,130},{130,2},{3,131},{131,3},{4... | collective-permute-start | bytes 884744 | tf_op jit(solution)/shard_map/ppermute | solution.py:257
  39.7 21.4 %collective-permute-start.3 = (f32[32,6656]{1,0:T(8,128)}, f32[32,6656]{1,0:T(8,128)}, u32[]{:S(2)}, u32[]{:S(2)}) collective-permute-start(f32[32,6656]{1,0:T(8,128)} %get-tuple-element.66), channel_id=1, source_target_pairs={{0,128},{128,0},{1,129},{129,1},{2,130},{130,2},{3,131},{131,3},{4... | collective-permute-start | bytes 2555912 | tf_op jit(solution)/shard_map/ppermute | solution.py:257
  47.3 7.6 %copy-start.2 = (f32[1,64,1024]{2,1,0:T(8,128)S(1)}, f32[1,64,1024]{2,1,0:T(8,128)}, u32[]{:S(2)}) copy-start(f32[1,64,1024]{2,1,0:T(8,128)} %shard_map.57) | copy-start | bytes 786436
  47.3 19.6 %copy-start = (f32[8,64,1536]{2,1,0:T(8,128)S(1)}, f32[8,64,1536]{2,1,0:T(8,128)}, u32[]{:S(2)}) copy-start(f32[8,64,1536]{2,1,0:T(8,128)} %get-tuple-element.103.front_ref) | copy-start | bytes 9437188
  61.1 115.8 %all-gather.6.cloned.1.call-start = ((), (), s32[]{:S(2)}) async-start(), calls=%async_computation.2 | async-start | bytes 8912896 | tf_op jit(solution)/shard_map/all_gather | solution.py:352
  61.1 11.4 %copy-start.4 = (f32[8,32,1536]{2,1,0:T(8,128)S(1)}, f32[8,32,1536]{2,1,0:T(8,128)}, u32[]{:S(2)}) copy-start(f32[8,32,1536]{2,1,0:T(8,128)} %get-tuple-element.73) | copy-start | bytes 4718596
  61.2 14.8 %collective-permute-start.5 = (f32[8,8,1664]{2,1,0:T(8,128)}, f32[8,8,1664]{2,1,0:T(8,128)}, u32[]{:S(2)}, u32[]{:S(2)}) collective-permute-start(f32[8,8,1664]{2,1,0:T(8,128)} %get-tuple-element.75), channel_id=1, source_target_pairs={{0,4},{1,5},{16,20},{17,21},{32,36},{33,37},{48,52},{49,53},{64,68... | collective-permute-start | bytes 1277960 | tf_op jit(solution)/shard_map/ppermute | solution.py:344
  62.7 23.4 %collective-permute-start.6 = (f32[8,8,1664]{2,1,0:T(8,128)}, f32[8,8,1664]{2,1,0:T(8,128)}, u32[]{:S(2)}, u32[]{:S(2)}) collective-permute-start(f32[8,8,1664]{2,1,0:T(8,128)} %get-tuple-element.76), channel_id=1, source_target_pairs={{0,6},{1,7},{16,22},{17,23},{32,38},{33,39},{48,54},{49,55},{64,70... | collective-permute-start | bytes 1277960 | tf_op jit(solution)/shard_map/ppermute | solution.py:344
  64.0 22.9 %collective-permute-start.7 = (f32[8,8,1664]{2,1,0:T(8,128)}, f32[8,8,1664]{2,1,0:T(8,128)}, u32[]{:S(2)}, u32[]{:S(2)}) collective-permute-start(f32[8,8,1664]{2,1,0:T(8,128)} %get-tuple-element.77), channel_id=1, source_target_pairs={{0,8},{1,9},{16,24},{17,25},{32,40},{33,41},{48,56},{49,57},{64,72... | collective-permute-start | bytes 1277960 | tf_op jit(solution)/shard_map/ppermute | solution.py:344
  65.5 21.4 %collective-permute-start.8 = (f32[8,8,1664]{2,1,0:T(8,128)}, f32[8,8,1664]{2,1,0:T(8,128)}, u32[]{:S(2)}, u32[]{:S(2)}) collective-permute-start(f32[8,8,1664]{2,1,0:T(8,128)} %get-tuple-element.78), channel_id=1, source_target_pairs={{0,10},{1,11},{16,26},{17,27},{32,42},{33,43},{48,58},{49,59},{64,... | collective-permute-start | bytes 1277960 | tf_op jit(solution)/shard_map/ppermute | solution.py:344
  71.7 15.2 %collective-permute-start.9 = (f32[8,8,1664]{2,1,0:T(8,128)}, f32[8,8,1664]{2,1,0:T(8,128)S(1)}, u32[]{:S(2)}, u32[]{:S(2)}) collective-permute-start(f32[8,8,1664]{2,1,0:T(8,128)} %get-tuple-element.79), channel_id=1, source_target_pairs={{0,12},{1,13},{16,28},{17,29},{32,44},{33,45},{48,60},{49,61},{64,... | collective-permute-start | bytes 1277960 | tf_op jit(solution)/shard_map/ppermute | solution.py:344
  72.5 3.4 %copy-start.9 = (f32[8,8,1664]{2,1,0:T(8,128)S(1)}, f32[8,8,1664]{2,1,0:T(8,128)}, u32[]{:S(2)}) copy-start(f32[8,8,1664]{2,1,0:T(8,128)} %get-tuple-element.80) | copy-start | bytes 1277956
  72.5 13.6 %copy-start.8 = (f32[8,8,1664]{2,1,0:T(8,128)S(1)}, f32[8,8,1664]{2,1,0:T(8,128)}, u32[]{:S(2)}) copy-start(f32[8,8,1664]{2,1,0:T(8,128)} %get-tuple-element.74) | copy-start | bytes 1277956
  72.6 14.4 %copy-start.6 = (f32[8,8,1664]{2,1,0:T(8,128)S(1)}, f32[8,8,1664]{2,1,0:T(8,128)}, u32[]{:S(2)}) copy-start(f32[8,8,1664]{2,1,0:T(8,128)} %get-tuple-element.70) | copy-start | bytes 1277956
  75.9 10.9 %collective-permute-start.10 = (f32[8,8,1664]{2,1,0:T(8,128)S(1)}, f32[8,8,1664]{2,1,0:T(8,128)S(1)}, u32[]{:S(2)}, u32[]{:S(2)}) collective-permute-start(f32[8,8,1664]{2,1,0:T(8,128)S(1)} %copy-done.9), channel_id=1, source_target_pairs={{0,14},{1,15},{16,30},{17,31},{32,46},{33,47},{48,62},{49,63},{64,... | collective-permute-start | bytes 1277960 | tf_op jit(solution)/shard_map/ppermute | solution.py:344
  86.2 0.7 collective-permute-start.4
  88.5 26.5 %copy-start.3 = (f32[8,8,1664]{2,1,0:T(8,128)}, f32[8,8,1664]{2,1,0:T(8,128)S(1)}, u32[]{:S(2)}) copy-start(f32[8,8,1664]{2,1,0:T(8,128)S(1)} %add_add_fusion) | copy-start | bytes 1277956
  115.0 81.0 %all-to-all-start.1 = ((f32[8,64,1536]{2,1,0:T(8,128)}), f32[8,64,1536]{2,1,0:T(8,128)S(1)}, u32[]{:S(2)}, u32[]{:S(2)}) async-start(f32[8,64,1536]{2,1,0:T(8,128)} %pad_maximum_fusion), calls=%async_computation.1 | async-start | bytes 6291456 | tf_op jit(solution)/shard_map/all_to_all | solution.py:337
  119.5 1.2 collective-permute-start.11
  196.0 1.6 copy-start.1
Sparse Core Ops, SparseCore 0:
  9.1 44.0 all-gather.7
  61.2 52.6 all-gather.9
  115.8 60.9 all-gather.5
